TPU v7x, 32 devices: a whole 2x2x4 slice. The times are simulated.
32 devices in a mesh: clip: 2 (over x), frame: 4 (over z), tile: 4 (over y, core).
Axes of the slice: x: 2, y: 2, z: 4, core: 2. Of those that a mesh axis runs over, the one named last changes fastest.
Arguments:
- queries: bfloat16 [8, 8, 64, 1536], P(('clip', 'frame'), None, 'tile'), parts along dimension 0, may hold values from -5 to 5
- keys: bfloat16 [8, 8, 64, 1536], P(('clip', 'frame'), None, 'tile'), parts along dimension 0, may hold values from -5 to 5
- values: bfloat16 [8, 8, 64, 1536], P(('clip', 'frame'), None, 'tile'), parts along dimension 0, may hold values from -6 to 6
- grad_out: bfloat16 [8, 8, 64, 1536], P(('clip', 'frame'), None, 'tile'), parts along dimension 0, may hold values from -6 to 6
- window: int32 [18, 3], replicated, may hold values from -1 to 1, as said below
Outputs:
- key_grad: bfloat16 [8, 8, 64, 1536], P(('clip', 'frame'), None, 'tile'), parts along dimension 0
- value_grad: bfloat16 [8, 8, 64, 1536], P(('clip', 'frame'), None, 'tile'), parts along dimension 0
There are 2 independent parts, one for each index of `clip`. A program takes and returns all parts, laid end to end along the dimension named above; an argument that names none is the same for every part. Nothing has to cross between parts.
Inputs may be any that keep to these rules, and one draw needn't show every extreme that they name: For each of the nine pairs of frame and column tile offsets the window lists exactly two of the three row offsets; it always lists (0, 0, 0); its rows are distinct.
All inputs are finite; a program needn't handle non-finite values.
Results may differ from a plain program's by a relative error of at most 0.0065.
Values may be sent and summed in bfloat16 or wider, within the bound.
No kernel may reach another device: no remote copies, remote signals or barrier semaphores. Data moves between devices by JAX's collectives and lax.ppermute only.
A program may use at most 64 MiB of HBM per device.

v0:
```python
import jax
import jax.numpy as jnp
from jax import lax
from jax.sharding import PartitionSpec as P

HD = 128
TT = 1
TH = 4
TW = 8


def padded(value, sides, width):
    for axis, dim in sides:
        peers, length = (lax.axis_size(axis), value.shape[dim])
        up = [(i, (i + 1) % peers) for i in range(peers - 1)]
        down = [(j, i) for i, j in up]
        last = lax.slice_in_dim(value, length - width, length, axis=dim)
        first = lax.slice_in_dim(value, 0, width, axis=dim)
        before = lax.ppermute(last, axis, up)
        after = lax.ppermute(first, axis, down)
        value = jnp.concatenate([before, value, after], axis=dim)
    return value


def window_mask(
    window, frame_pos, frame_count, strip_pos, strip_count, time_tiles, height_tiles, strip_tiles
):
    q_time = jnp.arange(time_tiles, dtype=jnp.int32)
    k_time = jnp.arange(time_tiles + 2, dtype=jnp.int32)
    q_high = jnp.arange(height_tiles, dtype=jnp.int32)
    q_wide = jnp.arange(strip_tiles, dtype=jnp.int32)
    k_wide = jnp.arange(strip_tiles + 2, dtype=jnp.int32)
    off_time = k_time[None, :] - q_time[:, None] - 1
    off_high = q_high[None, :] - q_high[:, None]
    off_wide = k_wide[None, :] - q_wide[:, None] - 1
    tile_codes = (
        (off_time[:, None, None, :, None, None] + 1) * 9
        + (off_high[None, :, None, None, :, None] + 1) * 3
        + (off_wide[None, None, :, None, None, :] + 1)
    )
    is_near = (
        (jnp.abs(off_time) <= 1)[:, None, None, :, None, None]
        & (jnp.abs(off_high) <= 1)[None, :, None, None, :, None]
        & (jnp.abs(off_wide) <= 1)[None, None, :, None, None, :]
    )
    listed_codes = (window[:, 0] + 1) * 9 + (window[:, 1] + 1) * 3 + (window[:, 2] + 1)
    code_range = jnp.arange(27, dtype=jnp.int32)
    chosen = jnp.any(listed_codes[:, None] == code_range[None, :], axis=0)
    allowed = jnp.any((tile_codes[..., None] == code_range) & chosen, axis=-1) & is_near
    glob_time = frame_pos * time_tiles + k_time - 1
    glob_wide = strip_pos * strip_tiles + k_wide - 1
    inside_time = (glob_time >= 0) & (glob_time < frame_count * time_tiles)
    inside_wide = (glob_wide >= 0) & (glob_wide < strip_count * strip_tiles)
    allowed = (
        allowed
        & inside_time[None, None, None, :, None, None]
        & inside_wide[None, None, None, None, None, :]
    )
    token_mask = jnp.broadcast_to(
        allowed[:, None, :, None, :, None, :, None, :, None, :, None],
        (
            time_tiles,
            TT,
            height_tiles,
            TH,
            strip_tiles,
            TW,
            time_tiles + 2,
            TT,
            height_tiles,
            TH,
            strip_tiles + 2,
            TW,
        ),
    )
    row_count = time_tiles * TT * height_tiles * TH * strip_tiles * TW
    return token_mask.reshape(row_count, -1)


def forward_stats(query_g, key_g, value_g, grad_g, token_mask):
    scale_qk = HD ** (-0.5)
    scores = (
        jnp.einsum("qhd,khd->hqk", query_g, key_g, preferred_element_type=jnp.float32) * scale_qk
    )
    scores = jnp.where(token_mask[None], scores, -jnp.inf)
    top_score = jnp.max(scores, axis=-1, keepdims=True)
    exp_scores = jnp.exp(scores - top_score)
    total = jnp.sum(exp_scores, axis=-1, keepdims=True)
    probs_low = (exp_scores / total).astype(jnp.bfloat16)
    attended = jnp.einsum("hqk,khd->qhd", probs_low, value_g, preferred_element_type=jnp.float32)
    row_delta = jnp.sum(grad_g.astype(jnp.float32) * attended, axis=-1)
    log_total = (top_score + jnp.log(total))[:, :, 0].T
    return (log_total, row_delta)


def own_key_grads(key_g, value_g, query_g, grad_g, lse_ext, delta_ext, key_mask):
    scale_qk = HD ** (-0.5)
    lse_g = lse_ext.T
    delta_g = delta_ext.T
    scores = (
        jnp.einsum("khd,qhd->hkq", key_g, query_g, preferred_element_type=jnp.float32) * scale_qk
    )
    attn_probs = jnp.exp(jnp.where(key_mask[None], scores - lse_g[:, None, :], -jnp.inf))
    probs_low = attn_probs.astype(jnp.bfloat16)
    value_part = jnp.einsum("hkq,qhd->khd", probs_low, grad_g, preferred_element_type=jnp.float32)
    grad_probs = jnp.einsum("khd,qhd->hkq", value_g, grad_g, preferred_element_type=jnp.float32)
    grad_scores = (attn_probs * (grad_probs - delta_g[:, None, :]) * scale_qk).astype(jnp.bfloat16)
    key_part = jnp.einsum("hkq,qhd->khd", grad_scores, query_g, preferred_element_type=jnp.float32)
    return (key_part, value_part)


def extend_tiles(stacked):
    return padded(stacked, (("tile", 3),), TW)


def extend_frames(stacked):
    return padded(stacked, (("frame", 1),), TT)


def extend_row_tiles(pair):
    return padded(pair, (("tile", 3),), TW)


def extend_row_frames(pair):
    return padded(pair, (("frame", 1),), TT)


def extend_stat_tiles(stats):
    return padded(stats, (("tile", 3),), TW)


def extend_stat_frames(stats):
    return padded(stats, (("frame", 1),), TT)


def on_device(queries, keys, values, grad_out, window):
    frames, height, strip, chans = queries.shape
    heads = chans // HD
    row_count = frames * height * strip
    ext_frames = frames + 2 * TT
    ext_strip = strip + 2 * TW
    ext_count = ext_frames * height * ext_strip
    stacked = jnp.stack([keys, values])
    extended = extend_frames(extend_tiles(stacked))
    frame_pos = lax.axis_index("frame")
    strip_pos = lax.axis_index("tile")
    token_mask = window_mask(
        window,
        frame_pos,
        lax.axis_size("frame"),
        strip_pos,
        lax.axis_size("tile"),
        frames // TT,
        height // TH,
        strip // TW,
    )
    query_heads = queries.reshape(row_count, heads, HD)
    grad_heads = grad_out.reshape(row_count, heads, HD)
    key_heads = extended[0].reshape(ext_count, heads, HD)
    value_heads = extended[1].reshape(ext_count, heads, HD)
    lse_rows, delta_rows = forward_stats(
        query_heads, key_heads, value_heads, grad_heads, token_mask
    )
    stats = jnp.stack([lse_rows, delta_rows]).reshape(2, frames, height, strip, heads)
    pair = jnp.stack([queries, grad_out])
    pair_ext = extend_row_frames(extend_row_tiles(pair))
    stats_ext = extend_stat_frames(extend_stat_tiles(stats))
    key_mask = window_mask(
        -window,
        frame_pos,
        lax.axis_size("frame"),
        strip_pos,
        lax.axis_size("tile"),
        frames // TT,
        height // TH,
        strip // TW,
    )
    key_own, value_own = own_key_grads(
        keys.reshape(row_count, heads, HD),
        values.reshape(row_count, heads, HD),
        pair_ext[0].reshape(ext_count, heads, HD),
        pair_ext[1].reshape(ext_count, heads, HD),
        stats_ext[0].reshape(ext_count, heads),
        stats_ext[1].reshape(ext_count, heads),
        key_mask,
    )
    key_out = key_own.reshape(frames, height, strip, chans)
    value_out = value_own.reshape(frames, height, strip, chans)
    return (key_out.astype(jnp.bfloat16), value_out.astype(jnp.bfloat16))


def solution(mesh):
    return jax.shard_map(
        on_device,
        mesh=mesh,
        in_specs=(
            P(("clip", "frame"), None, "tile", None),
            P(("clip", "frame"), None, "tile", None),
            P(("clip", "frame"), None, "tile", None),
            P(("clip", "frame"), None, "tile", None),
            P(),
        ),
        out_specs=(
            P(("clip", "frame"), None, "tile", None),
            P(("clip", "frame"), None, "tile", None),
        ),
        check_vma=False,
    )
```

profile of v0, /device:TPU:1, one launch (start us, length us, event | category | flops | bytes accessed | tf_op | source)
XLA Modules:
  0.0 148.1 jit_solution(13174001444713043489)
XLA Ops:
  2.1 4.5 %collective-permute-start.4 = (bf16[2,1,8,8,1536]{4,3,2,1,0:T(8,128)(2,1)S(1)}, bf16[2,1,8,8,1536]{4,3,2,1,0:T(8,128)(2,1)S(1)}, u32[]{:S(2)}, u32[]{:S(2)}) collective-permute-start(bf16[2,1,8,8,1536]{4,3,2,1,0:T(8,128)(2,1)S(1)} %get-tuple-element.10), channel_id=1, source_target_pairs={{0,1},{1,2},{2,3},{4,5},{5,6},{6,7},{8,9},{9,10},{10,11},{12,13},{... | collective-permute-start | bytes 1179656 | tf_op jit(solution)/shard_map/ppermute | solution.py:19
  6.6 1.9 %collective-permute-start.5 = (bf16[2,1,8,8,1536]{4,3,2,1,0:T(8,128)(2,1)S(1)}, bf16[2,1,8,8,1536]{4,3,2,1,0:T(8,128)(2,1)S(1)}, u32[]{:S(2)}, u32[]{:S(2)}) collective-permute-start(bf16[2,1,8,8,1536]{4,3,2,1,0:T(8,128)(2,1)S(1)} %get-tuple-element.11), channel_id=1, source_target_pairs={{1,0},{2,1},{3,2},{5,4},{6,5},{7,6},{9,8},{10,9},{11,10},{13,12},{... | collective-permute-start | bytes 1179656 | tf_op jit(solution)/shard_map/ppermute | solution.py:20
  8.5 2.1 %fusion.44 = (bf16[2,1,8,8,1536]{4,3,2,1,0:T(8,128)(2,1)}, bf16[2,1,8,8,1536]{4,3,2,1,0:T(8,128)(2,1)}) fusion(bf16[1,1,8,16,1536]{4,3,2,1,0:T(8,128)(2,1)} %bitcast.109, bf16[1,1,8,16,1536]{4,3,2,1,0:T(8,128)(2,1)} %bitcast.112), kind=kLoop, calls=%fused_computation.40 | loop fusion | flops 1572864 | bytes 1572864 | tf_op jit(solution)/shard_map/stack | solution.py:165
  10.7 3.6 %collective-permute-start = (bf16[2,1,8,8,1536]{4,3,2,1,0:T(8,128)(2,1)}, bf16[2,1,8,8,1536]{4,3,2,1,0:T(8,128)(2,1)S(1)}, u32[]{:S(2)}, u32[]{:S(2)}) collective-permute-start(bf16[2,1,8,8,1536]{4,3,2,1,0:T(8,128)(2,1)} %get-tuple-element.12), channel_id=1, source_target_pairs={{0,1},{1,2},{2,3},{4,5},{5,6},{6,7},{8,9},{9,10},{10,11},{12,13},{... | collective-permute-start | bytes 1179656 | tf_op jit(solution)/shard_map/ppermute | solution.py:19
  14.3 1.9 %collective-permute-start.1 = (bf16[2,1,8,8,1536]{4,3,2,1,0:T(8,128)(2,1)}, bf16[2,1,8,8,1536]{4,3,2,1,0:T(8,128)(2,1)}, u32[]{:S(2)}, u32[]{:S(2)}) collective-permute-start(bf16[2,1,8,8,1536]{4,3,2,1,0:T(8,128)(2,1)} %get-tuple-element.13), channel_id=1, source_target_pairs={{1,0},{2,1},{3,2},{5,4},{6,5},{7,6},{9,8},{10,9},{11,10},{13,12},{... | collective-permute-start | bytes 1179656 | tf_op jit(solution)/shard_map/ppermute | solution.py:20
  20.4 2.7 %pad_maximum_fusion.3 = bf16[2,1,8,32,1536]{4,3,2,1,0:T(8,128)(2,1)} fusion(bf16[2,1,8,8,1536]{4,3,2,1,0:T(8,128)(2,1)S(1)} %collective-permute-done.5, bf16[1,1,8,16,1536]{4,3,2,1,0:T(8,128)(2,1)} %bitcast.107, bf16[1,1,8,16,1536]{4,3,2,1,0:T(8,128)(2,1)} %bitcast.104, bf16[2,1,8,8,1536]{4,3,2,1,0:T(8,128)(2,1)S(1)} %collective-permute-done.4), kind=kLoop, calls=%fused_computation.27 | loop fusion | flops 6291456 | bytes 3145728 | tf_op jit(solution)/shard_map/concatenate | solution.py:21
  23.1 4.3 %collective-permute-start.6 = (bf16[2,1,8,32,1536]{4,3,2,1,0:T(8,128)(2,1)}, bf16[2,1,8,32,1536]{4,3,2,1,0:T(8,128)(2,1)}, u32[]{:S(2)}, u32[]{:S(2)}) collective-permute-start(bf16[2,1,8,32,1536]{4,3,2,1,0:T(8,128)(2,1)} %pad_maximum_fusion.3), channel_id=1, source_target_pairs={{0,4},{4,8},{8,12},{1,5},{5,9},{9,13},{2,6},{6,10},{10,14},{3,7},{... | collective-permute-start | bytes 4718600 | tf_op jit(solution)/shard_map/ppermute | solution.py:19
  36.9 5.4 %broadcast_in_dim.30 = pred[128,768]{1,0:T(8,128)(4,1)} reshape(pred[2,4,2,8,3,1,2,4,4,8]{9,8,7,6,4,3,2,1,0,5:T(4,128)(4,1)S(1)} %broadcast_in_dim.25) | data formatting | bytes 196608 | tf_op jit(solution)/shard_map/broadcast_in_dim | solution.py:59
  44.0 2.5 %copy.45 = f32[128,12,128]{0,2,1:T(8,128)} copy(f32[128,12,128]{2,1,0:T(8,128)} %reshape.234) | data formatting | bytes 1572864 | tf_op jit(solution)/shard_map/convert_element_type | solution.py:91
  47.4 5.4 %broadcast_in_dim.23 = pred[128,768]{1,0:T(8,128)(4,1)} reshape(pred[2,4,2,8,3,1,2,4,4,8]{9,8,7,6,4,3,2,1,0,5:T(4,128)(4,1)S(1)} %broadcast_in_dim.22) | data formatting | bytes 196608 | tf_op jit(solution)/shard_map/broadcast_in_dim | solution.py:59
  52.8 1.7 %copy.37 = pred[128,768]{0,1:T(8,128)(4,1)} copy(pred[128,768]{1,0:T(8,128)(4,1)} %broadcast_in_dim.23) | data formatting | bytes 196608 | tf_op jit(solution)/shard_map/broadcast_in_dim | solution.py:59
  54.5 2.3 %pad_maximum_fusion.2 = bf16[2,1,8,32,1536]{4,3,2,1,0:T(8,128)(2,1)} fusion(bf16[2,1,8,8,1536]{4,3,2,1,0:T(8,128)(2,1)} %collective-permute-done.1, bf16[1,1,8,16,1536]{4,3,2,1,0:T(8,128)(2,1)S(1)} %bitcast.113, bf16[1,1,8,16,1536]{4,3,2,1,0:T(8,128)(2,1)S(1)} %bitcast.110, bf16[2,1,8,8,1536]{4,3,2,1,0:T(8,128)(2,1)S(1)} %collective-permute-done), kind=kLoop, calls=%fused_computation.26 | loop fusion | flops 6291456 | bytes 3145728 | tf_op jit(solution)/shard_map/concatenate | solution.py:21
  56.8 5.1 %collective-permute-start.2 = (bf16[2,1,8,32,1536]{4,3,2,1,0:T(8,128)(2,1)}, bf16[2,1,8,32,1536]{4,3,2,1,0:T(8,128)(2,1)}, u32[]{:S(2)}, u32[]{:S(2)}) collective-permute-start(bf16[2,1,8,32,1536]{4,3,2,1,0:T(8,128)(2,1)} %pad_maximum_fusion.2), channel_id=1, source_target_pairs={{0,4},{4,8},{8,12},{1,5},{5,9},{9,13},{2,6},{6,10},{10,14},{3,7},{... | collective-permute-start | bytes 4718600 | tf_op jit(solution)/shard_map/ppermute | solution.py:19
  64.7 3.0 %pad_maximum_fusion.1 = bf16[2,3,8,32,1536]{4,3,2,1,0:T(8,128)(2,1)S(1)} fusion(bf16[2,1,8,32,1536]{4,3,2,1,0:T(8,128)(2,1)} %collective-permute-done.7, bf16[2,1,8,8,1536]{4,3,2,1,0:T(8,128)(2,1)} %copy-done.7, bf16[1,1,8,16,1536]{4,3,2,1,0:T(8,128)(2,1)S(1)} %bitcast.108, bf16[1,1,8,16,1536]{4,3,2,1,0:T(8,128)(2,1)S(1)} %bitcast.105, ...), kind=kLoop, calls=%fused_computation.1 | loop fusion | flops 28311552 | bytes 9437184 | tf_op jit(solution)/shard_map/concatenate | solution.py:21
  67.8 1.9 %fusion.67 = (bf16[1,3,8,32,1536]{4,3,2,1,0:T(8,128)(2,1)S(1)}, bf16[1,3,8,32,1536]{4,3,2,1,0:T(8,128)(2,1)}) fusion(bf16[2,3,8,32,1536]{4,3,2,1,0:T(8,128)(2,1)S(1)} %pad_maximum_fusion.1), kind=kLoop, calls=%fused_computation.88 | loop fusion | bytes 9437184 | tf_op jit(solution)/shard_map/slice | solution.py:160
  69.7 5.4 %reshape_squeeze.19 = bf16[768,12,128]{2,1,0:T(8,128)(2,1)} reshape(bf16[1,3,8,32,1536]{4,3,2,1,0:T(8,128)(2,1)} %get-tuple-element.9) | data formatting | bytes 4718592 | tf_op jit(solution)/shard_map/reshape;squeeze | solution.py:159
  75.1 3.3 %fusion.4 = (f32[12,128]{1,0:T(8,128)S(1)}, f32[12,768,128]{2,1,0:T(8,128)S(1)}) fusion(pred[128,768]{0,1:T(8,128)(4,1)} %copy.40, bf16[128,12,128]{2,1,0:T(8,128)(2,1)} %reshape.232, bf16[768,12,128]{2,1,0:T(8,128)(2,1)} %reshape_squeeze.19), kind=kOutput, calls=%fused_computation.11 | convolution fusion | flops 305527296 | bytes 7575552 | tf_op jit(solution)/shard_map/qhd,khd->hqk/dot_general | solution.py:83
  78.4 2.1 %copy-done.5 = f32[12,768,128]{2,1,0:T(8,128)} copy-done((f32[12,768,128]{2,1,0:T(8,128)}, f32[12,768,128]{2,1,0:T(8,128)S(1)}, u32[]{:S(2)}) %copy-start.5) | copy-done | bytes 4718616
  83.5 3.0 %reshape_squeeze.20 = bf16[768,12,128]{2,1,0:T(8,128)(2,1)} reshape(bf16[1,3,8,32,1536]{4,3,2,1,0:T(8,128)(2,1)S(1)} %get-tuple-element.8) | data formatting | bytes 4718592 | tf_op jit(solution)/shard_map/reshape;squeeze | solution.py:160
  86.5 5.7 %fusion.40 = f32[128,12]{0,1:T(8,128)S(1)} fusion(f32[128,12,128]{0,2,1:T(8,128)} %copy.45, f32[12,768,128]{2,1,0:T(8,128)} %copy-done.5, f32[12,128]{1,0:T(8,128)S(1)} %fusion.3, f32[12,128]{1,0:T(8,128)S(1)} %get-tuple-element.20, pred[128,768]{0,1:T(8,128)(4,1)} %copy.40, bf16[768,12,128]{2,1,0:T(8,128)(2,1)} %reshape_squeeze.20), kind=kOutput, calls=%fused_computation.34 | convolution fusion | flops 308279808 | bytes 7981056 | tf_op jit(solution)/shard_map/hqk,khd->qhd/dot_general | solution.py:90
  93.0 4.4 %collective-permute-start.8 = (f32[2,1,8,8,12]{3,2,1,4,0:T(8,128)}, f32[2,1,8,8,12]{3,2,1,4,0:T(8,128)}, u32[]{:S(2)}, u32[]{:S(2)}) collective-permute-start(f32[2,1,8,8,12]{3,2,1,4,0:T(8,128)} %get-tuple-element.16), channel_id=1, source_target_pairs={{0,1},{1,2},{2,3},{4,5},{5,6},{6,7},{8,9},{9,10},{10,11},{12,13},{... | collective-permute-start | bytes 18440 | tf_op jit(solution)/shard_map/ppermute | solution.py:19
  97.5 1.9 %collective-permute-start.9 = (f32[2,1,8,8,12]{3,2,1,4,0:T(8,128)}, f32[2,1,8,8,12]{3,2,1,4,0:T(8,128)}, u32[]{:S(2)}, u32[]{:S(2)}) collective-permute-start(f32[2,1,8,8,12]{3,2,1,4,0:T(8,128)} %get-tuple-element.17), channel_id=1, source_target_pairs={{1,0},{2,1},{3,2},{5,4},{6,5},{7,6},{9,8},{10,9},{11,10},{13,12},{... | collective-permute-start | bytes 18440 | tf_op jit(solution)/shard_map/ppermute | solution.py:20
  99.7 3.0 %pad_maximum_fusion = bf16[2,3,8,32,1536]{4,3,2,1,0:T(8,128)(2,1)S(1)} fusion(bf16[2,1,8,32,1536]{4,3,2,1,0:T(8,128)(2,1)} %collective-permute-done.3, bf16[2,1,8,8,1536]{4,3,2,1,0:T(8,128)(2,1)} %collective-permute-done.1, bf16[1,1,8,16,1536]{4,3,2,1,0:T(8,128)(2,1)S(1)} %bitcast.114, bf16[1,1,8,16,1536]{4,3,2,1,0:T(8,128)(2,1)S(1)} %bitcast.111, ...), kind=kLoop, calls=%fused_computation | loop fusion | flops 28311552 | bytes 9437184 | tf_op jit(solution)/shard_map/concatenate | solution.py:21
  102.7 2.7 %fusion.66 = (bf16[1,3,8,32,1536]{4,3,2,1,0:T(8,128)(2,1)}, bf16[1,3,8,32,1536]{4,3,2,1,0:T(8,128)(2,1)}) fusion(bf16[2,3,8,32,1536]{4,3,2,1,0:T(8,128)(2,1)S(1)} %pad_maximum_fusion), kind=kLoop, calls=%fused_computation.87 | loop fusion | bytes 9437184 | tf_op jit(solution)/shard_map/slice | solution.py:182
  105.4 4.2 %reshape_squeeze.18 = bf16[768,12,128]{2,1,0:T(8,128)(2,1)S(1)} reshape(bf16[1,3,8,32,1536]{4,3,2,1,0:T(8,128)(2,1)} %get-tuple-element.7) | data formatting | bytes 4718592 | tf_op jit(solution)/shard_map/reshape;squeeze | solution.py:181
  109.6 3.5 %copy.49 = bf16[768,12,128]{0,2,1:T(8,128)(2,1)} copy(bf16[768,12,128]{2,1,0:T(8,128)(2,1)S(1)} %reshape_squeeze.18) | data formatting | bytes 4718592 | tf_op jit(solution)/shard_map/reshape;squeeze | solution.py:181
  114.1 2.8 %collective-permute-start.10 = (f32[2,1,8,32,12]{3,2,1,4,0:T(8,128)S(1)}, f32[2,1,8,32,12]{3,2,1,4,0:T(8,128)S(1)}, u32[]{:S(2)}, u32[]{:S(2)}) collective-permute-start(f32[2,1,8,32,12]{3,2,1,4,0:T(8,128)S(1)} %pad_maximum_fusion.8), channel_id=1, source_target_pairs={{0,4},{4,8},{8,12},{1,5},{5,9},{9,13},{2,6},{6,10},{10,14},{3,7},{... | collective-permute-start | bytes 73736 | tf_op jit(solution)/shard_map/ppermute | solution.py:19
  118.4 4.7 %fusion.48 = f32[12,768,128]{2,1,0:T(8,128)} fusion(bf16[768,12,128]{0,2,1:T(8,128)(2,1)} %copy.49, bf16[128,12,128]{2,1,0:T(8,128)(2,1)} %reshape.231), kind=kOutput, calls=%fused_computation.45 | convolution fusion | flops 301989888 | bytes 7471104 | tf_op jit(solution)/shard_map/khd,qhd->hkq/dot_general | solution.py:101
  123.2 4.2 %reshape_squeeze.22 = bf16[768,12,128]{2,1,0:T(8,128)(2,1)S(1)} reshape(bf16[1,3,8,32,1536]{4,3,2,1,0:T(8,128)(2,1)} %get-tuple-element.6) | data formatting | bytes 4718592 | tf_op jit(solution)/shard_map/reshape;squeeze | solution.py:182
  127.3 3.5 %copy.52 = bf16[768,12,128]{0,2,1:T(8,128)(2,1)} copy(bf16[768,12,128]{2,1,0:T(8,128)(2,1)S(1)} %reshape_squeeze.22) | data formatting | bytes 4718592 | tf_op jit(solution)/shard_map/reshape;squeeze | solution.py:182
  132.6 5.0 %fusion.37 = bf16[128,12,128]{0,2,1:T(8,128)(2,1)} fusion(bf16[768,12,128]{0,2,1:T(8,128)(2,1)} %copy.52, f32[12,768,128]{2,1,0:T(8,128)} %fusion.48, f32[12,768]{1,0:T(8,128)S(1)} %bitcast.118, pred[128,768]{0,1:T(8,128)(4,1)} %copy.37), kind=kOutput, calls=%fused_computation.33 | convolution fusion | flops 306905088 | bytes 7606272 | tf_op jit(solution)/shard_map/hkq,qhd->khd/dot_general | solution.py:105
  140.1 6.5 %fusion.34 = bf16[128,12,128]{0,2,1:T(8,128)(2,1)S(1)} fusion(bf16[768,12,128]{0,2,1:T(8,128)(2,1)S(1)} %copy-done, f32[12,768,128]{2,1,0:T(8,128)} %fusion.48, f32[12,768]{1,0:T(8,128)S(1)} %bitcast.120, f32[12,768]{1,0:T(8,128)} %bitcast.119, pred[128,768]{0,1:T(8,128)(4,1)} %copy.37, bf16[768,12,128]{0,2,1:T(8,128)(2,1)} %copy.52, ...), kind=kOutput, calls=%fused_computation.32 | convolution fusion | flops 612433920 | bytes 10395648 | tf_op jit(solution)/shard_map/hkq,qhd->khd/dot_general | solution.py:108
  (85 shorter events, 32.7 us)
Async XLA Ops:
  0.6 32.1 %copy-start.1 = (bf16[1,8,16,1536]{3,2,1,0:T(8,128)(2,1)S(1)}, bf16[1,8,16,1536]{3,2,1,0:T(8,128)(2,1)}, u32[]{:S(2)}) copy-start(bf16[1,8,16,1536]{3,2,1,0:T(8,128)(2,1)} %param.6) | copy-start | bytes 1179652
  0.6 29.8 %copy-start.3 = (bf16[1,8,16,1536]{3,2,1,0:T(8,128)(2,1)S(1)}, bf16[1,8,16,1536]{3,2,1,0:T(8,128)(2,1)}, u32[]{:S(2)}) copy-start(bf16[1,8,16,1536]{3,2,1,0:T(8,128)(2,1)} %param.5) | copy-start | bytes 1179652
  0.7 30.9 %copy-start.4 = (bf16[1,8,16,1536]{3,2,1,0:T(8,128)(2,1)S(1)}, bf16[1,8,16,1536]{3,2,1,0:T(8,128)(2,1)}, u32[]{:S(2)}) copy-start(bf16[1,8,16,1536]{3,2,1,0:T(8,128)(2,1)} %param.8) | copy-start | bytes 1179652
  0.7 33.2 %copy-start.2 = (bf16[1,8,16,1536]{3,2,1,0:T(8,128)(2,1)S(1)}, bf16[1,8,16,1536]{3,2,1,0:T(8,128)(2,1)}, u32[]{:S(2)}) copy-start(bf16[1,8,16,1536]{3,2,1,0:T(8,128)(2,1)} %param.7) | copy-start | bytes 1179652
  2.1 18.3 %collective-permute-start.4 = (bf16[2,1,8,8,1536]{4,3,2,1,0:T(8,128)(2,1)S(1)}, bf16[2,1,8,8,1536]{4,3,2,1,0:T(8,128)(2,1)S(1)}, u32[]{:S(2)}, u32[]{:S(2)}) collective-permute-start(bf16[2,1,8,8,1536]{4,3,2,1,0:T(8,128)(2,1)S(1)} %get-tuple-element.10), channel_id=1, source_target_pairs={{0,1},{1,2},{2,3},{4,5},{5,6},{6,7},{8,9},{9,10},{10,11},{12,13},{... | collective-permute-start | bytes 1179656 | tf_op jit(solution)/shard_map/ppermute | solution.py:19
  6.6 13.8 %collective-permute-start.5 = (bf16[2,1,8,8,1536]{4,3,2,1,0:T(8,128)(2,1)S(1)}, bf16[2,1,8,8,1536]{4,3,2,1,0:T(8,128)(2,1)S(1)}, u32[]{:S(2)}, u32[]{:S(2)}) collective-permute-start(bf16[2,1,8,8,1536]{4,3,2,1,0:T(8,128)(2,1)S(1)} %get-tuple-element.11), channel_id=1, source_target_pairs={{1,0},{2,1},{3,2},{5,4},{6,5},{7,6},{9,8},{10,9},{11,10},{13,12},{... | collective-permute-start | bytes 1179656 | tf_op jit(solution)/shard_map/ppermute | solution.py:20
  10.7 43.8 %collective-permute-start = (bf16[2,1,8,8,1536]{4,3,2,1,0:T(8,128)(2,1)}, bf16[2,1,8,8,1536]{4,3,2,1,0:T(8,128)(2,1)S(1)}, u32[]{:S(2)}, u32[]{:S(2)}) collective-permute-start(bf16[2,1,8,8,1536]{4,3,2,1,0:T(8,128)(2,1)} %get-tuple-element.12), channel_id=1, source_target_pairs={{0,1},{1,2},{2,3},{4,5},{5,6},{6,7},{8,9},{9,10},{10,11},{12,13},{... | collective-permute-start | bytes 1179656 | tf_op jit(solution)/shard_map/ppermute | solution.py:19
  14.3 40.2 %collective-permute-start.1 = (bf16[2,1,8,8,1536]{4,3,2,1,0:T(8,128)(2,1)}, bf16[2,1,8,8,1536]{4,3,2,1,0:T(8,128)(2,1)}, u32[]{:S(2)}, u32[]{:S(2)}) collective-permute-start(bf16[2,1,8,8,1536]{4,3,2,1,0:T(8,128)(2,1)} %get-tuple-element.13), channel_id=1, source_target_pairs={{1,0},{2,1},{3,2},{5,4},{6,5},{7,6},{9,8},{10,9},{11,10},{13,12},{... | collective-permute-start | bytes 1179656 | tf_op jit(solution)/shard_map/ppermute | solution.py:20
  20.4 15.6 %copy-start.6 = (bf16[2,1,8,8,1536]{4,3,2,1,0:T(8,128)(2,1)}, bf16[2,1,8,8,1536]{4,3,2,1,0:T(8,128)(2,1)S(1)}, u32[]{:S(2)}) copy-start(bf16[2,1,8,8,1536]{4,3,2,1,0:T(8,128)(2,1)S(1)} %collective-permute-done.4) | copy-start | bytes 1179652
  20.4 15.5 %copy-start.15 = (pred[2,4]{1,0:T(4,128)(4,1)S(1)}, pred[2,4]{1,0:T(4,128)(4,1)}, u32[]{:S(2)}) copy-start(pred[2,4]{1,0:T(4,128)(4,1)} %abs_compare_fusion) | copy-start | bytes 28
  20.4 15.6 %copy-start.7 = (bf16[2,1,8,8,1536]{4,3,2,1,0:T(8,128)(2,1)}, bf16[2,1,8,8,1536]{4,3,2,1,0:T(8,128)(2,1)S(1)}, u32[]{:S(2)}) copy-start(bf16[2,1,8,8,1536]{4,3,2,1,0:T(8,128)(2,1)S(1)} %collective-permute-done.5) | copy-start | bytes 1179652
  23.1 40.3 %collective-permute-start.6 = (bf16[2,1,8,32,1536]{4,3,2,1,0:T(8,128)(2,1)}, bf16[2,1,8,32,1536]{4,3,2,1,0:T(8,128)(2,1)}, u32[]{:S(2)}, u32[]{:S(2)}) collective-permute-start(bf16[2,1,8,32,1536]{4,3,2,1,0:T(8,128)(2,1)} %pad_maximum_fusion.3), channel_id=1, source_target_pairs={{0,4},{4,8},{8,12},{1,5},{5,9},{9,13},{2,6},{6,10},{10,14},{3,7},{... | collective-permute-start | bytes 4718600 | tf_op jit(solution)/shard_map/ppermute | solution.py:19
  27.5 37.2 %collective-permute-start.7 = (bf16[2,1,8,32,1536]{4,3,2,1,0:T(8,128)(2,1)}, bf16[2,1,8,32,1536]{4,3,2,1,0:T(8,128)(2,1)}, u32[]{:S(2)}, u32[]{:S(2)}) collective-permute-start(bf16[2,1,8,32,1536]{4,3,2,1,0:T(8,128)(2,1)} %pad_maximum_fusion.3), channel_id=1, source_target_pairs={{4,0},{8,4},{12,8},{5,1},{9,5},{13,9},{6,2},{10,6},{14,10},{7,3},{... | collective-permute-start | bytes 4718600 | tf_op jit(solution)/shard_map/ppermute | solution.py:20
  56.8 42.6 %collective-permute-start.2 = (bf16[2,1,8,32,1536]{4,3,2,1,0:T(8,128)(2,1)}, bf16[2,1,8,32,1536]{4,3,2,1,0:T(8,128)(2,1)}, u32[]{:S(2)}, u32[]{:S(2)}) collective-permute-start(bf16[2,1,8,32,1536]{4,3,2,1,0:T(8,128)(2,1)} %pad_maximum_fusion.2), channel_id=1, source_target_pairs={{0,4},{4,8},{8,12},{1,5},{5,9},{9,13},{2,6},{6,10},{10,14},{3,7},{... | collective-permute-start | bytes 4718600 | tf_op jit(solution)/shard_map/ppermute | solution.py:19
  61.9 37.8 %collective-permute-start.3 = (bf16[2,1,8,32,1536]{4,3,2,1,0:T(8,128)(2,1)}, bf16[2,1,8,32,1536]{4,3,2,1,0:T(8,128)(2,1)}, u32[]{:S(2)}, u32[]{:S(2)}) collective-permute-start(bf16[2,1,8,32,1536]{4,3,2,1,0:T(8,128)(2,1)} %pad_maximum_fusion.2), channel_id=1, source_target_pairs={{4,0},{8,4},{12,8},{5,1},{9,5},{13,9},{6,2},{10,6},{14,10},{7,3},{... | collective-permute-start | bytes 4718600 | tf_op jit(solution)/shard_map/ppermute | solution.py:20
  75.1 5.4 %copy-start.13 = (pred[128,768]{0,1:T(8,128)(4,1)S(1)}, pred[128,768]{0,1:T(8,128)(4,1)}, u32[]{:S(2)}) copy-start(pred[128,768]{0,1:T(8,128)(4,1)} %copy.40) | copy-start | bytes 294916
  78.4 2.1 %copy-start.5 = (f32[12,768,128]{2,1,0:T(8,128)}, f32[12,768,128]{2,1,0:T(8,128)S(1)}, u32[]{:S(2)}) copy-start(f32[12,768,128]{2,1,0:T(8,128)S(1)} %get-tuple-element.21) | copy-start | bytes 14155780
  86.5 5.8 %copy-start.8 = (f32[1,1,8,16,12]{3,2,4,1,0:T(8,128)S(1)}, f32[1,1,8,16,12]{3,2,4,1,0:T(8,128)}, u32[]{:S(2)}) copy-start(f32[1,1,8,16,12]{3,2,4,1,0:T(8,128)} %stack.33) | copy-start | bytes 18436
  92.3 10.4 %copy-start.10 = (f32[1,1,8,16,12]{3,2,1,4,0:T(8,128)}, f32[1,1,8,16,12]{3,2,1,4,0:T(8,128)S(1)}, u32[]{:S(2)}) copy-start(f32[1,1,8,16,12]{3,2,1,4,0:T(8,128)S(1)} %stack.34) | copy-start | bytes 18436
  93.0 20.0 %collective-permute-start.8 = (f32[2,1,8,8,12]{3,2,1,4,0:T(8,128)}, f32[2,1,8,8,12]{3,2,1,4,0:T(8,128)}, u32[]{:S(2)}, u32[]{:S(2)}) collective-permute-start(f32[2,1,8,8,12]{3,2,1,4,0:T(8,128)} %get-tuple-element.16), channel_id=1, source_target_pairs={{0,1},{1,2},{2,3},{4,5},{5,6},{6,7},{8,9},{9,10},{10,11},{12,13},{... | collective-permute-start | bytes 18440 | tf_op jit(solution)/shard_map/ppermute | solution.py:19
  97.5 15.6 %collective-permute-start.9 = (f32[2,1,8,8,12]{3,2,1,4,0:T(8,128)}, f32[2,1,8,8,12]{3,2,1,4,0:T(8,128)}, u32[]{:S(2)}, u32[]{:S(2)}) collective-permute-start(f32[2,1,8,8,12]{3,2,1,4,0:T(8,128)} %get-tuple-element.17), channel_id=1, source_target_pairs={{1,0},{2,1},{3,2},{5,4},{6,5},{7,6},{9,8},{10,9},{11,10},{13,12},{... | collective-permute-start | bytes 18440 | tf_op jit(solution)/shard_map/ppermute | solution.py:20
  105.4 7.7 %copy-start.9 = (f32[1,1,8,16,12]{3,2,4,1,0:T(8,128)S(1)}, f32[1,1,8,16,12]{3,2,4,1,0:T(8,128)}, u32[]{:S(2)}) copy-start(f32[1,1,8,16,12]{3,2,4,1,0:T(8,128)} %stack.33) | copy-start | bytes 18436
  105.4 7.7 %copy-start.11 = (f32[1,1,8,16,12]{3,2,1,4,0:T(8,128)S(1)}, f32[1,1,8,16,12]{3,2,1,4,0:T(8,128)}, u32[]{:S(2)}) copy-start(f32[1,1,8,16,12]{3,2,1,4,0:T(8,128)} %copy-done.10) | copy-start | bytes 18436
  114.1 16.7 %collective-permute-start.10 = (f32[2,1,8,32,12]{3,2,1,4,0:T(8,128)S(1)}, f32[2,1,8,32,12]{3,2,1,4,0:T(8,128)S(1)}, u32[]{:S(2)}, u32[]{:S(2)}) collective-permute-start(f32[2,1,8,32,12]{3,2,1,4,0:T(8,128)S(1)} %pad_maximum_fusion.8), channel_id=1, source_target_pairs={{0,4},{4,8},{8,12},{1,5},{5,9},{9,13},{2,6},{6,10},{10,14},{3,7},{... | collective-permute-start | bytes 73736 | tf_op jit(solution)/shard_map/ppermute | solution.py:19
  116.9 13.9 %collective-permute-start.11 = (f32[2,1,8,32,12]{3,2,1,4,0:T(8,128)S(1)}, f32[2,1,8,32,12]{3,2,1,4,0:T(8,128)S(1)}, u32[]{:S(2)}, u32[]{:S(2)}) collective-permute-start(f32[2,1,8,32,12]{3,2,1,4,0:T(8,128)S(1)} %pad_maximum_fusion.8), channel_id=1, source_target_pairs={{4,0},{8,4},{12,8},{5,1},{9,5},{13,9},{6,2},{10,6},{14,10},{7,3},{... | collective-permute-start | bytes 73736 | tf_op jit(solution)/shard_map/ppermute | solution.py:20
  132.0 0.6 copy-start.14
  132.6 7.5 %copy-start = (bf16[768,12,128]{0,2,1:T(8,128)(2,1)S(1)}, bf16[768,12,128]{0,2,1:T(8,128)(2,1)}, u32[]{:S(2)}) copy-start(bf16[768,12,128]{0,2,1:T(8,128)(2,1)} %copy.49) | copy-start | bytes 7077892
  132.6 7.5 %copy-start.12 = (bf16[128,12,128]{2,1,0:T(8,128)(2,1)S(1)}, bf16[128,12,128]{2,1,0:T(8,128)(2,1)}, u32[]{:S(2)}) copy-start(bf16[128,12,128]{2,1,0:T(8,128)(2,1)} %reshape.233) | copy-start | bytes 1179652
where the time goes:
time: 150 us; the launch traced here: 148 us
  local copies, waits for them, and re-layouts  59.6 us (40%)
  starting transfers between devices  34.8 us (23%)
  other arithmetic  25.9 us (17%)
  matrix products  25.2 us (17%)
  waiting for transfers between devices  1.61 us (1%)
    ppermute x6, starting transfers between devices, padded(): before = lax.ppermute(last, axis, up)  24.8 us
    broadcast_in_dim x6, local copies, waits for them, and re-layouts, window_mask(): jnp.broadcast_to(allowed[:, None, :, None, :, None, :, None, :, None, :,...  16 us
    concatenate x6, other arithmetic, padded(): value = jnp.concatenate([before, value, after], axis=dim)  13.2 us
    ppermute x6, starting transfers between devices, padded(): after = lax.ppermute(first, axis, down)  10 us
    another operation x2, local copies, waits for them, and re-layouts, on_device(): pair_ext[0].reshape(ext_count, heads, HD)  7.66 us
    another operation x2, local copies, waits for them, and re-layouts, on_device(): pair_ext[1].reshape(ext_count, heads, HD)  7.64 us
    dot_general x1, matrix products, own_key_grads(): jnp.einsum('hkq,qhd->khd', grad_scores, query_g, preferred_element_type=j...  6.53 us
    dot_general x1, matrix products, forward_stats(): jnp.einsum('hqk,khd->qhd', probs_low, value_g, preferred_element_type=jnp...  5.69 us
  transfers between devices with their start and end apart: 12, of which 2 were waited for; matrix products, arithmetic and copies ran while one was open for 60% of the time, Pallas kernels for 0%

commit v1 on v0

v1 whole, which is shorter than its diff:
```python
import math

import jax
import jax.numpy as jnp
from jax import lax
from jax.experimental import pallas as pl
from jax.experimental.pallas import tpu as pltpu
from jax.sharding import PartitionSpec as P

HD = 128
TH = 4
TW = 8
STEP_HEADS = 3
NEG = -1e30
FLOOR = -1e29
SCALE = HD ** (-0.5)
SCALE2 = SCALE * math.log2(math.e)


def pair_lists(count):
    even = [(i, i + 1) for i in range(0, count - 1, 2)]
    odd = [(i, i + 1) for i in range(1, count - 1, 2)]
    far_a = [(i, i + 2) for i in range(count - 2) if i % 4 in (0, 1)]
    far_b = [(i, i + 2) for i in range(count - 2) if i % 4 in (2, 3)]
    return [pairs + [(j, i) for i, j in pairs] for pairs in (even, odd, far_a, far_b)]


def swap(value, axis, pairs):
    return lax.ppermute(value, axis, pairs)


def bit_table(window_ref):
    bits = jnp.int32(0)
    for i in range(window_ref.shape[0]):
        code = (window_ref[i, 0] + 1) * 9 + (window_ref[i, 1] + 1) * 3 + (window_ref[i, 2] + 1)
        bits = bits | jnp.left_shift(jnp.int32(1), code)
    return bits


def position_facts(place_ref, frame_count, strip_count):
    frame = place_ref[0]
    strip = place_ref[1]
    step_f = 1 - 2 * (frame & 1)
    step_s = 1 - 2 * (strip & 1)
    return (
        frame,
        step_f,
        step_s,
        ((frame + step_f >= 0) & (frame + step_f < frame_count)).astype(jnp.int32),
        ((frame - step_f >= 0) & (frame - step_f < frame_count)).astype(jnp.int32),
        ((strip + step_s >= 0) & (strip + step_s < strip_count)).astype(jnp.int32),
        ((strip - step_s >= 0) & (strip - step_s < strip_count)).astype(jnp.int32),
    )


def fill_bias(bias_ref, window_ref, place_ref, frame_count, strip_count, height, strip):
    bits = bit_table(window_ref)
    _, step_f, step_s, has_fa, has_fb, has_sa, has_sb = position_facts(
        place_ref, frame_count, strip_count
    )
    rows = height * strip
    half = height * TW
    tiles = strip // TW
    col_a = jnp.where(step_s > 0, tiles, -1)
    col_b = jnp.where(step_s > 0, -1, tiles)
    for slot, (off_time, has_f) in enumerate(((0, 1), (-step_f, has_fa), (step_f, has_fb))):
        start = 0
        for length, wide, k_col, has_s in (
            (rows, strip, None, 1),
            (half, TW, col_a, has_sa),
            (half, TW, col_b, has_sb),
        ):
            key_idx = lax.broadcasted_iota(jnp.int32, (length, rows), 0)
            query_idx = lax.broadcasted_iota(jnp.int32, (length, rows), 1)
            off_high = key_idx // (wide * TH) - query_idx // (strip * TH)
            k_wide = (key_idx % wide) // TW if k_col is None else k_col
            off_wide = k_wide - (query_idx % strip) // TW
            near = (jnp.abs(off_wide) <= 1) & (jnp.abs(off_high) <= 1)
            code = (off_time + 1) * 9 + (off_high + 1) * 3 + (off_wide + 1)
            listed = jnp.right_shift(bits, jnp.where(near, code, 0)) & 1
            flag = jnp.where(near, listed, 0) * (has_f * has_s)
            bias_ref[start : start + length, slot * rows : (slot + 1) * rows] = jnp.where(
                flag == 1, jnp.float32(0), jnp.float32(NEG)
            )
            start += length


def head_rows(ref, head):
    block = ref[0, :, :, head * HD : (head + 1) * HD]
    return block.reshape(-1, HD)


def load_queries(refs, head):
    return jnp.concatenate([head_rows(ref, head) for ref in refs], axis=0)


def load_keys(own_ref, a_ref, b_ref, which, head):
    lanes = slice(head * HD, (head + 1) * HD)
    return jnp.concatenate(
        [head_rows(own_ref, head), a_ref[which, :, lanes], b_ref[which, :, lanes]], axis=0
    )


def dot_nt(a, b):
    return lax.dot_general(a, b, (((1,), (1,)), ((), ())), preferred_element_type=jnp.float32)


def stats_kernel(frame_count, strip_count, height, strip, *refs):
    (window_ref, place_ref, q0, qa, qb, g0, ga, gb, k0, v0, ha, hb, own_out, a_out, b_out, c_out, d_out, bias_ref) = refs
    rows = height * strip

    @pl.when(pl.program_id(0) == 0)
    def _():
        fill_bias(bias_ref, window_ref, place_ref, frame_count, strip_count, height, strip)

    far_slot_a = ((place_ref[0] & 3) == 0) | ((place_ref[0] & 3) == 3)
    for head in range(STEP_HEADS):
        query = load_queries((q0, qa, qb), head)
        grad = load_queries((g0, ga, gb), head)
        key = load_keys(k0, ha, hb, 0, head)
        value = load_keys(v0, ha, hb, 1, head)
        scores = dot_nt(key, query) * SCALE2 + bias_ref[...]
        grad_probs = dot_nt(value, grad)
        top = jnp.max(scores, axis=0, keepdims=True)
        expo = jnp.exp2(scores - top)
        total = jnp.sum(expo, axis=0, keepdims=True)
        delta = jnp.sum(expo * grad_probs, axis=0, keepdims=True) / total
        lse = top + jnp.log2(total)
        parts = [
            jnp.concatenate([lse[:, i * rows : (i + 1) * rows], delta[:, i * rows : (i + 1) * rows]], axis=0)
            for i in range(3)
        ]
        own_out[head] = jnp.concatenate(parts, axis=0)
        a_out[head] = jnp.concatenate([parts[0], parts[1]], axis=0)
        b_out[head] = jnp.concatenate([parts[0], parts[2]], axis=0)
        c_out[head] = jnp.where(far_slot_a, parts[1], parts[2])
        d_out[head] = jnp.where(far_slot_a, parts[2], parts[1])


def merge(parts):
    top = parts[0][0]
    for lse, _ in parts[1:]:
        top = jnp.maximum(top, lse)
    weight_sum = jnp.zeros_like(top)
    delta_sum = jnp.zeros_like(top)
    for lse, delta in parts:
        weight = jnp.exp2(lse - top)
        weight_sum = weight_sum + weight
        delta_sum = delta_sum + weight * delta
    return jnp.maximum(top + jnp.log2(weight_sum), FLOOR), delta_sum / weight_sum


def grads_kernel(frame_count, strip_count, height, strip, *refs):
    (window_ref, place_ref, q0, qa, qb, g0, ga, gb, k0, v0, ha, hb, own_st, a_st, b_st, c_st, d_st, dk_out, dv_out, ra_out, rb_out, bias_ref) = refs
    rows = height * strip
    half = height * TW

    @pl.when(pl.program_id(0) == 0)
    def _():
        fill_bias(bias_ref, window_ref, place_ref, frame_count, strip_count, height, strip)

    frame, step_f, _, has_fa, has_fb, _, _ = position_facts(place_ref, frame_count, strip_count)
    beyond_a = frame + 2 * step_f
    beyond_b = frame - 2 * step_f
    has_ba = (beyond_a >= 0) & (beyond_a < frame_count)
    has_bb = (beyond_b >= 0) & (beyond_b < frame_count)
    far_slot_a = ((frame & 3) == 0) | ((frame & 3) == 3)

    def part(block, row, exists):
        lse = block[row : row + 1, :]
        return (lse if exists is None else jnp.where(exists, lse, NEG), block[row + 1 : row + 2, :])

    for head in range(STEP_HEADS):
        lanes = slice(head * HD, (head + 1) * HD)
        own, from_a, from_b, from_c, from_d = (r[head] for r in (own_st, a_st, b_st, c_st, d_st))
        far_a = jnp.where(far_slot_a, from_c, from_d)
        far_b = jnp.where(far_slot_a, from_d, from_c)
        merged = [
            merge([part(own, 0, None), part(from_a, 2, has_fa == 1), part(from_b, 2, has_fb == 1)]),
            merge([part(own, 2, None), part(from_a, 0, has_fa == 1), part(far_a, 0, has_ba)]),
            merge([part(own, 4, None), part(from_b, 0, has_fb == 1), part(far_b, 0, has_bb)]),
        ]
        lse = jnp.concatenate([m[0] for m in merged], axis=1)
        delta = jnp.concatenate([m[1] for m in merged], axis=1)
        query = load_queries((q0, qa, qb), head)
        grad = load_queries((g0, ga, gb), head)
        key = load_keys(k0, ha, hb, 0, head)
        value = load_keys(v0, ha, hb, 1, head)
        scores = dot_nt(key, query) * SCALE2 + bias_ref[...]
        probs = jnp.exp2(scores - lse)
        grad_probs = dot_nt(value, grad)
        grad_scores = (probs * (grad_probs - delta) * SCALE).astype(jnp.bfloat16)
        value_part = jnp.dot(probs.astype(jnp.bfloat16), grad, preferred_element_type=jnp.float32)
        key_part = jnp.dot(grad_scores, query, preferred_element_type=jnp.float32)
        dk_out[:, lanes] = key_part[:rows]
        dv_out[:, lanes] = value_part[:rows]
        for out, lo in ((ra_out, rows), (rb_out, rows + half)):
            out[0, :, lanes] = key_part[lo : lo + half].astype(jnp.bfloat16)
            out[1, :, lanes] = value_part[lo : lo + half].astype(jnp.bfloat16)


def finish_kernel(height, strip, place_ref, dk, dv, ra, rb, dk_out, dv_out):
    even = (place_ref[1] & 1) == 0
    for which, (part, out) in enumerate(((dk, dk_out), (dv, dv_out))):
        from_a = ra[which].astype(jnp.float32).reshape(height, TW, -1)
        from_b = rb[which].astype(jnp.float32).reshape(height, TW, -1)
        full = part[...].reshape(height, strip, -1)
        left = full[:, :TW] + jnp.where(even, from_b, from_a)
        right = full[:, TW:] + jnp.where(even, from_a, from_b)
        out[0] = jnp.concatenate([left, right], axis=1).astype(jnp.bfloat16)


def on_device(queries, keys, values, grad_out, window):
    _, height, strip, chans = queries.shape
    heads = chans // HD
    rows = height * strip
    half = height * TW
    frame_count = lax.axis_size("frame")
    strip_count = lax.axis_size("tile")
    frame_even, frame_odd, far_c, far_d = pair_lists(frame_count)
    tile_even, tile_odd, _, _ = pair_lists(strip_count)
    frame_pos = lax.axis_index("frame")
    strip_pos = lax.axis_index("tile")
    place = jnp.stack([frame_pos, strip_pos]).astype(jnp.int32)

    qa = swap(queries, "frame", frame_even)
    qb = swap(queries, "frame", frame_odd)
    ga = swap(grad_out, "frame", frame_even)
    gb = swap(grad_out, "frame", frame_odd)

    even = (strip_pos & 1) == 0
    start_a = jnp.where(even, strip - TW, 0)
    start_b = jnp.where(even, 0, strip - TW)

    def edge(start):
        cut = [lax.dynamic_slice_in_dim(x[0], start, TW, axis=1).reshape(half, chans) for x in (keys, values)]
        return jnp.stack(cut)

    ha = swap(edge(start_a), "tile", tile_even)
    hb = swap(edge(start_b), "tile", tile_odd)

    steps = heads // STEP_HEADS
    lanes = STEP_HEADS * HD
    wide_spec = pl.BlockSpec((1, height, strip, lanes), lambda i: (0, 0, 0, i))
    halo_spec = pl.BlockSpec((2, half, lanes), lambda i: (0, 0, i))
    flat_spec = pl.BlockSpec((rows, lanes), lambda i: (0, i))
    smem = pl.BlockSpec(memory_space=pltpu.SMEM)

    def stat_spec(count):
        return pl.BlockSpec((STEP_HEADS, count, rows), lambda i: (i, 0, 0))

    def stat_shape(count):
        return jax.ShapeDtypeStruct((heads, count, rows), jnp.float32)

    data = (queries, qa, qb, grad_out, ga, gb, keys, values, ha, hb)
    data_specs = [smem, smem] + [wide_spec] * 8 + [halo_spec] * 2
    sizes = (6, 4, 4, 2, 2)
    bias = pltpu.VMEM((rows + 2 * half, 3 * rows), jnp.float32)
    own_st, a_st, b_st, c_st, d_st = pl.pallas_call(
        lambda *refs: stats_kernel(frame_count, strip_count, height, strip, *refs),
        name="stats",
        grid=(steps,),
        in_specs=data_specs,
        out_specs=[stat_spec(n) for n in sizes],
        out_shape=[stat_shape(n) for n in sizes],
        scratch_shapes=[bias],
    )(window, place, *data)

    a_st = swap(a_st, "frame", frame_even)
    b_st = swap(b_st, "frame", frame_odd)
    if far_c:
        c_st = swap(c_st, "frame", far_c)
    if far_d:
        d_st = swap(d_st, "frame", far_d)

    dk, dv, ra, rb = pl.pallas_call(
        lambda *refs: grads_kernel(frame_count, strip_count, height, strip, *refs),
        name="grads",
        grid=(steps,),
        in_specs=data_specs + [stat_spec(n) for n in sizes],
        out_specs=[flat_spec, flat_spec, halo_spec, halo_spec],
        out_shape=[jax.ShapeDtypeStruct((rows, chans), jnp.float32)] * 2
        + [jax.ShapeDtypeStruct((2, half, chans), jnp.bfloat16)] * 2,
        scratch_shapes=[bias],
    )(window, place, *data, own_st, a_st, b_st, c_st, d_st)

    ra = swap(ra, "tile", tile_even)
    rb = swap(rb, "tile", tile_odd)
    return pl.pallas_call(
        lambda *refs: finish_kernel(height, strip, *refs),
        name="finish",
        grid=(steps,),
        in_specs=[smem, flat_spec, flat_spec, halo_spec, halo_spec],
        out_specs=[wide_spec, wide_spec],
        out_shape=[jax.ShapeDtypeStruct(keys.shape, jnp.bfloat16)] * 2,
    )(place, dk, dv, ra, rb)


def solution(mesh):
    spec = P(("clip", "frame"), None, "tile", None)
    return jax.shard_map(
        on_device,
        mesh=mesh,
        in_specs=(spec, spec, spec, spec, P()),
        out_specs=(spec, spec),
        check_vma=False,
    )
```

time: 150 us -> 60.8 us (0.41)
  local copies, waits for them, and re-layouts: 59.6 us -> 5.59 us
  other arithmetic: 25.9 us -> 0.69 us
  matrix products: 25.2 us -> 0 us
  Pallas kernels: 0 us -> 15.5 us
  waiting for transfers between devices: 1.61 us -> 14.7 us
  starting transfers between devices: 34.8 us -> 22.9 us
    dot_general x5 -> x0, matrix products: 25.2 us -> none  [the longest x1 6.53 us: own_key_grads(): jnp.einsum('hkq,qhd->khd', grad_scores, query_g, preferred_element_type=j...]
    another operation x10 -> x1, local copies, waits for them, and re-layouts: 25.4 us -> 1.27 us  [edge(): return jnp.stack(cut)]
    broadcast_in_dim x6 -> x0, local copies, waits for them, and re-layouts: 16 us -> none  [window_mask(): jnp.broadcast_to(allowed[:, None, :, None, :, None, :, None, :, None, :,...]
    pallas_call x0 -> x3, Pallas kernels: none -> 15.5 us  [the longest x1 6.65 us: on_device(): pl.pallas_call(lambda *refs: grads_kernel(frame_count, strip_count, heigh...]
    concatenate x6 -> x0, other arithmetic: 13.2 us -> none  [padded(): value = jnp.concatenate([before, value, after], axis=dim)]
    ppermute x12 -> x11, waiting for transfers between devices: 1.61 us -> 14.7 us  [swap(): return lax.ppermute(value, axis, pairs)]
    ppermute x12 -> x11, starting transfers between devices: 34.8 us -> 22.9 us  [swap(): return lax.ppermute(value, axis, pairs)]
    convert_element_type x6 -> x0, local copies, waits for them, and re-layouts: 7.57 us -> none  [the longest x4 3.87 us: on_device(): return (key_out.astype(jnp.bfloat16), value_out.astype(jnp.bfloat16))]
  transfers between devices with their start and end apart: 12 -> 11, of which waited for: 2 -> 3; matrix products, arithmetic and copies ran while one was open for 60% -> 4% of each run, Pallas kernels for 0% -> 0%
where the time goes in v1:
time: 60.8 us; the launch traced here: 60.2 us
  starting transfers between devices  22.9 us (38%)
  Pallas kernels  15.5 us (25%)
  waiting for transfers between devices  14.7 us (24%)
  local copies, waits for them, and re-layouts  5.59 us (9%)
  between operations  0.8 us (1%)
  other arithmetic  0.69 us (1%)
    ppermute x11, starting transfers between devices, swap(): return lax.ppermute(value, axis, pairs)  22.9 us
    ppermute x11, waiting for transfers between devices, swap(): return lax.ppermute(value, axis, pairs)  14.7 us
    pallas_call x1, Pallas kernels, on_device(): pl.pallas_call(lambda *refs: grads_kernel(frame_count, strip_count, heigh...  6.65 us
    pallas_call x1, Pallas kernels, on_device(): pl.pallas_call(lambda *refs: stats_kernel(frame_count, strip_count, heigh...  5.22 us
    unnamed x25, local copies, waits for them, and re-layouts  4.33 us
    pallas_call x1, Pallas kernels, on_device(): pl.pallas_call(lambda *refs: finish_kernel(height, strip, *refs), name='f...  3.64 us
    another operation x1, local copies, waits for them, and re-layouts, edge(): return jnp.stack(cut)  1.27 us
  transfers between devices with their start and end apart: 11, of which 3 were waited for; matrix products, arithmetic and copies ran while one was open for 4% of the time, Pallas kernels for 0%

profile of v1, /device:TPU:1, one launch (start us, length us, event | category | flops | bytes accessed | tf_op | source)
XLA Modules:
  0.0 60.2 jit_solution(4105778633445716314)
XLA Ops:
  0.6 0.7 %collective-permute-start.1 = (bf16[1,8,16,1536]{3,2,1,0:T(8,128)(2,1)}, bf16[1,8,16,1536]{3,2,1,0:T(8,128)(2,1)S(1)}, u32[]{:S(2)}, u32[]{:S(2)}) collective-permute-start(bf16[1,8,16,1536]{3,2,1,0:T(8,128)(2,1)} %refs_2_.3), channel_id=1, source_target_pairs={{4,8},{8,4},{5,9},{9,5},{6,10},{10,6},{7,11},{11,7},{20,24},{24,20... | collective-permute-start | bytes 1179656 | tf_op jit(solution)/shard_map/ppermute | solution.py:29
  1.3 4.7 %collective-permute-start = (bf16[1,8,16,1536]{3,2,1,0:T(8,128)(2,1)}, bf16[1,8,16,1536]{3,2,1,0:T(8,128)(2,1)S(1)}, u32[]{:S(2)}, u32[]{:S(2)}) collective-permute-start(bf16[1,8,16,1536]{3,2,1,0:T(8,128)(2,1)} %refs_2_.3), channel_id=1, source_target_pairs={{0,4},{8,12},{4,0},{12,8},{1,5},{9,13},{5,1},{13,9},{2,6},{10,14},... | collective-permute-start | bytes 1179656 | tf_op jit(solution)/shard_map/ppermute | solution.py:29
  6.0 0.7 %collective-permute-start.3 = (bf16[1,8,16,1536]{3,2,1,0:T(8,128)(2,1)}, bf16[1,8,16,1536]{3,2,1,0:T(8,128)(2,1)S(1)}, u32[]{:S(2)}, u32[]{:S(2)}) collective-permute-start(bf16[1,8,16,1536]{3,2,1,0:T(8,128)(2,1)} %refs_5_.3), channel_id=1, source_target_pairs={{4,8},{8,4},{5,9},{9,5},{6,10},{10,6},{7,11},{11,7},{20,24},{24,20... | collective-permute-start | bytes 1179656 | tf_op jit(solution)/shard_map/ppermute | solution.py:29
  6.7 1.5 %collective-permute-start.2 = (bf16[1,8,16,1536]{3,2,1,0:T(8,128)(2,1)}, bf16[1,8,16,1536]{3,2,1,0:T(8,128)(2,1)S(1)}, u32[]{:S(2)}, u32[]{:S(2)}) collective-permute-start(bf16[1,8,16,1536]{3,2,1,0:T(8,128)(2,1)} %refs_5_.3), channel_id=1, source_target_pairs={{0,4},{8,12},{4,0},{12,8},{1,5},{9,13},{5,1},{13,9},{2,6},{10,14},... | collective-permute-start | bytes 1179656 | tf_op jit(solution)/shard_map/ppermute | solution.py:29
  8.2 1.3 %dynamic-slice_bitcast_fusion = (bf16[1,64,1536]{2,1,0:T(8,128)(2,1)S(1)}, bf16[1,64,1536]{2,1,0:T(8,128)(2,1)S(1)}, bf16[1,64,1536]{2,1,0:T(8,128)(2,1)S(1)}, bf16[1,64,1536]{2,1,0:T(8,128)(2,1)S(1)}) fusion(bf16[1,8,16,1536]{3,2,1,0:T(8,128)(2,1)} %refs_9_.3, s32[]{:T(128)S(6)} %select_n.12, s32[]{:T(128)S(6)} %select_n.11, bf16[1,8,16,1536]{3,2,1,0:T(8,128)(2,1)} %refs_8_.3), kind=kLoop, calls=%fused_computation.2 | loop fusion | bytes 1572872 | tf_op jit(solution)/shard_map/stack;reshape | solution.py:237
  9.5 1.6 %collective-permute-start.4 = (bf16[2,64,1536]{2,1,0:T(8,128)(2,1)S(1)}, bf16[2,64,1536]{2,1,0:T(8,128)(2,1)S(1)}, u32[]{:S(2)}, u32[]{:S(2)}) collective-permute-start(bf16[2,64,1536]{2,1,0:T(8,128)(2,1)S(1)} %pad_maximum_fusion), channel_id=1, source_target_pairs={{0,1},{2,3},{1,0},{3,2},{4,5},{6,7},{5,4},{7,6},{8,9},{10,11},{9,8... | collective-permute-start | bytes 1179656 | tf_op jit(solution)/shard_map/ppermute | solution.py:29
  11.1 0.0 copy-start
  11.2 3.1 %collective-permute-start.5 = (bf16[2,64,1536]{2,1,0:T(8,128)(2,1)S(1)}, bf16[2,64,1536]{2,1,0:T(8,128)(2,1)S(1)}, u32[]{:S(2)}, u32[]{:S(2)}) collective-permute-start(bf16[2,64,1536]{2,1,0:T(8,128)(2,1)S(1)} %pad_maximum_fusion.1), channel_id=1, source_target_pairs={{1,2},{2,1},{5,6},{6,5},{9,10},{10,9},{13,14},{14,13},{17,18},{18,... | collective-permute-start | bytes 1179656 | tf_op jit(solution)/shard_map/ppermute | solution.py:29
  14.2 0.0 copy-start.11
  14.2 0.7 %copy-done.11 = s32[18,3]{0,1:T(4,128)S(1)} copy-done((s32[18,3]{0,1:T(4,128)S(1)}, s32[18,3]{0,1:T(4,128)}, u32[]{:S(2)}) %copy-start.11) | copy-done | bytes 240
  14.9 0.7 %copy.8.refs_0_ = s32[18,3]{1,0:T(8,128)} copy(s32[18,3]{0,1:T(4,128)S(1)} %copy-done.11) | data formatting | bytes 432 | tf_op args[4]
  15.6 0.6 %pad_add_fusion.refs_1_.refs_0_ = s32[2]{0:T(128)} fusion(s32[1]{0:T(128)} %bitcast.1, s32[1]{0:T(128)} %bitcast), kind=kLoop, calls=%fused_computation.6 | loop fusion | flops 2 | bytes 16 | tf_op jit(solution)/shard_map/stack | solution.py:224
  16.2 0.0 collective-permute-done.refs_3_
  16.2 0.0 collective-permute-done.3.refs_7_
  16.2 7.0 %collective-permute-done.2.refs_6_ = bf16[1,8,16,1536]{3,2,1,0:T(8,128)(2,1)S(1)} collective-permute-done((bf16[1,8,16,1536]{3,2,1,0:T(8,128)(2,1)}, bf16[1,8,16,1536]{3,2,1,0:T(8,128)(2,1)S(1)}, u32[]{:S(2)}, u32[]{:S(2)}) %collective-permute-start.2) | collective-permute-done | bytes 393248 | tf_op jit(solution)/shard_map/ppermute | solution.py:29
  23.2 0.7 %copy-done.3 = bf16[1,8,16,1536]{3,2,1,0:T(8,128)(2,1)} copy-done((bf16[1,8,16,1536]{3,2,1,0:T(8,128)(2,1)}, bf16[1,8,16,1536]{3,2,1,0:T(8,128)(2,1)S(1)}, u32[]{:S(2)}) %copy-start.3) | copy-done | bytes 393240
  24.0 0.1 copy-done.4
  24.1 0.7 %copy-done.5 = bf16[2,64,1536]{2,1,0:T(8,128)(2,1)} copy-done((bf16[2,64,1536]{2,1,0:T(8,128)(2,1)}, bf16[2,64,1536]{2,1,0:T(8,128)(2,1)S(1)}, u32[]{:S(2)}) %copy-start.5) | copy-done | bytes 393240
  24.8 5.2 %stats.1 = (f32[12,6,128]{2,1,0:T(8,128)}, f32[12,4,128]{2,1,0:T(4,128)}, f32[12,4,128]{2,1,0:T(4,128)}, f32[12,2,128]{2,1,0:T(2,128)}, f32[12,2,128]{2,1,0:T(2,128)}) custom-call(s32[18,3]{1,0:T(8,128)} %copy.8.refs_0_, s32[2]{0:T(128)} %pad_add_fusion.refs_1_.refs_0_, bf16[1,8,16,1536]{3,2,1,0:T(8,128)(2,1)} %refs_2_.3, ...), custom_call_target="tpu_custom_call" | custom-call | tf_op jit(solution)/shard_map/stats/pallas_call | solution.py:259
  30.1 2.0 %collective-permute-start.6 = (f32[12,4,128]{2,1,0:T(4,128)}, f32[12,4,128]{2,1,0:T(4,128)S(1)}, u32[]{:S(2)}, u32[]{:S(2)}) collective-permute-start(f32[12,4,128]{2,1,0:T(4,128)} %get-tuple-element.12), channel_id=1, source_target_pairs={{0,4},{8,12},{4,0},{12,8},{1,5},{9,13},{5,1},{13,9},{2,6},{10,14},... | collective-permute-start | bytes 73736 | tf_op jit(solution)/shard_map/ppermute | solution.py:29
  32.1 0.7 %collective-permute-start.7 = (f32[12,4,128]{2,1,0:T(4,128)}, f32[12,4,128]{2,1,0:T(4,128)S(1)}, u32[]{:S(2)}, u32[]{:S(2)}) collective-permute-start(f32[12,4,128]{2,1,0:T(4,128)} %get-tuple-element.13), channel_id=1, source_target_pairs={{4,8},{8,4},{5,9},{9,5},{6,10},{10,6},{7,11},{11,7},{20,24},{24,20... | collective-permute-start | bytes 73736 | tf_op jit(solution)/shard_map/ppermute | solution.py:29
  32.7 2.5 %collective-permute-start.8 = (f32[12,2,128]{2,1,0:T(2,128)}, f32[12,2,128]{2,1,0:T(2,128)S(1)}, u32[]{:S(2)}, u32[]{:S(2)}) collective-permute-start(f32[12,2,128]{2,1,0:T(2,128)} %get-tuple-element.14), channel_id=1, source_target_pairs={{0,8},{4,12},{8,0},{12,4},{1,9},{5,13},{9,1},{13,5},{2,10},{6,14},... | collective-permute-start | bytes 36872 | tf_op jit(solution)/shard_map/ppermute | solution.py:29
  35.3 1.5 %collective-permute-done.8.refs_15_ = f32[12,2,128]{2,1,0:T(2,128)S(1)} collective-permute-done((f32[12,2,128]{2,1,0:T(2,128)}, f32[12,2,128]{2,1,0:T(2,128)S(1)}, u32[]{:S(2)}, u32[]{:S(2)}) %collective-permute-start.8) | collective-permute-done | bytes 12320 | tf_op jit(solution)/shard_map/ppermute | solution.py:29
  36.8 0.6 copy-done.10
  37.3 0.0 copy-done.8
  37.3 0.0 copy-done.9
  37.4 6.7 %grads.1 = (f32[128,1536]{1,0:T(8,128)}, f32[128,1536]{1,0:T(8,128)}, bf16[2,64,1536]{2,1,0:T(8,128)(2,1)}, bf16[2,64,1536]{2,1,0:T(8,128)(2,1)}) custom-call(s32[18,3]{1,0:T(8,128)} %copy.8.refs_0_, s32[2]{0:T(128)} %pad_add_fusion.refs_1_.refs_0_, bf16[1,8,16,1536]{3,2,1,0:T(8,128)(2,1)} %refs_2_.3, bf16[1,8,16,1536]{3,2,1,0:T(8,128)(2,1)} %copy-done.1, ...), custom_call_target="tpu_custom_call" | custom-call | tf_op jit(solution)/shard_map/grads/pallas_call | solution.py:276
  44.0 2.5 %collective-permute-start.9 = (bf16[2,64,1536]{2,1,0:T(8,128)(2,1)}, bf16[2,64,1536]{2,1,0:T(8,128)(2,1)S(1)}, u32[]{:S(2)}, u32[]{:S(2)}) collective-permute-start(bf16[2,64,1536]{2,1,0:T(8,128)(2,1)} %get-tuple-element.18), channel_id=1, source_target_pairs={{0,1},{2,3},{1,0},{3,2},{4,5},{6,7},{5,4},{7,6},{8,9},{10,11},{9,8... | collective-permute-start | bytes 1179656 | tf_op jit(solution)/shard_map/ppermute | solution.py:29
  46.5 3.0 %collective-permute-start.10 = (bf16[2,64,1536]{2,1,0:T(8,128)(2,1)}, bf16[2,64,1536]{2,1,0:T(8,128)(2,1)S(1)}, u32[]{:S(2)}, u32[]{:S(2)}) collective-permute-start(bf16[2,64,1536]{2,1,0:T(8,128)(2,1)} %get-tuple-element.19), channel_id=1, source_target_pairs={{1,2},{2,1},{5,6},{6,5},{9,10},{10,9},{13,14},{14,13},{17,18},{18,... | collective-permute-start | bytes 1179656 | tf_op jit(solution)/shard_map/ppermute | solution.py:29
  49.6 6.2 %collective-permute-done.10.refs_4_ = bf16[2,64,1536]{2,1,0:T(8,128)(2,1)S(1)} collective-permute-done((bf16[2,64,1536]{2,1,0:T(8,128)(2,1)}, bf16[2,64,1536]{2,1,0:T(8,128)(2,1)S(1)}, u32[]{:S(2)}, u32[]{:S(2)}) %collective-permute-start.10) | collective-permute-done | bytes 393248 | tf_op jit(solution)/shard_map/ppermute | solution.py:29
  55.8 0.7 %copy-done.7 = bf16[2,64,1536]{2,1,0:T(8,128)(2,1)} copy-done((bf16[2,64,1536]{2,1,0:T(8,128)(2,1)}, bf16[2,64,1536]{2,1,0:T(8,128)(2,1)S(1)}, u32[]{:S(2)}) %copy-start.7) | copy-done | bytes 393240
  56.6 3.6 %finish.1 = (bf16[1,8,16,1536]{3,2,1,0:T(8,128)(2,1)}, bf16[1,8,16,1536]{3,2,1,0:T(8,128)(2,1)}) custom-call(s32[2]{0:T(128)} %pad_add_fusion.refs_1_.refs_0_, f32[128,1536]{1,0:T(8,128)} %get-tuple-element.16.refs_1_, f32[128,1536]{1,0:T(8,128)} %get-tuple-element.17.refs_2_, bf16[2,64,1536]{2,1,0:T(8,128)(2,1)} %copy-done.6, bf16[2,64,1536]{2,1,0:T(8,128)(2,1)} %copy-done.7), custom_call_target="tpu_custom_call" | custom-call | tf_op jit(solution)/shard_map/finish/pallas_call | solution.py:289
  (22 shorter events, 0.1 us)
Async XLA Ops:
  0.6 10.5 %collective-permute-start.1 = (bf16[1,8,16,1536]{3,2,1,0:T(8,128)(2,1)}, bf16[1,8,16,1536]{3,2,1,0:T(8,128)(2,1)S(1)}, u32[]{:S(2)}, u32[]{:S(2)}) collective-permute-start(bf16[1,8,16,1536]{3,2,1,0:T(8,128)(2,1)} %refs_2_.3), channel_id=1, source_target_pairs={{4,8},{8,4},{5,9},{9,5},{6,10},{10,6},{7,11},{11,7},{20,24},{24,20... | collective-permute-start | bytes 1179656 | tf_op jit(solution)/shard_map/ppermute | solution.py:29
  1.3 14.9 %collective-permute-start = (bf16[1,8,16,1536]{3,2,1,0:T(8,128)(2,1)}, bf16[1,8,16,1536]{3,2,1,0:T(8,128)(2,1)S(1)}, u32[]{:S(2)}, u32[]{:S(2)}) collective-permute-start(bf16[1,8,16,1536]{3,2,1,0:T(8,128)(2,1)} %refs_2_.3), channel_id=1, source_target_pairs={{0,4},{8,12},{4,0},{12,8},{1,5},{9,13},{5,1},{13,9},{2,6},{10,14},... | collective-permute-start | bytes 1179656 | tf_op jit(solution)/shard_map/ppermute | solution.py:29
  6.0 10.2 %collective-permute-start.3 = (bf16[1,8,16,1536]{3,2,1,0:T(8,128)(2,1)}, bf16[1,8,16,1536]{3,2,1,0:T(8,128)(2,1)S(1)}, u32[]{:S(2)}, u32[]{:S(2)}) collective-permute-start(bf16[1,8,16,1536]{3,2,1,0:T(8,128)(2,1)} %refs_5_.3), channel_id=1, source_target_pairs={{4,8},{8,4},{5,9},{9,5},{6,10},{10,6},{7,11},{11,7},{20,24},{24,20... | collective-permute-start | bytes 1179656 | tf_op jit(solution)/shard_map/ppermute | solution.py:29
  6.7 16.5 %collective-permute-start.2 = (bf16[1,8,16,1536]{3,2,1,0:T(8,128)(2,1)}, bf16[1,8,16,1536]{3,2,1,0:T(8,128)(2,1)S(1)}, u32[]{:S(2)}, u32[]{:S(2)}) collective-permute-start(bf16[1,8,16,1536]{3,2,1,0:T(8,128)(2,1)} %refs_5_.3), channel_id=1, source_target_pairs={{0,4},{8,12},{4,0},{12,8},{1,5},{9,13},{5,1},{13,9},{2,6},{10,14},... | collective-permute-start | bytes 1179656 | tf_op jit(solution)/shard_map/ppermute | solution.py:29
  9.5 13.7 %collective-permute-start.4 = (bf16[2,64,1536]{2,1,0:T(8,128)(2,1)S(1)}, bf16[2,64,1536]{2,1,0:T(8,128)(2,1)S(1)}, u32[]{:S(2)}, u32[]{:S(2)}) collective-permute-start(bf16[2,64,1536]{2,1,0:T(8,128)(2,1)S(1)} %pad_maximum_fusion), channel_id=1, source_target_pairs={{0,1},{2,3},{1,0},{3,2},{4,5},{6,7},{5,4},{7,6},{8,9},{10,11},{9,8... | collective-permute-start | bytes 1179656 | tf_op jit(solution)/shard_map/ppermute | solution.py:29
  11.1 12.1 %copy-start = (bf16[1,8,16,1536]{3,2,1,0:T(8,128)(2,1)}, bf16[1,8,16,1536]{3,2,1,0:T(8,128)(2,1)S(1)}, u32[]{:S(2)}) copy-start(bf16[1,8,16,1536]{3,2,1,0:T(8,128)(2,1)S(1)} %collective-permute-done.1.refs_4_) | copy-start | bytes 1179652
  11.2 12.1 %collective-permute-start.5 = (bf16[2,64,1536]{2,1,0:T(8,128)(2,1)S(1)}, bf16[2,64,1536]{2,1,0:T(8,128)(2,1)S(1)}, u32[]{:S(2)}, u32[]{:S(2)}) collective-permute-start(bf16[2,64,1536]{2,1,0:T(8,128)(2,1)S(1)} %pad_maximum_fusion.1), channel_id=1, source_target_pairs={{1,2},{2,1},{5,6},{6,5},{9,10},{10,9},{13,14},{14,13},{17,18},{18,... | collective-permute-start | bytes 1179656 | tf_op jit(solution)/shard_map/ppermute | solution.py:29
  14.2 0.7 %copy-start.11 = (s32[18,3]{0,1:T(4,128)S(1)}, s32[18,3]{0,1:T(4,128)}, u32[]{:S(2)}) copy-start(s32[18,3]{0,1:T(4,128)} %param.9) | copy-start | bytes 652
  16.2 7.0 %copy-start.1 = (bf16[1,8,16,1536]{3,2,1,0:T(8,128)(2,1)}, bf16[1,8,16,1536]{3,2,1,0:T(8,128)(2,1)S(1)}, u32[]{:S(2)}) copy-start(bf16[1,8,16,1536]{3,2,1,0:T(8,128)(2,1)S(1)} %collective-permute-done.refs_3_) | copy-start | bytes 1179652
  16.2 7.0 %copy-start.2 = (bf16[1,8,16,1536]{3,2,1,0:T(8,128)(2,1)}, bf16[1,8,16,1536]{3,2,1,0:T(8,128)(2,1)S(1)}, u32[]{:S(2)}) copy-start(bf16[1,8,16,1536]{3,2,1,0:T(8,128)(2,1)S(1)} %collective-permute-done.3.refs_7_) | copy-start | bytes 1179652
  23.2 0.8 %copy-start.3 = (bf16[1,8,16,1536]{3,2,1,0:T(8,128)(2,1)}, bf16[1,8,16,1536]{3,2,1,0:T(8,128)(2,1)S(1)}, u32[]{:S(2)}) copy-start(bf16[1,8,16,1536]{3,2,1,0:T(8,128)(2,1)S(1)} %collective-permute-done.2.refs_6_) | copy-start | bytes 1179652
  23.2 0.9 %copy-start.4 = (bf16[2,64,1536]{2,1,0:T(8,128)(2,1)}, bf16[2,64,1536]{2,1,0:T(8,128)(2,1)S(1)}, u32[]{:S(2)}) copy-start(bf16[2,64,1536]{2,1,0:T(8,128)(2,1)S(1)} %collective-permute-done.4.refs_10_) | copy-start | bytes 1179652
  24.1 0.8 %copy-start.5 = (bf16[2,64,1536]{2,1,0:T(8,128)(2,1)}, bf16[2,64,1536]{2,1,0:T(8,128)(2,1)S(1)}, u32[]{:S(2)}) copy-start(bf16[2,64,1536]{2,1,0:T(8,128)(2,1)S(1)} %collective-permute-done.5.refs_11_) | copy-start | bytes 1179652
  30.1 6.7 %collective-permute-start.6 = (f32[12,4,128]{2,1,0:T(4,128)}, f32[12,4,128]{2,1,0:T(4,128)S(1)}, u32[]{:S(2)}, u32[]{:S(2)}) collective-permute-start(f32[12,4,128]{2,1,0:T(4,128)} %get-tuple-element.12), channel_id=1, source_target_pairs={{0,4},{8,12},{4,0},{12,8},{1,5},{9,13},{5,1},{13,9},{2,6},{10,14},... | collective-permute-start | bytes 73736 | tf_op jit(solution)/shard_map/ppermute | solution.py:29
  32.1 4.7 %collective-permute-start.7 = (f32[12,4,128]{2,1,0:T(4,128)}, f32[12,4,128]{2,1,0:T(4,128)S(1)}, u32[]{:S(2)}, u32[]{:S(2)}) collective-permute-start(f32[12,4,128]{2,1,0:T(4,128)} %get-tuple-element.13), channel_id=1, source_target_pairs={{4,8},{8,4},{5,9},{9,5},{6,10},{10,6},{7,11},{11,7},{20,24},{24,20... | collective-permute-start | bytes 73736 | tf_op jit(solution)/shard_map/ppermute | solution.py:29
  32.7 4.0 %collective-permute-start.8 = (f32[12,2,128]{2,1,0:T(2,128)}, f32[12,2,128]{2,1,0:T(2,128)S(1)}, u32[]{:S(2)}, u32[]{:S(2)}) collective-permute-start(f32[12,2,128]{2,1,0:T(2,128)} %get-tuple-element.14), channel_id=1, source_target_pairs={{0,8},{4,12},{8,0},{12,4},{1,9},{5,13},{9,1},{13,5},{2,10},{6,14},... | collective-permute-start | bytes 36872 | tf_op jit(solution)/shard_map/ppermute | solution.py:29
  36.7 0.6 copy-start.10
  36.7 0.6 %copy-start.8 = (f32[12,4,128]{2,1,0:T(4,128)}, f32[12,4,128]{2,1,0:T(4,128)S(1)}, u32[]{:S(2)}) copy-start(f32[12,4,128]{2,1,0:T(4,128)S(1)} %collective-permute-done.6.refs_13_) | copy-start | bytes 73732
  36.7 0.6 %copy-start.9 = (f32[12,4,128]{2,1,0:T(4,128)}, f32[12,4,128]{2,1,0:T(4,128)S(1)}, u32[]{:S(2)}) copy-start(f32[12,4,128]{2,1,0:T(4,128)S(1)} %collective-permute-done.7.refs_14_) | copy-start | bytes 73732
  44.0 5.6 %collective-permute-start.9 = (bf16[2,64,1536]{2,1,0:T(8,128)(2,1)}, bf16[2,64,1536]{2,1,0:T(8,128)(2,1)S(1)}, u32[]{:S(2)}, u32[]{:S(2)}) collective-permute-start(bf16[2,64,1536]{2,1,0:T(8,128)(2,1)} %get-tuple-element.18), channel_id=1, source_target_pairs={{0,1},{2,3},{1,0},{3,2},{4,5},{6,7},{5,4},{7,6},{8,9},{10,11},{9,8... | collective-permute-start | bytes 1179656 | tf_op jit(solution)/shard_map/ppermute | solution.py:29
  46.5 9.3 %collective-permute-start.10 = (bf16[2,64,1536]{2,1,0:T(8,128)(2,1)}, bf16[2,64,1536]{2,1,0:T(8,128)(2,1)S(1)}, u32[]{:S(2)}, u32[]{:S(2)}) collective-permute-start(bf16[2,64,1536]{2,1,0:T(8,128)(2,1)} %get-tuple-element.19), channel_id=1, source_target_pairs={{1,2},{2,1},{5,6},{6,5},{9,10},{10,9},{13,14},{14,13},{17,18},{18,... | collective-permute-start | bytes 1179656 | tf_op jit(solution)/shard_map/ppermute | solution.py:29
  49.6 6.2 %copy-start.6 = (bf16[2,64,1536]{2,1,0:T(8,128)(2,1)}, bf16[2,64,1536]{2,1,0:T(8,128)(2,1)S(1)}, u32[]{:S(2)}) copy-start(bf16[2,64,1536]{2,1,0:T(8,128)(2,1)S(1)} %collective-permute-done.9.refs_3_) | copy-start | bytes 1179652
  55.8 0.7 %copy-start.7 = (bf16[2,64,1536]{2,1,0:T(8,128)(2,1)}, bf16[2,64,1536]{2,1,0:T(8,128)(2,1)S(1)}, u32[]{:S(2)}) copy-start(bf16[2,64,1536]{2,1,0:T(8,128)(2,1)S(1)} %collective-permute-done.10.refs_4_) | copy-start | bytes 1179652

commit v2 on v1

v2 whole, which is shorter than its diff:
```python
import math

import jax
import jax.numpy as jnp
from jax import lax
from jax.experimental import pallas as pl
from jax.experimental.pallas import tpu as pltpu
from jax.sharding import PartitionSpec as P

HD = 128
TH = 4
TW = 8
FINISH_STEPS = 4
KERNEL_VMEM = 16 << 20
NEG = -1e30
FLOOR = -1e29
SCALE = HD ** (-0.5)
SCALE2 = SCALE * math.log2(math.e)


def pair_lists(count):
    even = [(i, i + 1) for i in range(0, count - 1, 2)]
    odd = [(i, i + 1) for i in range(1, count - 1, 2)]
    far_a = [(i, i + 2) for i in range(count - 2) if i % 4 in (0, 1)]
    far_b = [(i, i + 2) for i in range(count - 2) if i % 4 in (2, 3)]
    return [pairs + [(j, i) for i, j in pairs] for pairs in (even, odd, far_a, far_b)]


def swap(value, axis, pairs):
    return lax.ppermute(value, axis, pairs)


def bit_table(window_ref):
    bits = jnp.int32(0)
    for i in range(window_ref.shape[0]):
        code = (window_ref[i, 0] + 1) * 9 + (window_ref[i, 1] + 1) * 3 + (window_ref[i, 2] + 1)
        bits = bits | jnp.left_shift(jnp.int32(1), code)
    return bits


def position_facts(place_ref, frame_count, strip_count):
    frame = place_ref[0]
    strip = place_ref[1]
    step_f = 1 - 2 * (frame & 1)
    step_s = 1 - 2 * (strip & 1)
    return (
        frame,
        step_f,
        step_s,
        ((frame + step_f >= 0) & (frame + step_f < frame_count)).astype(jnp.int32),
        ((frame - step_f >= 0) & (frame - step_f < frame_count)).astype(jnp.int32),
        ((strip + step_s >= 0) & (strip + step_s < strip_count)).astype(jnp.int32),
        ((strip - step_s >= 0) & (strip - step_s < strip_count)).astype(jnp.int32),
    )


def fill_bias(bias_ref, slots, window_ref, place_ref, frame_count, strip_count, height, strip):
    bits = bit_table(window_ref)
    _, step_f, step_s, has_fa, has_fb, has_sa, has_sb = position_facts(
        place_ref, frame_count, strip_count
    )
    rows = height * strip
    half = height * TW
    tiles = strip // TW
    col_a = jnp.where(step_s > 0, tiles, -1)
    col_b = jnp.where(step_s > 0, -1, tiles)
    frames = ((0, 1), (-step_f, has_fa), (step_f, has_fb))
    for place, slot in enumerate(slots):
        off_time, has_f = frames[slot]
        start = 0
        for length, wide, k_col, has_s in (
            (rows, strip, None, 1),
            (half, TW, col_a, has_sa),
            (half, TW, col_b, has_sb),
        ):
            key_idx = lax.broadcasted_iota(jnp.int32, (length, rows), 0)
            query_idx = lax.broadcasted_iota(jnp.int32, (length, rows), 1)
            off_high = key_idx // (wide * TH) - query_idx // (strip * TH)
            k_wide = (key_idx % wide) // TW if k_col is None else k_col
            off_wide = k_wide - (query_idx % strip) // TW
            near = (jnp.abs(off_wide) <= 1) & (jnp.abs(off_high) <= 1)
            code = (off_time + 1) * 9 + (off_high + 1) * 3 + (off_wide + 1)
            listed = jnp.right_shift(bits, jnp.where(near, code, 0)) & 1
            flag = jnp.where(near, listed, 0) * (has_f * has_s)
            bias_ref[start : start + length, place * rows : (place + 1) * rows] = jnp.where(
                flag == 1, jnp.float32(0), jnp.float32(NEG)
            )
            start += length


def lanes_of(head):
    return slice(head * HD, (head + 1) * HD)


def head_rows(ref, head):
    return ref[0, :, :, lanes_of(head)].reshape(-1, HD)


def load_keys(own_ref, a_ref, b_ref, which, head):
    lanes = lanes_of(head)
    return jnp.concatenate(
        [head_rows(own_ref, head), a_ref[which, :, lanes], b_ref[which, :, lanes]], axis=0
    )


def dot_nt(a, b):
    return lax.dot_general(a, b, (((1,), (1,)), ((), ())), preferred_element_type=jnp.float32)


def local_stats(query, grad, key, value, bias):
    scores = dot_nt(key, query) * SCALE2 + bias
    grad_probs = dot_nt(value, grad)
    top = jnp.max(scores, axis=0, keepdims=True)
    expo = jnp.exp2(scores - top)
    total = jnp.sum(expo, axis=0, keepdims=True)
    delta = jnp.sum(expo * grad_probs, axis=0, keepdims=True) / total
    return expo, grad_probs, top, top + jnp.log2(total), delta


def own_kernel(sizes, window_ref, place_ref, q0, g0, k0, v0, ha, hb, part, expo_out, gp_out, bias_ref):
    fill_bias(bias_ref, (0,), window_ref, place_ref, *sizes)
    for head in range(part.shape[0]):
        key = load_keys(k0, ha, hb, 0, head)
        value = load_keys(v0, ha, hb, 1, head)
        expo, grad_probs, top, lse, delta = local_stats(
            head_rows(q0, head), head_rows(g0, head), key, value, bias_ref[...]
        )
        part[head] = jnp.concatenate([lse, delta, top], axis=0)
        expo_out[head] = expo
        gp_out[head] = grad_probs


def near_kernel(sizes, window_ref, place_ref, qa, qb, ga, gb, k0, v0, ha, hb, own_part, part, a_out, b_out, c_out, d_out, expo_out, gp_out, bias_ref):
    rows = sizes[2] * sizes[3]
    fill_bias(bias_ref, (1, 2), window_ref, place_ref, *sizes)
    far_slot_a = ((place_ref[0] & 3) == 0) | ((place_ref[0] & 3) == 3)
    for head in range(part.shape[0]):
        key = load_keys(k0, ha, hb, 0, head)
        value = load_keys(v0, ha, hb, 1, head)
        query = jnp.concatenate([head_rows(qa, head), head_rows(qb, head)], axis=0)
        grad = jnp.concatenate([head_rows(ga, head), head_rows(gb, head)], axis=0)
        expo, grad_probs, top, lse, delta = local_stats(query, grad, key, value, bias_ref[...])
        expo_out[head] = expo
        gp_out[head] = grad_probs
        own = own_part[head][0:2]
        near = jnp.concatenate([lse, delta, top], axis=0)
        part[head] = near
        part_a = near[0:2, :rows]
        part_b = near[0:2, rows:]
        a_out[head] = jnp.concatenate([own, part_a], axis=0)
        b_out[head] = jnp.concatenate([own, part_b], axis=0)
        c_out[head] = jnp.where(far_slot_a, part_a, part_b)
        d_out[head] = jnp.where(far_slot_a, part_b, part_a)


def merge(parts):
    top = parts[0][0]
    for lse, _ in parts[1:]:
        top = jnp.maximum(top, lse)
    weight_sum = jnp.zeros_like(top)
    delta_sum = jnp.zeros_like(top)
    for lse, delta in parts:
        weight = jnp.exp2(lse - top)
        weight_sum = weight_sum + weight
        delta_sum = delta_sum + weight * delta
    return jnp.maximum(top + jnp.log2(weight_sum), FLOOR), delta_sum / weight_sum


def halo_kernel(sizes, place_ref, q0, qa, qb, g0, ga, gb, e0, p0, en, pn, own_st, near_st, a_st, b_st, c_st, d_st, ra_out, rb_out, row_out):
    frame_count, strip_count, height, strip = sizes
    rows = height * strip
    half = height * TW
    frame, step_f, _, has_fa, has_fb, _, _ = position_facts(place_ref, frame_count, strip_count)
    beyond_a = frame + 2 * step_f
    beyond_b = frame - 2 * step_f
    has_ba = (beyond_a >= 0) & (beyond_a < frame_count)
    has_bb = (beyond_b >= 0) & (beyond_b < frame_count)
    far_slot_a = ((frame & 3) == 0) | ((frame & 3) == 3)

    def part(block, row, exists):
        lse = block[row : row + 1, :]
        return (lse if exists is None else jnp.where(exists, lse, NEG), block[row + 1 : row + 2, :])

    for head in range(own_st.shape[0]):
        own, near, from_a, from_b, from_c, from_d = (
            r[head] for r in (own_st, near_st, a_st, b_st, c_st, d_st)
        )
        near_a = near[:, :rows]
        near_b = near[:, rows:]
        far_a = jnp.where(far_slot_a, from_c, from_d)
        far_b = jnp.where(far_slot_a, from_d, from_c)
        merged = [
            merge([part(own, 0, None), part(from_a, 2, has_fa == 1), part(from_b, 2, has_fb == 1)]),
            merge([part(near_a, 0, None), part(from_a, 0, has_fa == 1), part(far_a, 0, has_ba)]),
            merge([part(near_b, 0, None), part(from_b, 0, has_fb == 1), part(far_b, 0, has_bb)]),
        ]
        lse = jnp.concatenate([m[0] for m in merged], axis=1)
        delta = jnp.concatenate([m[1] for m in merged], axis=1)
        top = jnp.concatenate([own[2:3], near_a[2:3], near_b[2:3]], axis=1)
        factor = jnp.exp2(top - lse)
        row_out[head] = jnp.concatenate([factor, delta], axis=0)
        key_part, value_part = head_grads(
            head, slice(rows, rows + 2 * half), factor, delta, q0, qa, qb, g0, ga, gb, e0, p0, en, pn
        )
        lanes = lanes_of(head)
        for out, lo in ((ra_out, 0), (rb_out, half)):
            out[0, :, lanes] = key_part[lo : lo + half].astype(jnp.bfloat16)
            out[1, :, lanes] = value_part[lo : lo + half].astype(jnp.bfloat16)


def head_grads(head, keys, factor, delta, q0, qa, qb, g0, ga, gb, e0, p0, en, pn):
    query = jnp.concatenate([head_rows(r, head) for r in (q0, qa, qb)], axis=0)
    grad = jnp.concatenate([head_rows(r, head) for r in (g0, ga, gb)], axis=0)
    expo = jnp.concatenate([e0[head, keys, :], en[head, keys, :]], axis=1)
    grad_probs = jnp.concatenate([p0[head, keys, :], pn[head, keys, :]], axis=1)
    probs = expo * factor
    grad_scores = (probs * (grad_probs - delta)).astype(jnp.bfloat16)
    value_part = jnp.dot(probs.astype(jnp.bfloat16), grad, preferred_element_type=jnp.float32)
    key_part = jnp.dot(grad_scores, query, preferred_element_type=jnp.float32) * SCALE
    return key_part, value_part


def main_kernel(sizes, row_st, q0, qa, qb, g0, ga, gb, e0, p0, en, pn, dk_out, dv_out):
    rows = sizes[2] * sizes[3]
    for head in range(row_st.shape[0]):
        row = row_st[head]
        key_part, value_part = head_grads(
            head, slice(0, rows), row[0:1], row[1:2], q0, qa, qb, g0, ga, gb, e0, p0, en, pn
        )
        dk_out[:, lanes_of(head)] = key_part
        dv_out[:, lanes_of(head)] = value_part


def finish_kernel(sizes, lanes, place_ref, dk, dv, ra, rb, dk_out, dv_out):
    _, _, height, strip = sizes
    even = (place_ref[1] & 1) == 0
    span = pl.ds(pl.multiple_of(pl.program_id(0) * lanes, lanes), lanes)
    for which, (part, out) in enumerate(((dk, dk_out), (dv, dv_out))):
        from_a = ra[which, :, span].astype(jnp.float32).reshape(height, TW, lanes)
        from_b = rb[which, :, span].astype(jnp.float32).reshape(height, TW, lanes)
        full = part[:, span].reshape(height, strip, lanes)
        left = full[:, :TW] + jnp.where(even, from_b, from_a)
        right = full[:, TW:] + jnp.where(even, from_a, from_b)
        out[0] = jnp.concatenate([left, right], axis=1).astype(jnp.bfloat16)


def vmem(value):
    return pltpu.with_memory_space_constraint(value, pltpu.VMEM)


def on_device(queries, keys, values, grad_out, window):
    _, height, strip, chans = queries.shape
    heads = chans // HD
    rows = height * strip
    half = height * TW
    ext = rows + 2 * half
    frame_count = lax.axis_size("frame")
    strip_count = lax.axis_size("tile")
    sizes = (frame_count, strip_count, height, strip)
    frame_even, frame_odd, far_c, far_d = pair_lists(frame_count)
    tile_even, tile_odd, _, _ = pair_lists(strip_count)
    frame_pos = lax.axis_index("frame")
    strip_pos = lax.axis_index("tile")
    place = jnp.stack([frame_pos, strip_pos]).astype(jnp.int32)

    qa = swap(queries, "frame", frame_even)
    qb = swap(queries, "frame", frame_odd)
    ga = swap(grad_out, "frame", frame_even)
    gb = swap(grad_out, "frame", frame_odd)

    even = (strip_pos & 1) == 0
    start_a = jnp.where(even, strip - TW, 0)
    start_b = jnp.where(even, 0, strip - TW)

    def edge(start):
        cut = [lax.dynamic_slice_in_dim(x[0], start, TW, axis=1).reshape(half, chans) for x in (keys, values)]
        return jnp.stack(cut)

    ha = swap(edge(start_a), "tile", tile_even)
    hb = swap(edge(start_b), "tile", tile_odd)

    smem = pl.BlockSpec(memory_space=pltpu.SMEM)
    whole = pl.BlockSpec(memory_space=pltpu.VMEM)

    def call(kernel, name, scalars, arrays, outs, scratch=()):
        return pl.pallas_call(
            lambda *refs: kernel(sizes, *refs),
            name=name,
            in_specs=[smem] * len(scalars) + [whole] * len(arrays),
            out_specs=[whole] * len(outs),
            out_shape=[pltpu.VMEM(shape, dtype) for shape, dtype in outs],
            scratch_shapes=list(scratch),
            compiler_params=pltpu.CompilerParams(vmem_limit_bytes=KERNEL_VMEM),
        )(*scalars, *[vmem(x) for x in arrays])

    f32 = jnp.float32
    part, e0, p0 = call(
        own_kernel,
        "own_stats",
        (window, place),
        (queries, grad_out, keys, values, ha, hb),
        [((heads, 3, rows), f32), ((heads, ext, rows), f32), ((heads, ext, rows), f32)],
        [pltpu.VMEM((ext, rows), f32)],
    )
    near, a_st, b_st, c_st, d_st, en, pn = call(
        near_kernel,
        "near_stats",
        (window, place),
        (qa, qb, ga, gb, keys, values, ha, hb, part),
        [((heads, 3, 2 * rows), f32)]
        + [((heads, n, rows), f32) for n in (4, 4, 2, 2)]
        + [((heads, ext, 2 * rows), f32)] * 2,
        [pltpu.VMEM((ext, 2 * rows), f32)],
    )
    a_st = swap(a_st, "frame", frame_even)
    b_st = swap(b_st, "frame", frame_odd)
    if far_c:
        c_st = swap(c_st, "frame", far_c)
    if far_d:
        d_st = swap(d_st, "frame", far_d)

    data = (queries, qa, qb, grad_out, ga, gb, e0, p0, en, pn)
    ra, rb, row = call(
        halo_kernel,
        "halo_grads",
        (place,),
        data + (part, near, a_st, b_st, c_st, d_st),
        [((2, half, chans), jnp.bfloat16)] * 2 + [((heads, 2, 3 * rows), f32)],
    )
    ra = swap(ra, "tile", tile_even)
    rb = swap(rb, "tile", tile_odd)
    dk, dv = call(main_kernel, "main_grads", (), (row,) + data, [((rows, chans), f32)] * 2)

    lanes = chans // FINISH_STEPS
    out_spec = pl.BlockSpec((1, height, strip, lanes), lambda i: (0, 0, 0, i))
    return pl.pallas_call(
        lambda *refs: finish_kernel(sizes, lanes, *refs),
        name="finish",
        grid=(FINISH_STEPS,),
        compiler_params=pltpu.CompilerParams(vmem_limit_bytes=KERNEL_VMEM),
        in_specs=[smem] + [whole] * 4,
        out_specs=[out_spec, out_spec],
        out_shape=[jax.ShapeDtypeStruct(keys.shape, jnp.bfloat16)] * 2,
    )(place, vmem(dk), vmem(dv), vmem(ra), vmem(rb))


def solution(mesh):
    spec = P(("clip", "frame"), None, "tile", None)
    return jax.shard_map(
        on_device,
        mesh=mesh,
        in_specs=(spec, spec, spec, spec, P()),
        out_specs=(spec, spec),
        check_vma=False,
    )
```

time: 60.8 us -> 51.4 us (0.85)
  Pallas kernels: 15.5 us -> 8.77 us
  local copies, waits for them, and re-layouts: 5.59 us -> 1.49 us
  waiting for transfers between devices: 14.7 us -> 18.6 us
  starting transfers between devices: 22.9 us -> 20.5 us
    pallas_call x3 -> x5, Pallas kernels: 15.5 us -> 8.77 us  [the longest x4 6.73 us: call(): pl.pallas_call(lambda *refs: kernel(sizes, *refs), name=name, in_specs=[s...]
    unnamed x25 -> x11, local copies, waits for them, and re-layouts: 4.33 us -> 0.12 us
    ppermute x11, waiting for transfers between devices: 14.7 us -> 18.6 us  [swap(): return lax.ppermute(value, axis, pairs)]
    ppermute x11, starting transfers between devices: 22.9 us -> 20.5 us  [swap(): return lax.ppermute(value, axis, pairs)]
    another operation x2, other arithmetic: 0.08 us -> 0.82 us  [edge(): return jnp.stack(cut)]
  transfers between devices with their start and end apart: 11 -> 11, of which waited for: 3 -> 4; matrix products, arithmetic and copies ran while one was open for 4% -> 2% of each run, Pallas kernels for 0% -> 5%
where the time goes in v2:
time: 51.4 us; the launch traced here: 51.1 us
  starting transfers between devices  20.5 us (40%)
  waiting for transfers between devices  18.6 us (36%)
  Pallas kernels  8.77 us (17%)
  local copies, waits for them, and re-layouts  1.49 us (3%)
  other arithmetic  0.9 us (2%)
  between operations  0.8 us (2%)
    ppermute x11, starting transfers between devices, swap(): return lax.ppermute(value, axis, pairs)  20.5 us
    ppermute x11, waiting for transfers between devices, swap(): return lax.ppermute(value, axis, pairs)  18.6 us
    pallas_call x4, Pallas kernels, call(): pl.pallas_call(lambda *refs: kernel(sizes, *refs), name=name, in_specs=[s...  6.73 us
    pallas_call x1, Pallas kernels, on_device(): pl.pallas_call(lambda *refs: finish_kernel(sizes, lanes, *refs), name='fi...  2.04 us
    another operation x1, local copies, waits for them, and re-layouts, edge(): return jnp.stack(cut)  1.37 us
  transfers between devices with their start and end apart: 11, of which 4 were waited for; matrix products, arithmetic and copies ran while one was open for 2% of the time, Pallas kernels for 5%

profile of v2, /device:TPU:1, one launch (start us, length us, event | category | flops | bytes accessed | tf_op | source)
XLA Modules:
  0.0 51.1 jit_solution(886565361343546174)
XLA Ops:
  0.7 0.0 copy-start
  0.7 1.4 %dynamic-slice_bitcast_fusion = (bf16[1,64,1536]{2,1,0:T(8,128)(2,1)S(1)}, bf16[1,64,1536]{2,1,0:T(8,128)(2,1)S(1)}, bf16[1,64,1536]{2,1,0:T(8,128)(2,1)S(1)}, bf16[1,64,1536]{2,1,0:T(8,128)(2,1)S(1)}) fusion(bf16[1,8,16,1536]{3,2,1,0:T(8,128)(2,1)} %refs_7_.1, s32[]{:T(128)S(6)} %select_n.12, s32[]{:T(128)S(6)} %select_n.11, bf16[1,8,16,1536]{3,2,1,0:T(8,128)(2,1)} %refs_6_.1), kind=kLoop, calls=%fused_computation.2 | loop fusion | bytes 1572872 | tf_op jit(solution)/shard_map/stack;reshape | solution.py:277
  2.1 0.1 collective-permute-start.4
  2.2 0.7 %collective-permute-start.1 = (bf16[1,8,16,1536]{3,2,1,0:T(8,128)(2,1)}, bf16[1,8,16,1536]{3,2,1,0:T(8,128)(2,1)S(1)}, u32[]{:S(2)}, u32[]{:S(2)}) collective-permute-start(bf16[1,8,16,1536]{3,2,1,0:T(8,128)(2,1)} %refs_1_.3), channel_id=1, source_target_pairs={{4,8},{8,4},{5,9},{9,5},{6,10},{10,6},{7,11},{11,7},{20,24},{24,20... | collective-permute-start | bytes 1179656 | tf_op jit(solution)/shard_map/ppermute | solution.py:30
  2.9 0.8 %pad_maximum_fusion.1 = bf16[2,64,1536]{2,1,0:T(8,128)(2,1)} fusion(bf16[1,64,1536]{2,1,0:T(8,128)(2,1)S(1)} %get-tuple-element.34, bf16[1,64,1536]{2,1,0:T(8,128)(2,1)S(1)} %get-tuple-element.37), kind=kLoop, calls=%fused_computation.1 | loop fusion | flops 196608 | bytes 786432 | tf_op jit(solution)/shard_map/stack | solution.py:277
  3.7 4.5 %collective-permute-start.5 = (bf16[2,64,1536]{2,1,0:T(8,128)(2,1)}, bf16[2,64,1536]{2,1,0:T(8,128)(2,1)}, u32[]{:S(2)}, u32[]{:S(2)}) collective-permute-start(bf16[2,64,1536]{2,1,0:T(8,128)(2,1)} %pad_maximum_fusion.1), channel_id=1, source_target_pairs={{1,2},{2,1},{5,6},{6,5},{9,10},{10,9},{13,14},{14,13},{17,18},{18,... | collective-permute-start | bytes 1179656 | tf_op jit(solution)/shard_map/ppermute | solution.py:30
  8.2 4.2 %collective-permute-start = (bf16[1,8,16,1536]{3,2,1,0:T(8,128)(2,1)S(1)}, bf16[1,8,16,1536]{3,2,1,0:T(8,128)(2,1)S(1)}, u32[]{:S(2)}, u32[]{:S(2)}) collective-permute-start(bf16[1,8,16,1536]{3,2,1,0:T(8,128)(2,1)S(1)} %copy-done), channel_id=1, source_target_pairs={{0,4},{8,12},{4,0},{12,8},{1,5},{9,13},{5,1},{13,9},{2,6},{10,14},... | collective-permute-start | bytes 1179656 | tf_op jit(solution)/shard_map/ppermute | solution.py:30
  12.4 0.7 %collective-permute-start.3 = (bf16[1,8,16,1536]{3,2,1,0:T(8,128)(2,1)S(1)}, bf16[1,8,16,1536]{3,2,1,0:T(8,128)(2,1)S(1)}, u32[]{:S(2)}, u32[]{:S(2)}) collective-permute-start(bf16[1,8,16,1536]{3,2,1,0:T(8,128)(2,1)S(1)} %copy-done.1), channel_id=1, source_target_pairs={{4,8},{8,4},{5,9},{9,5},{6,10},{10,6},{7,11},{11,7},{20,24},{24,20... | collective-permute-start | bytes 1179656 | tf_op jit(solution)/shard_map/ppermute | solution.py:30
  13.1 0.0 collective-permute-done.4.refs_6_.refs_8_
  13.1 1.5 %collective-permute-start.2 = (bf16[1,8,16,1536]{3,2,1,0:T(8,128)(2,1)S(1)}, bf16[1,8,16,1536]{3,2,1,0:T(8,128)(2,1)S(1)}, u32[]{:S(2)}, u32[]{:S(2)}) collective-permute-start(bf16[1,8,16,1536]{3,2,1,0:T(8,128)(2,1)S(1)} %copy-done.1), channel_id=1, source_target_pairs={{0,4},{8,12},{4,0},{12,8},{1,5},{9,13},{5,1},{13,9},{2,6},{10,14},... | collective-permute-start | bytes 1179656 | tf_op jit(solution)/shard_map/ppermute | solution.py:30
  14.6 0.1 copy.7.refs_0_
  14.7 0.1 pad_add_fusion.refs_1_.refs_0_
  14.7 0.0 collective-permute-done.5.refs_7_.refs_9_
  14.7 1.8 %own_stats.1 = (f32[12,3,128]{2,1,0:T(4,128)S(1)}, f32[12,256,128]{2,1,0:T(8,128)S(1)}, f32[12,256,128]{2,1,0:T(8,128)S(1)}) custom-call(s32[18,3]{1,0:T(8,128)S(1)} %copy.7.refs_0_, s32[2]{0:T(128)S(1)} %pad_add_fusion.refs_1_.refs_0_, bf16[1,8,16,1536]{3,2,1,0:T(8,128)(2,1)S(1)} %copy-done, bf16[1,8,16,1536]{3,2,1,0:T(8,128)(2,1)S(1)} %copy-done.1, ...), custom_call_target="tpu_custom_call" | custom-call | tf_op jit(solution)/shard_map/own_stats/pallas_call | solution.py:286
  16.5 0.0 collective-permute-done.1.refs_3_
  16.5 5.5 %collective-permute-done.refs_2_ = bf16[1,8,16,1536]{3,2,1,0:T(8,128)(2,1)S(1)} collective-permute-done((bf16[1,8,16,1536]{3,2,1,0:T(8,128)(2,1)S(1)}, bf16[1,8,16,1536]{3,2,1,0:T(8,128)(2,1)S(1)}, u32[]{:S(2)}, u32[]{:S(2)}) %collective-permute-start) | collective-permute-done | bytes 393248 | tf_op jit(solution)/shard_map/ppermute | solution.py:30
  22.0 0.0 collective-permute-done.3.refs_5_.refs_6_
  22.0 6.6 %collective-permute-done.2.refs_4_.refs_5_ = bf16[1,8,16,1536]{3,2,1,0:T(8,128)(2,1)S(1)} collective-permute-done((bf16[1,8,16,1536]{3,2,1,0:T(8,128)(2,1)S(1)}, bf16[1,8,16,1536]{3,2,1,0:T(8,128)(2,1)S(1)}, u32[]{:S(2)}, u32[]{:S(2)}) %collective-permute-start.2) | collective-permute-done | bytes 393248 | tf_op jit(solution)/shard_map/ppermute | solution.py:30
  28.7 2.4 %near_stats.1 = (f32[12,3,256]{2,1,0:T(4,128)S(1)}, f32[12,4,128]{2,1,0:T(4,128)S(1)}, f32[12,4,128]{2,1,0:T(4,128)S(1)}, f32[12,2,128]{2,1,0:T(2,128)S(1)}, f32...) custom-call(s32[18,3]{1,0:T(8,128)S(1)} %copy.7.refs_0_, ...), custom_call_target="tpu_custom_call" | custom-call | tf_op jit(solution)/shard_map/near_stats/pallas_call | solution.py:286
  31.1 1.8 %collective-permute-start.6 = (f32[12,4,128]{2,1,0:T(4,128)S(1)}, f32[12,4,128]{2,1,0:T(4,128)S(1)}, u32[]{:S(2)}, u32[]{:S(2)}) collective-permute-start(f32[12,4,128]{2,1,0:T(4,128)S(1)} %get-tuple-element.23), channel_id=1, source_target_pairs={{0,4},{8,12},{4,0},{12,8},{1,5},{9,13},{5,1},{13,9},{2,6},{10,14},... | collective-permute-start | bytes 73736 | tf_op jit(solution)/shard_map/ppermute | solution.py:30
  32.9 0.7 %collective-permute-start.7 = (f32[12,4,128]{2,1,0:T(4,128)S(1)}, f32[12,4,128]{2,1,0:T(4,128)S(1)}, u32[]{:S(2)}, u32[]{:S(2)}) collective-permute-start(f32[12,4,128]{2,1,0:T(4,128)S(1)} %get-tuple-element.24), channel_id=1, source_target_pairs={{4,8},{8,4},{5,9},{9,5},{6,10},{10,6},{7,11},{11,7},{20,24},{24,20... | collective-permute-start | bytes 73736 | tf_op jit(solution)/shard_map/ppermute | solution.py:30
  33.5 2.5 %collective-permute-start.8 = (f32[12,2,128]{2,1,0:T(2,128)S(1)}, f32[12,2,128]{2,1,0:T(2,128)S(1)}, u32[]{:S(2)}, u32[]{:S(2)}) collective-permute-start(f32[12,2,128]{2,1,0:T(2,128)S(1)} %get-tuple-element.25), channel_id=1, source_target_pairs={{0,8},{4,12},{8,0},{12,4},{1,9},{5,13},{9,1},{13,5},{2,10},{6,14},... | collective-permute-start | bytes 36872 | tf_op jit(solution)/shard_map/ppermute | solution.py:30
  36.1 1.8 %collective-permute-done.8.refs_15_ = f32[12,2,128]{2,1,0:T(2,128)S(1)} collective-permute-done((f32[12,2,128]{2,1,0:T(2,128)S(1)}, f32[12,2,128]{2,1,0:T(2,128)S(1)}, u32[]{:S(2)}, u32[]{:S(2)}) %collective-permute-start.8) | collective-permute-done | bytes 12320 | tf_op jit(solution)/shard_map/ppermute | solution.py:30
  37.8 0.0 collective-permute-done.6.refs_13_
  37.8 0.0 collective-permute-done.7.refs_14_
  37.8 1.7 %halo_grads.1 = (bf16[2,64,1536]{2,1,0:T(8,128)(2,1)S(1)}, bf16[2,64,1536]{2,1,0:T(8,128)(2,1)S(1)}, f32[12,2,384]{2,1,0:T(2,128)S(1)}) custom-call(s32[2]{0:T(128)S(1)} %pad_add_fusion.refs_1_.refs_0_, bf16[1,8,16,1536]{3,2,1,0:T(8,128)(2,1)S(1)} %copy-done, bf16[1,8,16,1536]{3,2,1,0:T(8,128)(2,1)S(1)} %collective-permute-done.refs_2_, ...), custom_call_target="tpu_custom_call" | custom-call | tf_op jit(solution)/shard_map/halo_grads/pallas_call | solution.py:286
  39.5 0.5 collective-permute-start.9
  40.0 3.5 %collective-permute-start.10 = (bf16[2,64,1536]{2,1,0:T(8,128)(2,1)S(1)}, bf16[2,64,1536]{2,1,0:T(8,128)(2,1)S(1)}, u32[]{:S(2)}, u32[]{:S(2)}) collective-permute-start(bf16[2,64,1536]{2,1,0:T(8,128)(2,1)S(1)} %get-tuple-element.31), channel_id=1, source_target_pairs={{1,2},{2,1},{5,6},{6,5},{9,10},{10,9},{13,14},{14,13},{17,18},{18,... | collective-permute-start | bytes 1179656 | tf_op jit(solution)/shard_map/ppermute | solution.py:30
  43.4 0.9 %main_grads.1 = (f32[128,1536]{1,0:T(8,128)S(1)}, f32[128,1536]{1,0:T(8,128)S(1)}) custom-call(f32[12,2,384]{2,1,0:T(2,128)S(1)} %get-tuple-element.27.refs_0_, bf16[1,8,16,1536]{3,2,1,0:T(8,128)(2,1)S(1)} %copy-done, bf16[1,8,16,1536]{3,2,1,0:T(8,128)(2,1)S(1)} %collective-permute-done.refs_2_, bf16[1,8,16,1536]{3,2,1,0:T(8,128)(2,1)S(1)} %collective-permute-done.1.refs_3_, ...), custom_call_target="tpu_custom_call" | custom-call | tf_op jit(solution)/shard_map/main_grads/pallas_call | solution.py:286
  44.4 0.0 collective-permute-done.9.refs_3_
  44.4 4.7 %collective-permute-done.10.refs_4_ = bf16[2,64,1536]{2,1,0:T(8,128)(2,1)S(1)} collective-permute-done((bf16[2,64,1536]{2,1,0:T(8,128)(2,1)S(1)}, bf16[2,64,1536]{2,1,0:T(8,128)(2,1)S(1)}, u32[]{:S(2)}, u32[]{:S(2)}) %collective-permute-start.10) | collective-permute-done | bytes 393248 | tf_op jit(solution)/shard_map/ppermute | solution.py:30
  49.0 2.0 %finish.1 = (bf16[1,8,16,1536]{3,2,1,0:T(8,128)(2,1)}, bf16[1,8,16,1536]{3,2,1,0:T(8,128)(2,1)}) custom-call(s32[2]{0:T(128)S(1)} %pad_add_fusion.refs_1_.refs_0_, f32[128,1536]{1,0:T(8,128)S(1)} %get-tuple-element.28.refs_1_, f32[128,1536]{1,0:T(8,128)S(1)} %get-tuple-element.29.refs_2_, bf16[2,64,1536]{2,1,0:T(8,128)(2,1)S(1)} %collective-permute-done.9.refs_3_, ...), custom_call_target="tpu_custom_call" | custom-call | tf_op jit(solution)/shard_map/finish/pallas_call | solution.py:336
  (10 shorter events, 0.1 us)
Async XLA Ops:
  0.6 14.1 %copy-start.3 = (bf16[1,8,16,1536]{3,2,1,0:T(8,128)(2,1)S(1)}, bf16[1,8,16,1536]{3,2,1,0:T(8,128)(2,1)}, u32[]{:S(2)}) copy-start(bf16[1,8,16,1536]{3,2,1,0:T(8,128)(2,1)} %refs_7_.1) | copy-start | bytes 1179652
  0.6 14.1 %copy-start.2 = (bf16[1,8,16,1536]{3,2,1,0:T(8,128)(2,1)S(1)}, bf16[1,8,16,1536]{3,2,1,0:T(8,128)(2,1)}, u32[]{:S(2)}) copy-start(bf16[1,8,16,1536]{3,2,1,0:T(8,128)(2,1)} %refs_6_.1) | copy-start | bytes 1179652
  0.7 7.5 %copy-start = (bf16[1,8,16,1536]{3,2,1,0:T(8,128)(2,1)S(1)}, bf16[1,8,16,1536]{3,2,1,0:T(8,128)(2,1)}, u32[]{:S(2)}) copy-start(bf16[1,8,16,1536]{3,2,1,0:T(8,128)(2,1)} %refs_1_.3) | copy-start | bytes 1179652
  0.7 11.7 %copy-start.1 = (bf16[1,8,16,1536]{3,2,1,0:T(8,128)(2,1)S(1)}, bf16[1,8,16,1536]{3,2,1,0:T(8,128)(2,1)}, u32[]{:S(2)}) copy-start(bf16[1,8,16,1536]{3,2,1,0:T(8,128)(2,1)} %refs_4_.5) | copy-start | bytes 1179652
  0.7 13.9 %copy-start.4 = (s32[18,3]{0,1:T(4,128)S(1)}, s32[18,3]{0,1:T(4,128)}, u32[]{:S(2)}) copy-start(s32[18,3]{0,1:T(4,128)} %param.9) | copy-start | bytes 652
  2.1 10.9 %collective-permute-start.4 = (bf16[2,64,1536]{2,1,0:T(8,128)(2,1)S(1)}, bf16[2,64,1536]{2,1,0:T(8,128)(2,1)S(1)}, u32[]{:S(2)}, u32[]{:S(2)}) collective-permute-start(bf16[2,64,1536]{2,1,0:T(8,128)(2,1)S(1)} %pad_maximum_fusion), channel_id=1, source_target_pairs={{0,1},{2,3},{1,0},{3,2},{4,5},{6,7},{5,4},{7,6},{8,9},{10,11},{9,8... | collective-permute-start | bytes 1179656 | tf_op jit(solution)/shard_map/ppermute | solution.py:30
  2.2 14.3 %collective-permute-start.1 = (bf16[1,8,16,1536]{3,2,1,0:T(8,128)(2,1)}, bf16[1,8,16,1536]{3,2,1,0:T(8,128)(2,1)S(1)}, u32[]{:S(2)}, u32[]{:S(2)}) collective-permute-start(bf16[1,8,16,1536]{3,2,1,0:T(8,128)(2,1)} %refs_1_.3), channel_id=1, source_target_pairs={{4,8},{8,4},{5,9},{9,5},{6,10},{10,6},{7,11},{11,7},{20,24},{24,20... | collective-permute-start | bytes 1179656 | tf_op jit(solution)/shard_map/ppermute | solution.py:30
  3.7 11.1 %collective-permute-start.5 = (bf16[2,64,1536]{2,1,0:T(8,128)(2,1)}, bf16[2,64,1536]{2,1,0:T(8,128)(2,1)}, u32[]{:S(2)}, u32[]{:S(2)}) collective-permute-start(bf16[2,64,1536]{2,1,0:T(8,128)(2,1)} %pad_maximum_fusion.1), channel_id=1, source_target_pairs={{1,2},{2,1},{5,6},{6,5},{9,10},{10,9},{13,14},{14,13},{17,18},{18,... | collective-permute-start | bytes 1179656 | tf_op jit(solution)/shard_map/ppermute | solution.py:30
  8.2 13.8 %collective-permute-start = (bf16[1,8,16,1536]{3,2,1,0:T(8,128)(2,1)S(1)}, bf16[1,8,16,1536]{3,2,1,0:T(8,128)(2,1)S(1)}, u32[]{:S(2)}, u32[]{:S(2)}) collective-permute-start(bf16[1,8,16,1536]{3,2,1,0:T(8,128)(2,1)S(1)} %copy-done), channel_id=1, source_target_pairs={{0,4},{8,12},{4,0},{12,8},{1,5},{9,13},{5,1},{13,9},{2,6},{10,14},... | collective-permute-start | bytes 1179656 | tf_op jit(solution)/shard_map/ppermute | solution.py:30
  12.4 9.7 %collective-permute-start.3 = (bf16[1,8,16,1536]{3,2,1,0:T(8,128)(2,1)S(1)}, bf16[1,8,16,1536]{3,2,1,0:T(8,128)(2,1)S(1)}, u32[]{:S(2)}, u32[]{:S(2)}) collective-permute-start(bf16[1,8,16,1536]{3,2,1,0:T(8,128)(2,1)S(1)} %copy-done.1), channel_id=1, source_target_pairs={{4,8},{8,4},{5,9},{9,5},{6,10},{10,6},{7,11},{11,7},{20,24},{24,20... | collective-permute-start | bytes 1179656 | tf_op jit(solution)/shard_map/ppermute | solution.py:30
  13.1 15.6 %collective-permute-start.2 = (bf16[1,8,16,1536]{3,2,1,0:T(8,128)(2,1)S(1)}, bf16[1,8,16,1536]{3,2,1,0:T(8,128)(2,1)S(1)}, u32[]{:S(2)}, u32[]{:S(2)}) collective-permute-start(bf16[1,8,16,1536]{3,2,1,0:T(8,128)(2,1)S(1)} %copy-done.1), channel_id=1, source_target_pairs={{0,4},{8,12},{4,0},{12,8},{1,5},{9,13},{5,1},{13,9},{2,6},{10,14},... | collective-permute-start | bytes 1179656 | tf_op jit(solution)/shard_map/ppermute | solution.py:30
  31.1 6.8 %collective-permute-start.6 = (f32[12,4,128]{2,1,0:T(4,128)S(1)}, f32[12,4,128]{2,1,0:T(4,128)S(1)}, u32[]{:S(2)}, u32[]{:S(2)}) collective-permute-start(f32[12,4,128]{2,1,0:T(4,128)S(1)} %get-tuple-element.23), channel_id=1, source_target_pairs={{0,4},{8,12},{4,0},{12,8},{1,5},{9,13},{5,1},{13,9},{2,6},{10,14},... | collective-permute-start | bytes 73736 | tf_op jit(solution)/shard_map/ppermute | solution.py:30
  32.9 4.9 %collective-permute-start.7 = (f32[12,4,128]{2,1,0:T(4,128)S(1)}, f32[12,4,128]{2,1,0:T(4,128)S(1)}, u32[]{:S(2)}, u32[]{:S(2)}) collective-permute-start(f32[12,4,128]{2,1,0:T(4,128)S(1)} %get-tuple-element.24), channel_id=1, source_target_pairs={{4,8},{8,4},{5,9},{9,5},{6,10},{10,6},{7,11},{11,7},{20,24},{24,20... | collective-permute-start | bytes 73736 | tf_op jit(solution)/shard_map/ppermute | solution.py:30
  33.5 4.3 %collective-permute-start.8 = (f32[12,2,128]{2,1,0:T(2,128)S(1)}, f32[12,2,128]{2,1,0:T(2,128)S(1)}, u32[]{:S(2)}, u32[]{:S(2)}) collective-permute-start(f32[12,2,128]{2,1,0:T(2,128)S(1)} %get-tuple-element.25), channel_id=1, source_target_pairs={{0,8},{4,12},{8,0},{12,4},{1,9},{5,13},{9,1},{13,5},{2,10},{6,14},... | collective-permute-start | bytes 36872 | tf_op jit(solution)/shard_map/ppermute | solution.py:30
  39.5 4.9 %collective-permute-start.9 = (bf16[2,64,1536]{2,1,0:T(8,128)(2,1)S(1)}, bf16[2,64,1536]{2,1,0:T(8,128)(2,1)S(1)}, u32[]{:S(2)}, u32[]{:S(2)}) collective-permute-start(bf16[2,64,1536]{2,1,0:T(8,128)(2,1)S(1)} %get-tuple-element.30), channel_id=1, source_target_pairs={{0,1},{2,3},{1,0},{3,2},{4,5},{6,7},{5,4},{7,6},{8,9},{10,11},{9,8... | collective-permute-start | bytes 1179656 | tf_op jit(solution)/shard_map/ppermute | solution.py:30
  40.0 9.1 %collective-permute-start.10 = (bf16[2,64,1536]{2,1,0:T(8,128)(2,1)S(1)}, bf16[2,64,1536]{2,1,0:T(8,128)(2,1)S(1)}, u32[]{:S(2)}, u32[]{:S(2)}) collective-permute-start(bf16[2,64,1536]{2,1,0:T(8,128)(2,1)S(1)} %get-tuple-element.31), channel_id=1, source_target_pairs={{1,2},{2,1},{5,6},{6,5},{9,10},{10,9},{13,14},{14,13},{17,18},{18,... | collective-permute-start | bytes 1179656 | tf_op jit(solution)/shard_map/ppermute | solution.py:30

commit v3 on v2

v3 whole, which is shorter than its diff:
```python
import math

import jax
import jax.numpy as jnp
from jax import lax
from jax.experimental import pallas as pl
from jax.experimental.pallas import tpu as pltpu
from jax.sharding import PartitionSpec as P

HD = 128
TH = 4
TW = 8
FINISH_STEPS = 4
FLOPS = 1_500_000_000
KERNEL_VMEM = 16 << 20
NEG = -1e30
FLOOR = -1e29
SCALE = HD ** (-0.5)
SCALE2 = SCALE * math.log2(math.e)


def pair_lists(count):
    even = [(i, i + 1) for i in range(0, count - 1, 2)]
    odd = [(i, i + 1) for i in range(1, count - 1, 2)]
    far_a = [(i, i + 2) for i in range(count - 2) if i % 4 in (0, 1)]
    far_b = [(i, i + 2) for i in range(count - 2) if i % 4 in (2, 3)]
    return [pairs + [(j, i) for i, j in pairs] for pairs in (even, odd, far_a, far_b)]


def swap(value, axis, pairs):
    return lax.ppermute(value, axis, pairs)


def bit_table(window_ref):
    bits = jnp.int32(0)
    for i in range(window_ref.shape[0]):
        code = (window_ref[i, 0] + 1) * 9 + (window_ref[i, 1] + 1) * 3 + (window_ref[i, 2] + 1)
        bits = bits | jnp.left_shift(jnp.int32(1), code)
    return bits


def position_facts(place_ref, frame_count, strip_count):
    frame = place_ref[0]
    strip = place_ref[1]
    step_f = 1 - 2 * (frame & 1)
    step_s = 1 - 2 * (strip & 1)
    return (
        frame,
        step_f,
        step_s,
        ((frame + step_f >= 0) & (frame + step_f < frame_count)).astype(jnp.int32),
        ((frame - step_f >= 0) & (frame - step_f < frame_count)).astype(jnp.int32),
        ((strip + step_s >= 0) & (strip + step_s < strip_count)).astype(jnp.int32),
        ((strip - step_s >= 0) & (strip - step_s < strip_count)).astype(jnp.int32),
    )


def fill_bias(bias_ref, slots, window_ref, place_ref, frame_count, strip_count, height, strip):
    bits = bit_table(window_ref)
    _, step_f, step_s, has_fa, has_fb, has_sa, has_sb = position_facts(
        place_ref, frame_count, strip_count
    )
    rows = height * strip
    half = height * TW
    tiles = strip // TW
    col_a = jnp.where(step_s > 0, tiles, -1)
    col_b = jnp.where(step_s > 0, -1, tiles)
    frames = ((0, 1), (-step_f, has_fa), (step_f, has_fb))
    for place, slot in enumerate(slots):
        off_time, has_f = frames[slot]
        start = 0
        for length, wide, k_col, has_s in (
            (rows, strip, None, 1),
            (half, TW, col_a, has_sa),
            (half, TW, col_b, has_sb),
        ):
            key_idx = lax.broadcasted_iota(jnp.int32, (length, rows), 0)
            query_idx = lax.broadcasted_iota(jnp.int32, (length, rows), 1)
            off_high = key_idx // (wide * TH) - query_idx // (strip * TH)
            k_wide = (key_idx % wide) // TW if k_col is None else k_col
            off_wide = k_wide - (query_idx % strip) // TW
            near = (jnp.abs(off_wide) <= 1) & (jnp.abs(off_high) <= 1)
            code = (off_time + 1) * 9 + (off_high + 1) * 3 + (off_wide + 1)
            listed = jnp.right_shift(bits, jnp.where(near, code, 0)) & 1
            flag = jnp.where(near, listed, 0) * (has_f * has_s)
            bias_ref[start : start + length, place * rows : (place + 1) * rows] = jnp.where(
                flag == 1, jnp.float32(0), jnp.float32(NEG)
            )
            start += length


def lanes_of(head):
    return slice(head * HD, (head + 1) * HD)


def head_rows(ref, head):
    return ref[0, :, :, lanes_of(head)].reshape(-1, HD)


def load_keys(own_ref, a_ref, b_ref, which, head):
    lanes = lanes_of(head)
    return jnp.concatenate(
        [head_rows(own_ref, head), a_ref[which, :, lanes], b_ref[which, :, lanes]], axis=0
    )


def dot_nt(a, b):
    return lax.dot_general(a, b, (((1,), (1,)), ((), ())), preferred_element_type=jnp.float32)


def edges_kernel(sizes, place_ref, k0, v0, a_out, b_out):
    _, _, height, strip = sizes
    even = (place_ref[1] & 1) == 0
    for which, ref in enumerate((k0, v0)):
        left = ref[0, :, :TW, :].reshape(height * TW, -1)
        right = ref[0, :, strip - TW :, :].reshape(height * TW, -1)
        a_out[which] = jnp.where(even, right, left)
        b_out[which] = jnp.where(even, left, right)


def scores_kernel(sizes, window_ref, place_ref, q0, qa, qb, g0, k0, v0, ha, hb, expo_out, gp_out, st_out, delta_out, bias_ref):
    rows = sizes[2] * sizes[3]
    fill_bias(bias_ref, (0, 1, 2), window_ref, place_ref, *sizes)
    for head in range(st_out.shape[0]):
        key = load_keys(k0, ha, hb, 0, head)
        value = load_keys(v0, ha, hb, 1, head)
        query = jnp.concatenate([head_rows(r, head) for r in (q0, qa, qb)], axis=0)
        scores = dot_nt(key, query) * SCALE2 + bias_ref[...]
        grad_probs = dot_nt(value, head_rows(g0, head))
        top = jnp.max(scores, axis=0, keepdims=True)
        expo = jnp.exp2(scores - top)
        total = jnp.sum(expo, axis=0, keepdims=True)
        inverse = 1.0 / total
        expo_out[head] = expo
        gp_out[head] = grad_probs
        st_out[head] = jnp.concatenate([top + jnp.log2(total), top, inverse], axis=0)
        delta_out[head] = jnp.sum(expo[:, :rows] * grad_probs, axis=0, keepdims=True) * inverse[:, :rows]


def deltas_kernel(sizes, place_ref, ga, gb, v0, ha, hb, expo, st, own_delta, gp_out, delta_out, a_out, b_out, c_out, d_out):
    rows = sizes[2] * sizes[3]
    far_slot_a = ((place_ref[0] & 3) == 0) | ((place_ref[0] & 3) == 3)
    for head in range(st.shape[0]):
        value = load_keys(v0, ha, hb, 1, head)
        grad = jnp.concatenate([head_rows(ga, head), head_rows(gb, head)], axis=0)
        grad_probs = dot_nt(value, grad)
        gp_out[head] = grad_probs
        stat = st[head]
        near = jnp.sum(expo[head, :, rows:] * grad_probs, axis=0, keepdims=True) * stat[2:3, rows:]
        delta = jnp.concatenate([own_delta[head], near], axis=1)
        delta_out[head] = delta
        own, part_a, part_b = (
            jnp.concatenate([x[:, i * rows : (i + 1) * rows] for x in (stat[0:1], delta)], axis=0)
            for i in range(3)
        )
        a_out[head] = jnp.concatenate([own, part_a], axis=0)
        b_out[head] = jnp.concatenate([own, part_b], axis=0)
        c_out[head] = jnp.where(far_slot_a, part_a, part_b)
        d_out[head] = jnp.where(far_slot_a, part_b, part_a)


def merge(parts):
    top = parts[0][0]
    for lse, _ in parts[1:]:
        top = jnp.maximum(top, lse)
    weight_sum = jnp.zeros_like(top)
    delta_sum = jnp.zeros_like(top)
    for lse, delta in parts:
        weight = jnp.exp2(lse - top)
        weight_sum = weight_sum + weight
        delta_sum = delta_sum + weight * delta
    return jnp.maximum(top + jnp.log2(weight_sum), FLOOR), delta_sum / weight_sum


def halo_kernel(sizes, place_ref, q0, qa, qb, g0, ga, gb, expo, p0, pn, st, local_delta, a_st, b_st, c_st, d_st, rb_out, ra_out, row_out):
    frame_count, strip_count, height, strip = sizes
    rows = height * strip
    half = height * TW
    frame, step_f, _, has_fa, has_fb, _, _ = position_facts(place_ref, frame_count, strip_count)
    beyond_a = frame + 2 * step_f
    beyond_b = frame - 2 * step_f
    has_ba = (beyond_a >= 0) & (beyond_a < frame_count)
    has_bb = (beyond_b >= 0) & (beyond_b < frame_count)
    far_slot_a = ((frame & 3) == 0) | ((frame & 3) == 3)

    def part(block, row, exists):
        return (jnp.where(exists, block[row : row + 1, :], NEG), block[row + 1 : row + 2, :])

    for head in range(st.shape[0]):
        stat, local, from_a, from_b, from_c, from_d = (
            r[head] for r in (st, local_delta, a_st, b_st, c_st, d_st)
        )
        own, near_a, near_b = (
            (stat[0:1, i * rows : (i + 1) * rows], local[:, i * rows : (i + 1) * rows]) for i in range(3)
        )
        far_a = jnp.where(far_slot_a, from_c, from_d)
        far_b = jnp.where(far_slot_a, from_d, from_c)
        merged = [
            merge([own, part(from_a, 2, has_fa == 1), part(from_b, 2, has_fb == 1)]),
            merge([near_a, part(from_a, 0, has_fa == 1), part(far_a, 0, has_ba)]),
            merge([near_b, part(from_b, 0, has_fb == 1), part(far_b, 0, has_bb)]),
        ]
        lse = jnp.concatenate([m[0] for m in merged], axis=1)
        delta = jnp.concatenate([m[1] for m in merged], axis=1)
        row = jnp.concatenate([jnp.exp2(stat[1:2] - lse), delta], axis=0)
        row_out[head] = row
        key_part, value_part = head_grads(
            head, slice(rows, rows + 2 * half), row, q0, qa, qb, g0, ga, gb, expo, p0, pn
        )
        lanes = lanes_of(head)
        for out, lo in ((ra_out, 0), (rb_out, half)):
            out[0, :, lanes] = key_part[lo : lo + half].astype(jnp.bfloat16)
            out[1, :, lanes] = value_part[lo : lo + half].astype(jnp.bfloat16)


def head_grads(head, keys, row, q0, qa, qb, g0, ga, gb, expo_ref, p0, pn):
    query = jnp.concatenate([head_rows(r, head) for r in (q0, qa, qb)], axis=0)
    grad = jnp.concatenate([head_rows(r, head) for r in (g0, ga, gb)], axis=0)
    expo = expo_ref[head, keys, :]
    grad_probs = jnp.concatenate([p0[head, keys, :], pn[head, keys, :]], axis=1)
    factor = row[0:1]
    probs = expo * factor
    grad_scores = (expo * (factor * SCALE) * (grad_probs - row[1:2])).astype(jnp.bfloat16)
    value_part = jnp.dot(probs.astype(jnp.bfloat16), grad, preferred_element_type=jnp.float32)
    key_part = jnp.dot(grad_scores, query, preferred_element_type=jnp.float32)
    return key_part, value_part


def main_kernel(sizes, row_st, q0, qa, qb, g0, ga, gb, expo, p0, pn, dk_out, dv_out):
    rows = sizes[2] * sizes[3]
    for head in range(row_st.shape[0]):
        key_part, value_part = head_grads(
            head, slice(0, rows), row_st[head], q0, qa, qb, g0, ga, gb, expo, p0, pn
        )
        lanes = lanes_of(head)
        dk_out[:, lanes] = key_part
        dv_out[:, lanes] = value_part


def finish_kernel(sizes, step_rows, place_ref, rb, ra, dk, dv, dk_out, dv_out):
    _, _, height, strip = sizes
    even = (place_ref[1] & 1) == 0
    step = pl.program_id(0)
    edge = pl.ds(pl.multiple_of(step * step_rows * TW, step_rows * TW), step_rows * TW)
    span = pl.ds(pl.multiple_of(step * step_rows * strip, step_rows * strip), step_rows * strip)
    for which, (part, out) in enumerate(((dk, dk_out), (dv, dv_out))):
        from_a = ra[which, edge, :].astype(jnp.float32).reshape(step_rows, TW, -1)
        from_b = rb[which, edge, :].astype(jnp.float32).reshape(step_rows, TW, -1)
        full = part[span, :].reshape(step_rows, strip, -1)
        left = full[:, :TW] + jnp.where(even, from_b, from_a)
        right = full[:, TW:] + jnp.where(even, from_a, from_b)
        out[0] = jnp.concatenate([left, right], axis=1).astype(jnp.bfloat16)


def vmem(value):
    return pltpu.with_memory_space_constraint(value, pltpu.VMEM)


def on_device(queries, keys, values, grad_out, window):
    _, height, strip, chans = queries.shape
    heads = chans // HD
    rows = height * strip
    half = height * TW
    ext = rows + 2 * half
    frame_count = lax.axis_size("frame")
    strip_count = lax.axis_size("tile")
    sizes = (frame_count, strip_count, height, strip)
    frame_even, frame_odd, far_c, far_d = pair_lists(frame_count)
    tile_even, tile_odd, _, _ = pair_lists(strip_count)
    frame_pos = lax.axis_index("frame")
    strip_pos = lax.axis_index("tile")
    place = jnp.stack([frame_pos, strip_pos]).astype(jnp.int32)

    qa = swap(queries, "frame", frame_even)
    qb = swap(queries, "frame", frame_odd)
    ga = swap(grad_out, "frame", frame_even)
    gb = swap(grad_out, "frame", frame_odd)

    smem = pl.BlockSpec(memory_space=pltpu.SMEM)
    whole = pl.BlockSpec(memory_space=pltpu.VMEM)

    def call(kernel, name, scalars, arrays, outs, scratch=(), flops=FLOPS):
        return pl.pallas_call(
            lambda *refs: kernel(sizes, *refs),
            name=name,
            in_specs=[smem] * len(scalars) + [whole] * len(arrays),
            out_specs=[whole] * len(outs),
            out_shape=[pltpu.VMEM(shape, dtype) for shape, dtype in outs],
            scratch_shapes=list(scratch),
            cost_estimate=pl.CostEstimate(flops=flops, transcendentals=0, bytes_accessed=0),
            compiler_params=pltpu.CompilerParams(vmem_limit_bytes=KERNEL_VMEM),
        )(*scalars, *[vmem(x) for x in arrays])

    f32 = jnp.float32
    ea, eb = call(
        edges_kernel, "edges", (place,), (keys, values), [((2, half, chans), jnp.bfloat16)] * 2
    )
    ha = swap(ea, "tile", tile_even)
    hb = swap(eb, "tile", tile_odd)
    expo, p0, st, own_delta = call(
        scores_kernel,
        "scores",
        (window, place),
        (queries, qa, qb, grad_out, keys, values, ha, hb),
        [
            ((heads, ext, 3 * rows), f32),
            ((heads, ext, rows), f32),
            ((heads, 3, 3 * rows), f32),
            ((heads, 1, rows), f32),
        ],
        [pltpu.VMEM((ext, 3 * rows), f32)],
    )
    pn, local_delta, a_st, b_st, c_st, d_st = call(
        deltas_kernel,
        "deltas",
        (place,),
        (ga, gb, values, ha, hb, expo, st, own_delta),
        [((heads, ext, 2 * rows), f32), ((heads, 1, 3 * rows), f32)]
        + [((heads, n, rows), f32) for n in (4, 4, 2, 2)],
    )
    a_st = swap(a_st, "frame", frame_even)
    b_st = swap(b_st, "frame", frame_odd)
    if far_c:
        c_st = swap(c_st, "frame", far_c)
    if far_d:
        d_st = swap(d_st, "frame", far_d)

    data = (queries, qa, qb, grad_out, ga, gb, expo, p0, pn)
    rb, ra, row = call(
        halo_kernel,
        "halo_grads",
        (place,),
        data + (st, local_delta, a_st, b_st, c_st, d_st),
        [((2, half, chans), jnp.bfloat16)] * 2 + [((heads, 2, 3 * rows), f32)],
    )
    rb = swap(rb, "tile", tile_odd)
    ra = swap(ra, "tile", tile_even)
    dk, dv = call(
        main_kernel,
        "main_grads",
        (),
        (row,) + data,
        [((rows, chans), f32)] * 2,
    )

    step_rows = height // FINISH_STEPS
    out_spec = pl.BlockSpec((1, step_rows, strip, chans), lambda i: (0, i, 0, 0))
    return pl.pallas_call(
        lambda *refs: finish_kernel(sizes, step_rows, *refs),
        name="finish",
        grid=(FINISH_STEPS,),
        compiler_params=pltpu.CompilerParams(vmem_limit_bytes=KERNEL_VMEM),
        in_specs=[smem] + [whole] * 4,
        out_specs=[out_spec, out_spec],
        out_shape=[jax.ShapeDtypeStruct(keys.shape, jnp.bfloat16)] * 2,
    )(place, vmem(rb), vmem(ra), vmem(dk), vmem(dv))


def solution(mesh):
    spec = P(("clip", "frame"), None, "tile", None)
    return jax.shard_map(
        on_device,
        mesh=mesh,
        in_specs=(spec, spec, spec, spec, P()),
        out_specs=(spec, spec),
        check_vma=False,
    )
```

time: 51.4 us -> 46.7 us (0.909)
  waiting for transfers between devices: 18.6 us -> 8.73 us
  starting transfers between devices: 20.5 us -> 23.2 us
  local copies, waits for them, and re-layouts: 1.49 us -> 3.77 us
  Pallas kernels: 8.77 us -> 9.79 us
  other arithmetic: 0.9 us -> 0.08 us
    ppermute x11, waiting for transfers between devices: 18.6 us -> 8.73 us  [swap(): return lax.ppermute(value, axis, pairs)]
    unnamed x11 -> x13, local copies, waits for them, and re-layouts: 0.12 us -> 3.77 us
    ppermute x11, starting transfers between devices: 20.5 us -> 23.2 us  [swap(): return lax.ppermute(value, axis, pairs)]
    another operation x1 -> x0, local copies, waits for them, and re-layouts: 1.37 us -> none  [edge(): return jnp.stack(cut)]
    pallas_call x4 -> x5, Pallas kernels: 6.73 us -> 7.76 us  [call(): pl.pallas_call(lambda *refs: kernel(sizes, *refs), name=name, in_specs=[s...]
    another operation x2 -> x0, other arithmetic: 0.82 us -> none  [edge(): return jnp.stack(cut)]
  transfers between devices with their start and end apart: 11 -> 11, of which waited for: 4 -> 4; matrix products, arithmetic and copies ran while one was open for 2% -> 2% of each run, Pallas kernels for 5% -> 11%
where the time goes in v3:
time: 46.7 us; the launch traced here: 46.3 us
  starting transfers between devices  23.2 us (50%)
  Pallas kernels  9.79 us (21%)
  waiting for transfers between devices  8.73 us (19%)
  local copies, waits for them, and re-layouts  3.77 us (8%)
  between operations  0.75 us (2%)
    ppermute x11, starting transfers between devices, swap(): return lax.ppermute(value, axis, pairs)  23.2 us
    ppermute x11, waiting for transfers between devices, swap(): return lax.ppermute(value, axis, pairs)  8.73 us
    pallas_call x5, Pallas kernels, call(): pl.pallas_call(lambda *refs: kernel(sizes, *refs), name=name, in_specs=[s...  7.76 us
    unnamed x13, local copies, waits for them, and re-layouts  3.77 us
    pallas_call x1, Pallas kernels, on_device(): pl.pallas_call(lambda *refs: finish_kernel(sizes, step_rows, *refs), name...  2.03 us
  transfers between devices with their start and end apart: 11, of which 4 were waited for; matrix products, arithmetic and copies ran while one was open for 2% of the time, Pallas kernels for 11%

profile of v3, /device:TPU:1, one launch (start us, length us, event | category | flops | bytes accessed | tf_op | source)
XLA Modules:
  0.0 46.3 jit_solution(16812060021382308649)
XLA Ops:
  0.6 2.2 %collective-permute-start = (bf16[1,8,16,1536]{3,2,1,0:T(8,128)(2,1)}, bf16[1,8,16,1536]{3,2,1,0:T(8,128)(2,1)S(1)}, u32[]{:S(2)}, u32[]{:S(2)}) collective-permute-start(bf16[1,8,16,1536]{3,2,1,0:T(8,128)(2,1)} %refs_1_.5), channel_id=1, source_target_pairs={{0,4},{8,12},{4,0},{12,8},{1,5},{9,13},{5,1},{13,9},{2,6},{10,14},... | collective-permute-start | bytes 1179656 | tf_op jit(solution)/shard_map/ppermute | solution.py:31
  2.8 0.7 %collective-permute-start.1 = (bf16[1,8,16,1536]{3,2,1,0:T(8,128)(2,1)}, bf16[1,8,16,1536]{3,2,1,0:T(8,128)(2,1)S(1)}, u32[]{:S(2)}, u32[]{:S(2)}) collective-permute-start(bf16[1,8,16,1536]{3,2,1,0:T(8,128)(2,1)} %refs_1_.5), channel_id=1, source_target_pairs={{4,8},{8,4},{5,9},{9,5},{6,10},{10,6},{7,11},{11,7},{20,24},{24,20... | collective-permute-start | bytes 1179656 | tf_op jit(solution)/shard_map/ppermute | solution.py:31
  3.5 0.1 pad_add_fusion.refs_0_.refs_1_
  3.6 1.0 %copy-done.2 = bf16[1,8,16,1536]{3,2,1,0:T(8,128)(2,1)S(1)} copy-done((bf16[1,8,16,1536]{3,2,1,0:T(8,128)(2,1)S(1)}, bf16[1,8,16,1536]{3,2,1,0:T(8,128)(2,1)}, u32[]{:S(2)}) %copy-start.2) | copy-done | bytes 393240
  4.6 1.0 %copy-done.4 = bf16[1,8,16,1536]{3,2,1,0:T(8,128)(2,1)S(1)} copy-done((bf16[1,8,16,1536]{3,2,1,0:T(8,128)(2,1)S(1)}, bf16[1,8,16,1536]{3,2,1,0:T(8,128)(2,1)}, u32[]{:S(2)}) %copy-start.4) | copy-done | bytes 393240
  5.6 1.5 %edges.1 = (bf16[2,64,1536]{2,1,0:T(8,128)(2,1)}, bf16[2,64,1536]{2,1,0:T(8,128)(2,1)}) custom-call(s32[2]{0:T(128)S(1)} %pad_add_fusion.refs_0_.refs_1_, bf16[1,8,16,1536]{3,2,1,0:T(8,128)(2,1)S(1)} %copy-done.4, bf16[1,8,16,1536]{3,2,1,0:T(8,128)(2,1)S(1)} %copy-done.2), custom_call_target="tpu_custom_call" | custom-call | flops 1500000000 | tf_op jit(solution)/shard_map/edges/pallas_call | solution.py:283
  7.1 1.0 %collective-permute-start.4 = (bf16[2,64,1536]{2,1,0:T(8,128)(2,1)}, bf16[2,64,1536]{2,1,0:T(8,128)(2,1)S(1)}, u32[]{:S(2)}, u32[]{:S(2)}) collective-permute-start(bf16[2,64,1536]{2,1,0:T(8,128)(2,1)} %get-tuple-element.19), channel_id=1, source_target_pairs={{0,1},{2,3},{1,0},{3,2},{4,5},{6,7},{5,4},{7,6},{8,9},{10,11},{9,8... | collective-permute-start | bytes 1179656 | tf_op jit(solution)/shard_map/ppermute | solution.py:31
  8.0 3.0 %collective-permute-start.5 = (bf16[2,64,1536]{2,1,0:T(8,128)(2,1)}, bf16[2,64,1536]{2,1,0:T(8,128)(2,1)S(1)}, u32[]{:S(2)}, u32[]{:S(2)}) collective-permute-start(bf16[2,64,1536]{2,1,0:T(8,128)(2,1)} %get-tuple-element.20), channel_id=1, source_target_pairs={{1,2},{2,1},{5,6},{6,5},{9,10},{10,9},{13,14},{14,13},{17,18},{18,... | collective-permute-start | bytes 1179656 | tf_op jit(solution)/shard_map/ppermute | solution.py:31
  11.1 4.2 %collective-permute-start.2 = (bf16[1,8,16,1536]{3,2,1,0:T(8,128)(2,1)S(1)}, bf16[1,8,16,1536]{3,2,1,0:T(8,128)(2,1)S(1)}, u32[]{:S(2)}, u32[]{:S(2)}) collective-permute-start(bf16[1,8,16,1536]{3,2,1,0:T(8,128)(2,1)S(1)} %copy-done.1), channel_id=1, source_target_pairs={{0,4},{8,12},{4,0},{12,8},{1,5},{9,13},{5,1},{13,9},{2,6},{10,14},... | collective-permute-start | bytes 1179656 | tf_op jit(solution)/shard_map/ppermute | solution.py:31
  15.2 0.0 collective-permute-done.refs_3_.refs_2_
  15.2 0.7 %collective-permute-start.3 = (bf16[1,8,16,1536]{3,2,1,0:T(8,128)(2,1)S(1)}, bf16[1,8,16,1536]{3,2,1,0:T(8,128)(2,1)S(1)}, u32[]{:S(2)}, u32[]{:S(2)}) collective-permute-start(bf16[1,8,16,1536]{3,2,1,0:T(8,128)(2,1)S(1)} %copy-done.1), channel_id=1, source_target_pairs={{4,8},{8,4},{5,9},{9,5},{6,10},{10,6},{7,11},{11,7},{20,24},{24,20... | collective-permute-start | bytes 1179656 | tf_op jit(solution)/shard_map/ppermute | solution.py:31
  15.9 0.8 %copy.7.refs_0_ = s32[18,3]{1,0:T(8,128)S(1)} copy(s32[18,3]{0,1:T(4,128)} %param.9) | data formatting | bytes 432 | tf_op args[4]
  16.7 0.0 collective-permute-done.1.refs_4_.refs_3_
  16.7 0.0 collective-permute-done.4.refs_8_.refs_4_
  16.7 0.9 %collective-permute-done.5.refs_9_.refs_5_ = bf16[2,64,1536]{2,1,0:T(8,128)(2,1)S(1)} collective-permute-done((bf16[2,64,1536]{2,1,0:T(8,128)(2,1)}, bf16[2,64,1536]{2,1,0:T(8,128)(2,1)S(1)}, u32[]{:S(2)}, u32[]{:S(2)}) %collective-permute-start.5) | collective-permute-done | bytes 393248 | tf_op jit(solution)/shard_map/ppermute | solution.py:31
  17.6 1.0 %copy-done.5 = bf16[1,8,16,1536]{3,2,1,0:T(8,128)(2,1)S(1)} copy-done((bf16[1,8,16,1536]{3,2,1,0:T(8,128)(2,1)S(1)}, bf16[1,8,16,1536]{3,2,1,0:T(8,128)(2,1)}, u32[]{:S(2)}) %copy-start.5) | copy-done | bytes 393240
  18.6 2.6 %scores.1 = (f32[12,256,384]{2,1,0:T(8,128)S(1)}, f32[12,256,128]{2,1,0:T(8,128)S(1)}, f32[12,3,384]{2,1,0:T(4,128)S(1)}, f32[12,1,128]{2,1,0:T(1,128)S(1)}) custom-call(s32[18,3]{1,0:T(8,128)S(1)} %copy.7.refs_0_, s32[2]{0:T(128)S(1)} %pad_add_fusion.refs_0_.refs_1_, bf16[1,8,16,1536]{3,2,1,0:T(8,128)(2,1)S(1)} %copy-done, ...), custom_call_target="tpu_custom_call" | custom-call | flops 1500000000 | tf_op jit(solution)/shard_map/scores/pallas_call | solution.py:283
  21.2 1.2 %collective-permute-done.2.refs_1_.refs_5_ = bf16[1,8,16,1536]{3,2,1,0:T(8,128)(2,1)S(1)} collective-permute-done((bf16[1,8,16,1536]{3,2,1,0:T(8,128)(2,1)S(1)}, bf16[1,8,16,1536]{3,2,1,0:T(8,128)(2,1)S(1)}, u32[]{:S(2)}, u32[]{:S(2)}) %collective-permute-start.2) | collective-permute-done | bytes 393248 | tf_op jit(solution)/shard_map/ppermute | solution.py:31
  22.4 0.0 collective-permute-done.3.refs_2_.refs_6_
  22.4 1.1 %deltas.1 = (f32[12,256,256]{2,1,0:T(8,128)S(1)}, f32[12,1,384]{2,1,0:T(1,128)S(1)}, f32[12,4,128]{2,1,0:T(4,128)S(1)}, f32[12,4,128]{2,1,0:T(4,128)S(1)}, f32[1...) custom-call(s32[2]{0:T(128)S(1)} %pad_add_fusion.refs_0_.refs_1_, ...), custom_call_target="tpu_custom_call" | custom-call | flops 1500000000 | tf_op jit(solution)/shard_map/deltas/pallas_call | solution.py:283
  23.6 5.5 %collective-permute-start.6 = (f32[12,4,128]{2,1,0:T(4,128)S(1)}, f32[12,4,128]{2,1,0:T(4,128)S(1)}, u32[]{:S(2)}, u32[]{:S(2)}) collective-permute-start(f32[12,4,128]{2,1,0:T(4,128)S(1)} %get-tuple-element.27), channel_id=1, source_target_pairs={{0,4},{8,12},{4,0},{12,8},{1,5},{9,13},{5,1},{13,9},{2,6},{10,14},... | collective-permute-start | bytes 73736 | tf_op jit(solution)/shard_map/ppermute | solution.py:31
  29.0 0.7 %collective-permute-start.7 = (f32[12,4,128]{2,1,0:T(4,128)S(1)}, f32[12,4,128]{2,1,0:T(4,128)S(1)}, u32[]{:S(2)}, u32[]{:S(2)}) collective-permute-start(f32[12,4,128]{2,1,0:T(4,128)S(1)} %get-tuple-element.28), channel_id=1, source_target_pairs={{4,8},{8,4},{5,9},{9,5},{6,10},{10,6},{7,11},{11,7},{20,24},{24,20... | collective-permute-start | bytes 73736 | tf_op jit(solution)/shard_map/ppermute | solution.py:31
  29.7 2.5 %collective-permute-start.8 = (f32[12,2,128]{2,1,0:T(2,128)S(1)}, f32[12,2,128]{2,1,0:T(2,128)S(1)}, u32[]{:S(2)}, u32[]{:S(2)}) collective-permute-start(f32[12,2,128]{2,1,0:T(2,128)S(1)} %get-tuple-element.29), channel_id=1, source_target_pairs={{0,8},{4,12},{8,0},{12,4},{1,9},{5,13},{9,1},{13,5},{2,10},{6,14},... | collective-permute-start | bytes 36872 | tf_op jit(solution)/shard_map/ppermute | solution.py:31
  32.2 1.3 %collective-permute-done.8.refs_14_ = f32[12,2,128]{2,1,0:T(2,128)S(1)} collective-permute-done((f32[12,2,128]{2,1,0:T(2,128)S(1)}, f32[12,2,128]{2,1,0:T(2,128)S(1)}, u32[]{:S(2)}, u32[]{:S(2)}) %collective-permute-start.8) | collective-permute-done | bytes 12320 | tf_op jit(solution)/shard_map/ppermute | solution.py:31
  33.5 0.0 collective-permute-done.6.refs_12_
  33.5 0.0 collective-permute-done.7.refs_13_
  33.5 1.7 %halo_grads.1 = (bf16[2,64,1536]{2,1,0:T(8,128)(2,1)S(1)}, bf16[2,64,1536]{2,1,0:T(8,128)(2,1)S(1)}, f32[12,2,384]{2,1,0:T(2,128)S(1)}) custom-call(s32[2]{0:T(128)S(1)} %pad_add_fusion.refs_0_.refs_1_, bf16[1,8,16,1536]{3,2,1,0:T(8,128)(2,1)S(1)} %copy-done, bf16[1,8,16,1536]{3,2,1,0:T(8,128)(2,1)S(1)} %collective-permute-done.refs_3_.refs_2_, ...), custom_call_target="tpu_custom_call" | custom-call | flops 1500000000 | tf_op jit(solution)/shard_map/halo_grads/pallas_call | solution.py:283
  35.2 2.8 %collective-permute-start.9 = (bf16[2,64,1536]{2,1,0:T(8,128)(2,1)S(1)}, bf16[2,64,1536]{2,1,0:T(8,128)(2,1)S(1)}, u32[]{:S(2)}, u32[]{:S(2)}) collective-permute-start(bf16[2,64,1536]{2,1,0:T(8,128)(2,1)S(1)} %get-tuple-element.31), channel_id=1, source_target_pairs={{1,2},{2,1},{5,6},{6,5},{9,10},{10,9},{13,14},{14,13},{17,18},{18,... | collective-permute-start | bytes 1179656 | tf_op jit(solution)/shard_map/ppermute | solution.py:31
  38.0 0.1 collective-permute-start.10
  38.1 0.9 %main_grads.1 = (f32[128,1536]{1,0:T(8,128)S(1)}, f32[128,1536]{1,0:T(8,128)S(1)}) custom-call(f32[12,2,384]{2,1,0:T(2,128)S(1)} %get-tuple-element.33.refs_0_, bf16[1,8,16,1536]{3,2,1,0:T(8,128)(2,1)S(1)} %copy-done, bf16[1,8,16,1536]{3,2,1,0:T(8,128)(2,1)S(1)} %collective-permute-done.refs_3_.refs_2_, ...), custom_call_target="tpu_custom_call" | custom-call | flops 1500000000 | tf_op jit(solution)/shard_map/main_grads/pallas_call | solution.py:283
  39.0 5.3 %collective-permute-done.9.refs_1_ = bf16[2,64,1536]{2,1,0:T(8,128)(2,1)S(1)} collective-permute-done((bf16[2,64,1536]{2,1,0:T(8,128)(2,1)S(1)}, bf16[2,64,1536]{2,1,0:T(8,128)(2,1)S(1)}, u32[]{:S(2)}, u32[]{:S(2)}) %collective-permute-start.9) | collective-permute-done | bytes 393248 | tf_op jit(solution)/shard_map/ppermute | solution.py:31
  44.3 2.0 %finish.1 = (bf16[1,8,16,1536]{3,2,1,0:T(8,128)(2,1)}, bf16[1,8,16,1536]{3,2,1,0:T(8,128)(2,1)}) custom-call(s32[2]{0:T(128)S(1)} %pad_add_fusion.refs_0_.refs_1_, bf16[2,64,1536]{2,1,0:T(8,128)(2,1)S(1)} %collective-permute-done.9.refs_1_, bf16[2,64,1536]{2,1,0:T(8,128)(2,1)S(1)} %collective-permute-done.10.refs_2_, ...), custom_call_target="tpu_custom_call" | custom-call | tf_op jit(solution)/shard_map/finish/pallas_call | solution.py:348
  (10 shorter events, 0.0 us)
Async XLA Ops:
  0.6 17.0 %copy-start = (bf16[1,8,16,1536]{3,2,1,0:T(8,128)(2,1)S(1)}, bf16[1,8,16,1536]{3,2,1,0:T(8,128)(2,1)}, u32[]{:S(2)}) copy-start(bf16[1,8,16,1536]{3,2,1,0:T(8,128)(2,1)} %refs_1_.5) | copy-start | bytes 1179652
  0.6 10.4 %copy-start.1 = (bf16[1,8,16,1536]{3,2,1,0:T(8,128)(2,1)S(1)}, bf16[1,8,16,1536]{3,2,1,0:T(8,128)(2,1)}, u32[]{:S(2)}) copy-start(bf16[1,8,16,1536]{3,2,1,0:T(8,128)(2,1)} %refs_4_.3) | copy-start | bytes 1179652
  0.6 14.6 %collective-permute-start = (bf16[1,8,16,1536]{3,2,1,0:T(8,128)(2,1)}, bf16[1,8,16,1536]{3,2,1,0:T(8,128)(2,1)S(1)}, u32[]{:S(2)}, u32[]{:S(2)}) collective-permute-start(bf16[1,8,16,1536]{3,2,1,0:T(8,128)(2,1)} %refs_1_.5), channel_id=1, source_target_pairs={{0,4},{8,12},{4,0},{12,8},{1,5},{9,13},{5,1},{13,9},{2,6},{10,14},... | collective-permute-start | bytes 1179656 | tf_op jit(solution)/shard_map/ppermute | solution.py:31
  2.8 13.9 %collective-permute-start.1 = (bf16[1,8,16,1536]{3,2,1,0:T(8,128)(2,1)}, bf16[1,8,16,1536]{3,2,1,0:T(8,128)(2,1)S(1)}, u32[]{:S(2)}, u32[]{:S(2)}) collective-permute-start(bf16[1,8,16,1536]{3,2,1,0:T(8,128)(2,1)} %refs_1_.5), channel_id=1, source_target_pairs={{4,8},{8,4},{5,9},{9,5},{6,10},{10,6},{7,11},{11,7},{20,24},{24,20... | collective-permute-start | bytes 1179656 | tf_op jit(solution)/shard_map/ppermute | solution.py:31
  3.6 1.0 %copy-start.2 = (bf16[1,8,16,1536]{3,2,1,0:T(8,128)(2,1)S(1)}, bf16[1,8,16,1536]{3,2,1,0:T(8,128)(2,1)}, u32[]{:S(2)}) copy-start(bf16[1,8,16,1536]{3,2,1,0:T(8,128)(2,1)} %refs_3_.1) | copy-start | bytes 1179652
  4.6 1.0 %copy-start.4 = (bf16[1,8,16,1536]{3,2,1,0:T(8,128)(2,1)S(1)}, bf16[1,8,16,1536]{3,2,1,0:T(8,128)(2,1)}, u32[]{:S(2)}) copy-start(bf16[1,8,16,1536]{3,2,1,0:T(8,128)(2,1)} %refs_6_.1) | copy-start | bytes 1179652
  5.6 12.0 %copy-start.3 = (bf16[1,8,16,1536]{3,2,1,0:T(8,128)(2,1)S(1)}, bf16[1,8,16,1536]{3,2,1,0:T(8,128)(2,1)}, u32[]{:S(2)}) copy-start(bf16[1,8,16,1536]{3,2,1,0:T(8,128)(2,1)} %refs_3_.1) | copy-start | bytes 1179652
  7.1 9.6 %collective-permute-start.4 = (bf16[2,64,1536]{2,1,0:T(8,128)(2,1)}, bf16[2,64,1536]{2,1,0:T(8,128)(2,1)S(1)}, u32[]{:S(2)}, u32[]{:S(2)}) collective-permute-start(bf16[2,64,1536]{2,1,0:T(8,128)(2,1)} %get-tuple-element.19), channel_id=1, source_target_pairs={{0,1},{2,3},{1,0},{3,2},{4,5},{6,7},{5,4},{7,6},{8,9},{10,11},{9,8... | collective-permute-start | bytes 1179656 | tf_op jit(solution)/shard_map/ppermute | solution.py:31
  8.0 9.6 %collective-permute-start.5 = (bf16[2,64,1536]{2,1,0:T(8,128)(2,1)}, bf16[2,64,1536]{2,1,0:T(8,128)(2,1)S(1)}, u32[]{:S(2)}, u32[]{:S(2)}) collective-permute-start(bf16[2,64,1536]{2,1,0:T(8,128)(2,1)} %get-tuple-element.20), channel_id=1, source_target_pairs={{1,2},{2,1},{5,6},{6,5},{9,10},{10,9},{13,14},{14,13},{17,18},{18,... | collective-permute-start | bytes 1179656 | tf_op jit(solution)/shard_map/ppermute | solution.py:31
  11.1 11.4 %collective-permute-start.2 = (bf16[1,8,16,1536]{3,2,1,0:T(8,128)(2,1)S(1)}, bf16[1,8,16,1536]{3,2,1,0:T(8,128)(2,1)S(1)}, u32[]{:S(2)}, u32[]{:S(2)}) collective-permute-start(bf16[1,8,16,1536]{3,2,1,0:T(8,128)(2,1)S(1)} %copy-done.1), channel_id=1, source_target_pairs={{0,4},{8,12},{4,0},{12,8},{1,5},{9,13},{5,1},{13,9},{2,6},{10,14},... | collective-permute-start | bytes 1179656 | tf_op jit(solution)/shard_map/ppermute | solution.py:31
  15.2 7.2 %collective-permute-start.3 = (bf16[1,8,16,1536]{3,2,1,0:T(8,128)(2,1)S(1)}, bf16[1,8,16,1536]{3,2,1,0:T(8,128)(2,1)S(1)}, u32[]{:S(2)}, u32[]{:S(2)}) collective-permute-start(bf16[1,8,16,1536]{3,2,1,0:T(8,128)(2,1)S(1)} %copy-done.1), channel_id=1, source_target_pairs={{4,8},{8,4},{5,9},{9,5},{6,10},{10,6},{7,11},{11,7},{20,24},{24,20... | collective-permute-start | bytes 1179656 | tf_op jit(solution)/shard_map/ppermute | solution.py:31
  17.6 1.0 %copy-start.5 = (bf16[1,8,16,1536]{3,2,1,0:T(8,128)(2,1)S(1)}, bf16[1,8,16,1536]{3,2,1,0:T(8,128)(2,1)}, u32[]{:S(2)}) copy-start(bf16[1,8,16,1536]{3,2,1,0:T(8,128)(2,1)} %refs_6_.1) | copy-start | bytes 1179652
  23.6 9.9 %collective-permute-start.6 = (f32[12,4,128]{2,1,0:T(4,128)S(1)}, f32[12,4,128]{2,1,0:T(4,128)S(1)}, u32[]{:S(2)}, u32[]{:S(2)}) collective-permute-start(f32[12,4,128]{2,1,0:T(4,128)S(1)} %get-tuple-element.27), channel_id=1, source_target_pairs={{0,4},{8,12},{4,0},{12,8},{1,5},{9,13},{5,1},{13,9},{2,6},{10,14},... | collective-permute-start | bytes 73736 | tf_op jit(solution)/shard_map/ppermute | solution.py:31
  29.0 4.4 %collective-permute-start.7 = (f32[12,4,128]{2,1,0:T(4,128)S(1)}, f32[12,4,128]{2,1,0:T(4,128)S(1)}, u32[]{:S(2)}, u32[]{:S(2)}) collective-permute-start(f32[12,4,128]{2,1,0:T(4,128)S(1)} %get-tuple-element.28), channel_id=1, source_target_pairs={{4,8},{8,4},{5,9},{9,5},{6,10},{10,6},{7,11},{11,7},{20,24},{24,20... | collective-permute-start | bytes 73736 | tf_op jit(solution)/shard_map/ppermute | solution.py:31
  29.7 3.8 %collective-permute-start.8 = (f32[12,2,128]{2,1,0:T(2,128)S(1)}, f32[12,2,128]{2,1,0:T(2,128)S(1)}, u32[]{:S(2)}, u32[]{:S(2)}) collective-permute-start(f32[12,2,128]{2,1,0:T(2,128)S(1)} %get-tuple-element.29), channel_id=1, source_target_pairs={{0,8},{4,12},{8,0},{12,4},{1,9},{5,13},{9,1},{13,5},{2,10},{6,14},... | collective-permute-start | bytes 36872 | tf_op jit(solution)/shard_map/ppermute | solution.py:31
  35.2 9.1 %collective-permute-start.9 = (bf16[2,64,1536]{2,1,0:T(8,128)(2,1)S(1)}, bf16[2,64,1536]{2,1,0:T(8,128)(2,1)S(1)}, u32[]{:S(2)}, u32[]{:S(2)}) collective-permute-start(bf16[2,64,1536]{2,1,0:T(8,128)(2,1)S(1)} %get-tuple-element.31), channel_id=1, source_target_pairs={{1,2},{2,1},{5,6},{6,5},{9,10},{10,9},{13,14},{14,13},{17,18},{18,... | collective-permute-start | bytes 1179656 | tf_op jit(solution)/shard_map/ppermute | solution.py:31
  38.0 6.3 %collective-permute-start.10 = (bf16[2,64,1536]{2,1,0:T(8,128)(2,1)S(1)}, bf16[2,64,1536]{2,1,0:T(8,128)(2,1)S(1)}, u32[]{:S(2)}, u32[]{:S(2)}) collective-permute-start(bf16[2,64,1536]{2,1,0:T(8,128)(2,1)S(1)} %get-tuple-element.32), channel_id=1, source_target_pairs={{0,1},{2,3},{1,0},{3,2},{4,5},{6,7},{5,4},{7,6},{8,9},{10,11},{9,8... | collective-permute-start | bytes 1179656 | tf_op jit(solution)/shard_map/ppermute | solution.py:31

commit v4 on v2

v4 whole, which is shorter than its diff:
```python
import math

import jax
import jax.numpy as jnp
from jax import lax
from jax.experimental import pallas as pl
from jax.experimental.pallas import tpu as pltpu
from jax.sharding import PartitionSpec as P

HD = 128
TH = 4
TW = 8
FINISH_STEPS = 4
FLOPS = 1_000_000_000
KERNEL_VMEM = 16 << 20
NEG = -1e30
FLOOR = -1e29
SCALE = HD ** (-0.5)
SCALE2 = SCALE * math.log2(math.e)


def pair_lists(count):
    even = [(i, i + 1) for i in range(0, count - 1, 2)]
    odd = [(i, i + 1) for i in range(1, count - 1, 2)]
    far_a = [(i, i + 2) for i in range(count - 2) if i % 4 in (0, 1)]
    far_b = [(i, i + 2) for i in range(count - 2) if i % 4 in (2, 3)]
    return [pairs + [(j, i) for i, j in pairs] for pairs in (even, odd, far_a, far_b)]


def swap(value, axis, pairs):
    return lax.ppermute(value, axis, pairs)


def bit_table(window_ref):
    bits = jnp.int32(0)
    for i in range(window_ref.shape[1]):
        code = (window_ref[0, i] + 1) * 9 + (window_ref[1, i] + 1) * 3 + (window_ref[2, i] + 1)
        bits = bits | jnp.left_shift(jnp.int32(1), code)
    return bits


def position_facts(place_ref, frame_count, strip_count):
    frame = place_ref[0]
    strip = place_ref[1]
    step_f = 1 - 2 * (frame & 1)
    step_s = 1 - 2 * (strip & 1)
    return (
        frame,
        step_f,
        step_s,
        ((frame + step_f >= 0) & (frame + step_f < frame_count)).astype(jnp.int32),
        ((frame - step_f >= 0) & (frame - step_f < frame_count)).astype(jnp.int32),
        ((strip + step_s >= 0) & (strip + step_s < strip_count)).astype(jnp.int32),
        ((strip - step_s >= 0) & (strip - step_s < strip_count)).astype(jnp.int32),
    )


def fill_bias(bias_ref, slots, window_ref, place_ref, frame_count, strip_count, height, strip):
    bits = bit_table(window_ref)
    _, step_f, step_s, has_fa, has_fb, has_sa, has_sb = position_facts(
        place_ref, frame_count, strip_count
    )
    rows = height * strip
    half = height * TW
    tiles = strip // TW
    col_a = jnp.where(step_s > 0, tiles, -1)
    col_b = jnp.where(step_s > 0, -1, tiles)
    frames = ((0, 1), (-step_f, has_fa), (step_f, has_fb))
    for place, slot in enumerate(slots):
        off_time, has_f = frames[slot]
        start = 0
        for length, wide, k_col, has_s in (
            (rows, strip, None, 1),
            (half, TW, col_a, has_sa),
            (half, TW, col_b, has_sb),
        ):
            key_idx = lax.broadcasted_iota(jnp.int32, (length, rows), 0)
            query_idx = lax.broadcasted_iota(jnp.int32, (length, rows), 1)
            off_high = key_idx // (wide * TH) - query_idx // (strip * TH)
            k_wide = (key_idx % wide) // TW if k_col is None else k_col
            off_wide = k_wide - (query_idx % strip) // TW
            near = (jnp.abs(off_wide) <= 1) & (jnp.abs(off_high) <= 1)
            code = (off_time + 1) * 9 + (off_high + 1) * 3 + (off_wide + 1)
            listed = jnp.right_shift(bits, jnp.where(near, code, 0)) & 1
            flag = jnp.where(near, listed, 0) * (has_f * has_s)
            bias_ref[start : start + length, place * rows : (place + 1) * rows] = jnp.where(
                flag == 1, jnp.float32(0), jnp.float32(NEG)
            )
            start += length


def lanes_of(head):
    return slice(head * HD, (head + 1) * HD)


def head_rows(ref, which, head):
    return ref[which, :, :, lanes_of(head)].reshape(-1, HD)


def load_keys(kv, a_ref, b_ref, which, head):
    lanes = lanes_of(head)
    return jnp.concatenate(
        [head_rows(kv, which, head), a_ref[which, :, lanes], b_ref[which, :, lanes]], axis=0
    )


def dot_nt(a, b):
    return lax.dot_general(a, b, (((1,), (1,)), ((), ())), preferred_element_type=jnp.float32)


def run_copies(pairs, sems):
    copies = [pltpu.make_async_copy(src, dst, sems.at[i]) for i, (src, dst) in enumerate(pairs)]
    for copy in copies:
        copy.start()
    for copy in copies:
        copy.wait()


def pair_kernel(q_in, g_in, out, sems):
    run_copies([(q_in.at[0], out.at[0]), (g_in.at[0], out.at[1])], sems)


def stage_kernel(sizes, place_ref, k_in, v_in, out, a_out, b_out, sems):
    _, _, height, strip = sizes
    even = (place_ref[1] & 1) == 0
    start_a = pl.multiple_of(jnp.where(even, strip - TW, 0), TW)
    start_b = pl.multiple_of(jnp.where(even, 0, strip - TW), TW)
    pairs = []
    for edge, start in ((a_out, start_a), (b_out, start_b)):
        for which, ref in enumerate((k_in, v_in)):
            for row in range(height):
                pairs.append((ref.at[0, row, pl.ds(start, TW), :], edge.at[which, row * TW : (row + 1) * TW, :]))
    run_copies(pairs + [(k_in.at[0], out.at[0]), (v_in.at[0], out.at[1])], sems)


def local_stats(head, frames, kv, ha, hb, bias):
    query, grad = (
        jnp.concatenate([head_rows(ref, which, head) for ref in frames], axis=0) for which in (0, 1)
    )
    scores = dot_nt(load_keys(kv, ha, hb, 0, head), query) * SCALE2 + bias
    grad_probs = dot_nt(load_keys(kv, ha, hb, 1, head), grad)
    top = jnp.max(scores, axis=0, keepdims=True)
    expo = jnp.exp2(scores - top)
    total = jnp.sum(expo, axis=0, keepdims=True)
    delta = jnp.sum(expo * grad_probs, axis=0, keepdims=True) / total
    return expo, grad_probs, jnp.concatenate([top + jnp.log2(total), delta, top], axis=0)


def own_kernel(sizes, window_ref, place_ref, own, kv, ha, hb, st_out, expo_out, gp_out, bias_ref):
    fill_bias(bias_ref, (0,), window_ref, place_ref, *sizes)
    for head in range(st_out.shape[0]):
        expo_out[head], gp_out[head], st_out[head] = local_stats(head, (own,), kv, ha, hb, bias_ref[...])


def near_kernel(sizes, window_ref, place_ref, near_a, near_b, kv, ha, hb, own_st, st_out, a_out, b_out, c_out, d_out, expo_out, gp_out, bias_ref):
    rows = sizes[2] * sizes[3]
    fill_bias(bias_ref, (1, 2), window_ref, place_ref, *sizes)
    far_slot_a = ((place_ref[0] & 3) == 0) | ((place_ref[0] & 3) == 3)
    for head in range(st_out.shape[0]):
        expo_out[head], gp_out[head], near = local_stats(
            head, (near_a, near_b), kv, ha, hb, bias_ref[...]
        )
        st_out[head] = near
        own = own_st[head][0:2]
        part_a = near[0:2, :rows]
        part_b = near[0:2, rows:]
        a_out[head] = jnp.concatenate([own, part_a], axis=0)
        b_out[head] = jnp.concatenate([own, part_b], axis=0)
        c_out[head] = jnp.where(far_slot_a, part_a, part_b)
        d_out[head] = jnp.where(far_slot_a, part_b, part_a)


def merge(parts):
    top = parts[0][0]
    for lse, _ in parts[1:]:
        top = jnp.maximum(top, lse)
    weight_sum = jnp.zeros_like(top)
    delta_sum = jnp.zeros_like(top)
    for lse, delta in parts:
        weight = jnp.exp2(lse - top)
        weight_sum = weight_sum + weight
        delta_sum = delta_sum + weight * delta
    return jnp.maximum(top + jnp.log2(weight_sum), FLOOR), delta_sum / weight_sum


def halo_kernel(sizes, place_ref, c_st, d_st, b_st, a_st, own, near_a, near_b, e0, en, p0, pn, own_st, near_st, rb_out, ra_out, row_out):
    frame_count, strip_count, height, strip = sizes
    rows = height * strip
    half = height * TW
    frame, step_f, _, has_fa, has_fb, _, _ = position_facts(place_ref, frame_count, strip_count)
    beyond_a = frame + 2 * step_f
    beyond_b = frame - 2 * step_f
    has_ba = (beyond_a >= 0) & (beyond_a < frame_count)
    has_bb = (beyond_b >= 0) & (beyond_b < frame_count)
    far_slot_a = ((frame & 3) == 0) | ((frame & 3) == 3)

    def part(block, row, exists):
        return (jnp.where(exists, block[row : row + 1, :], NEG), block[row + 1 : row + 2, :])

    for head in range(own_st.shape[0]):
        from_a, from_b, from_c, from_d = (r[head] for r in (a_st, b_st, c_st, d_st))
        stat = jnp.concatenate([own_st[head], near_st[head]], axis=1)
        own_part, part_a, part_b = (
            (stat[0:1, i * rows : (i + 1) * rows], stat[1:2, i * rows : (i + 1) * rows]) for i in range(3)
        )
        far_a = jnp.where(far_slot_a, from_c, from_d)
        far_b = jnp.where(far_slot_a, from_d, from_c)
        merged = [
            merge([own_part, part(from_a, 2, has_fa == 1), part(from_b, 2, has_fb == 1)]),
            merge([part_a, part(from_a, 0, has_fa == 1), part(far_a, 0, has_ba)]),
            merge([part_b, part(from_b, 0, has_fb == 1), part(far_b, 0, has_bb)]),
        ]
        lse = jnp.concatenate([m[0] for m in merged], axis=1)
        delta = jnp.concatenate([m[1] for m in merged], axis=1)
        row = jnp.concatenate([jnp.exp2(stat[2:3] - lse), delta], axis=0)
        row_out[head] = row
        key_part, value_part = head_grads(
            head, slice(rows, rows + 2 * half), row, own, near_a, near_b, e0, en, p0, pn
        )
        lanes = lanes_of(head)
        for out, lo in ((ra_out, 0), (rb_out, half)):
            out[0, :, lanes] = key_part[lo : lo + half].astype(jnp.bfloat16)
            out[1, :, lanes] = value_part[lo : lo + half].astype(jnp.bfloat16)


def head_grads(head, keys, row, own, near_a, near_b, e0, en, p0, pn):
    query, grad = (
        jnp.concatenate([head_rows(r, which, head) for r in (own, near_a, near_b)], axis=0)
        for which in (0, 1)
    )
    expo = jnp.concatenate([e0[head, keys, :], en[head, keys, :]], axis=1)
    grad_probs = jnp.concatenate([p0[head, keys, :], pn[head, keys, :]], axis=1)
    factor = row[0:1]
    probs = expo * factor
    grad_scores = (expo * (factor * SCALE) * (grad_probs - row[1:2])).astype(jnp.bfloat16)
    value_part = jnp.dot(probs.astype(jnp.bfloat16), grad, preferred_element_type=jnp.float32)
    key_part = jnp.dot(grad_scores, query, preferred_element_type=jnp.float32)
    return key_part, value_part


def main_kernel(sizes, row_st, own, near_a, near_b, e0, en, p0, pn, dk_out, dv_out):
    rows = sizes[2] * sizes[3]
    for head in range(row_st.shape[0]):
        key_part, value_part = head_grads(
            head, slice(0, rows), row_st[head], own, near_a, near_b, e0, en, p0, pn
        )
        lanes = lanes_of(head)
        dk_out[:, lanes] = key_part
        dv_out[:, lanes] = value_part


def finish_kernel(sizes, place_ref, rb, ra, dk, dv, dk_out, dv_out, full_ref, sems):
    _, _, height, strip = sizes
    even = (place_ref[1] & 1) == 0
    count = height // FINISH_STEPS
    copies = []
    for step in range(FINISH_STEPS):
        lines = slice(step * count, (step + 1) * count)
        edge = slice(step * count * TW, (step + 1) * count * TW)
        span = slice(step * count * strip, (step + 1) * count * strip)
        for which, (part, out) in enumerate(((dk, dk_out), (dv, dv_out))):
            from_a = ra[which, edge, :].astype(jnp.float32).reshape(count, TW, -1)
            from_b = rb[which, edge, :].astype(jnp.float32).reshape(count, TW, -1)
            full = part[span, :].reshape(count, strip, -1)
            left = full[:, :TW] + jnp.where(even, from_b, from_a)
            right = full[:, TW:] + jnp.where(even, from_a, from_b)
            full_ref[which, lines] = jnp.concatenate([left, right], axis=1).astype(jnp.bfloat16)
            copy = pltpu.make_async_copy(
                full_ref.at[which, lines], out.at[0, lines], sems.at[2 * step + which]
            )
            copy.start()
            copies.append(copy)
    for copy in copies:
        copy.wait()


def vmem(value):
    return pltpu.with_memory_space_constraint(value, pltpu.VMEM)


def on_device(queries, keys, values, grad_out, window):
    _, height, strip, chans = queries.shape
    heads = chans // HD
    rows = height * strip
    half = height * TW
    ext = rows + 2 * half
    frame_count = lax.axis_size("frame")
    strip_count = lax.axis_size("tile")
    sizes = (frame_count, strip_count, height, strip)
    frame_even, frame_odd, far_c, far_d = pair_lists(frame_count)
    tile_even, tile_odd, _, _ = pair_lists(strip_count)
    frame_pos = lax.axis_index("frame")
    strip_pos = lax.axis_index("tile")
    place = jnp.stack([frame_pos, strip_pos]).astype(jnp.int32)

    smem = pl.BlockSpec(memory_space=pltpu.SMEM)
    whole = pl.BlockSpec(memory_space=pltpu.VMEM)
    raw = pl.BlockSpec(memory_space=pl.ANY)
    window = window.T

    def call(kernel, name, scalars, arrays, outs, scratch=(), flops=0):
        return pl.pallas_call(
            lambda *refs: kernel(sizes, *refs),
            name=name,
            in_specs=[smem] * len(scalars) + [whole] * len(arrays),
            out_specs=[whole] * len(outs),
            out_shape=[pltpu.VMEM(shape, dtype) for shape, dtype in outs],
            scratch_shapes=list(scratch),
            cost_estimate=pl.CostEstimate(flops=flops, transcendentals=0, bytes_accessed=0),
            compiler_params=pltpu.CompilerParams(vmem_limit_bytes=KERNEL_VMEM),
        )(*scalars, *[vmem(x) for x in arrays])

    def raw_call(kernel, name, arrays, scalars, outs, copies):
        return pl.pallas_call(
            kernel,
            name=name,
            in_specs=[smem] * len(scalars) + [raw] * len(arrays),
            out_specs=[whole] * len(outs),
            out_shape=[pltpu.VMEM(shape, jnp.bfloat16) for shape in outs],
            scratch_shapes=[pltpu.SemaphoreType.DMA((copies,))],
            compiler_params=pltpu.CompilerParams(vmem_limit_bytes=KERNEL_VMEM),
            cost_estimate=pl.CostEstimate(flops=0, transcendentals=0, bytes_accessed=0),
        )(*scalars, *[pltpu.with_memory_space_constraint(x, pltpu.HBM) for x in arrays])

    f32 = jnp.float32
    wide = queries.shape
    two = (2, height, strip, chans)
    edge = (2, half, chans)
    (own,) = raw_call(pair_kernel, "pair", (queries, grad_out), (), [two], 2)
    near_a = swap(own, "frame", frame_even)
    near_b = swap(own, "frame", frame_odd)
    kv, ea, eb = raw_call(
        lambda *refs: stage_kernel(sizes, *refs),
        "stage",
        (keys, values),
        (place,),
        [two, edge, edge],
        4 * height + 2,
    )
    hb = swap(eb, "tile", tile_odd)
    ha = swap(ea, "tile", tile_even)
    own_st, e0, p0 = call(
        own_kernel,
        "own_stats",
        (window, place),
        (own, kv, ha, hb),
        [((heads, 3, rows), f32), ((heads, ext, rows), f32), ((heads, ext, rows), f32)],
        [pltpu.VMEM((ext, rows), f32)],
    )
    near_st, a_st, b_st, c_st, d_st, en, pn = call(
        near_kernel,
        "near_stats",
        (window, place),
        (near_a, near_b, kv, ha, hb, own_st),
        [((heads, 3, 2 * rows), f32)]
        + [((heads, n, rows), f32) for n in (4, 4, 2, 2)]
        + [((heads, ext, 2 * rows), f32)] * 2,
        [pltpu.VMEM((ext, 2 * rows), f32)],
    )
    a_st = swap(a_st, "frame", frame_even)
    b_st = swap(b_st, "frame", frame_odd)
    if far_c:
        c_st = swap(c_st, "frame", far_c)
    if far_d:
        d_st = swap(d_st, "frame", far_d)

    data = (own, near_a, near_b, e0, en, p0, pn)
    rb, ra, row = call(
        halo_kernel,
        "halo_grads",
        (place,),
        (c_st, d_st, b_st, a_st) + data + (own_st, near_st),
        [(edge, jnp.bfloat16)] * 2 + [((heads, 2, 3 * rows), f32)],
    )
    rb = swap(rb, "tile", tile_odd)
    ra = swap(ra, "tile", tile_even)
    dk, dv = call(main_kernel, "main_grads", (), (row,) + data, [((rows, chans), f32)] * 2, flops=FLOPS)

    return pl.pallas_call(
        lambda *refs: finish_kernel(sizes, *refs),
        name="finish",
        compiler_params=pltpu.CompilerParams(vmem_limit_bytes=KERNEL_VMEM),
        in_specs=[smem] + [whole] * 4,
        out_specs=[raw, raw],
        out_shape=[jax.ShapeDtypeStruct(wide, jnp.bfloat16)] * 2,
        scratch_shapes=[
            pltpu.VMEM((2, height, strip, chans), jnp.bfloat16),
            pltpu.SemaphoreType.DMA((2 * FINISH_STEPS,)),
        ],
    )(place, vmem(rb), vmem(ra), vmem(dk), vmem(dv))


def solution(mesh):
    spec = P(("clip", "frame"), None, "tile", None)
    return jax.shard_map(
        on_device,
        mesh=mesh,
        in_specs=(spec, spec, spec, spec, P()),
        out_specs=(spec, spec),
        check_vma=False,
    )
```

time: 51.4 us -> 49.5 us (0.963)
  waiting for transfers between devices: 18.6 us -> 16 us
  Pallas kernels: 8.77 us -> 10.8 us
  other arithmetic: 0.9 us -> 0.08 us
  local copies, waits for them, and re-layouts: 1.49 us -> 0.68 us
    pallas_call x1 -> x3, Pallas kernels: 2.04 us -> 4.93 us  [the longest x2 3.42 us: raw_call(): pl.pallas_call(kernel, name=name, in_specs=[smem] * len(scalars) + [raw]...]
    ppermute x11 -> x9, waiting for transfers between devices: 18.6 us -> 16 us  [swap(): return lax.ppermute(value, axis, pairs)]
    another operation x1 -> x0, local copies, waits for them, and re-layouts: 1.37 us -> none  [edge(): return jnp.stack(cut)]
    pallas_call x4, Pallas kernels: 6.73 us -> 5.88 us  [call(): pl.pallas_call(lambda *refs: kernel(sizes, *refs), name=name, in_specs=[s...]
    another operation x2 -> x0, other arithmetic: 0.82 us -> none  [edge(): return jnp.stack(cut)]
    unnamed x11 -> x2, local copies, waits for them, and re-layouts: 0.12 us -> 0.68 us
    ppermute x11 -> x9, starting transfers between devices: 20.5 us -> 20.9 us  [swap(): return lax.ppermute(value, axis, pairs)]
  transfers between devices with their start and end apart: 11 -> 9, of which waited for: 4 -> 4; matrix products, arithmetic and copies ran while one was open for 2% -> 0% of each run, Pallas kernels for 5% -> 9%
where the time goes in v4:
time: 49.5 us; the launch traced here: 49.2 us
  starting transfers between devices  20.9 us (42%)
  waiting for transfers between devices  16 us (32%)
  Pallas kernels  10.8 us (22%)
  between operations  0.73 us (1%)
  local copies, waits for them, and re-layouts  0.68 us (1%)
    ppermute x9, starting transfers between devices, swap(): return lax.ppermute(value, axis, pairs)  20.9 us
    ppermute x9, waiting for transfers between devices, swap(): return lax.ppermute(value, axis, pairs)  16 us
    pallas_call x4, Pallas kernels, call(): pl.pallas_call(lambda *refs: kernel(sizes, *refs), name=name, in_specs=[s...  5.88 us
    pallas_call x2, Pallas kernels, raw_call(): pl.pallas_call(kernel, name=name, in_specs=[smem] * len(scalars) + [raw]...  3.42 us
    pallas_call x1, Pallas kernels, on_device(): pl.pallas_call(lambda *refs: finish_kernel(sizes, *refs), name='finish',...  1.5 us
  transfers between devices with their start and end apart: 9, of which 4 were waited for; matrix products, arithmetic and copies ran while one was open for 0% of the time, Pallas kernels for 9%

profile of v4, /device:TPU:1, one launch (start us, length us, event | category | flops | bytes accessed | tf_op | source)
XLA Modules:
  0.0 49.2 jit_solution(6134597617719939562)
XLA Ops:
  0.6 1.1 %pair.1.refs_2_.refs_5_.refs_1_ = bf16[2,8,16,1536]{3,2,1,0:T(8,128)(2,1)S(1)} custom-call(bf16[1,8,16,1536]{3,2,1,0:T(8,128)(2,1)} %q_in.1, bf16[1,8,16,1536]{3,2,1,0:T(8,128)(2,1)} %g_in.1), custom_call_target="tpu_custom_call" | custom-call | tf_op jit(solution)/shard_map/pair/pallas_call | solution.py:314
  1.8 2.2 %collective-permute-start = (bf16[2,8,16,1536]{3,2,1,0:T(8,128)(2,1)S(1)}, bf16[2,8,16,1536]{3,2,1,0:T(8,128)(2,1)S(1)}, u32[]{:S(2)}, u32[]{:S(2)}) collective-permute-start(bf16[2,8,16,1536]{3,2,1,0:T(8,128)(2,1)S(1)} %pair.1.refs_2_.refs_5_.refs_1_), channel_id=1, source_target_pairs={{0,4},{8,12},{4,0},{12,8},{1,5},{9,13},{5,1},{13,9},{2,6},{10,14},... | collective-permute-start | bytes 2359304 | tf_op jit(solution)/shard_map/ppermute | solution.py:31
  3.9 0.7 %collective-permute-start.1 = (bf16[2,8,16,1536]{3,2,1,0:T(8,128)(2,1)S(1)}, bf16[2,8,16,1536]{3,2,1,0:T(8,128)(2,1)S(1)}, u32[]{:S(2)}, u32[]{:S(2)}) collective-permute-start(bf16[2,8,16,1536]{3,2,1,0:T(8,128)(2,1)S(1)} %pair.1.refs_2_.refs_5_.refs_1_), channel_id=1, source_target_pairs={{4,8},{8,4},{5,9},{9,5},{6,10},{10,6},{7,11},{11,7},{20,24},{24,20... | collective-permute-start | bytes 2359304 | tf_op jit(solution)/shard_map/ppermute | solution.py:31
  4.7 0.1 pad_add_fusion.refs_0_.refs_1_
  4.7 2.3 %stage.1 = (bf16[2,8,16,1536]{3,2,1,0:T(8,128)(2,1)S(1)}, bf16[2,64,1536]{2,1,0:T(8,128)(2,1)S(1)}, bf16[2,64,1536]{2,1,0:T(8,128)(2,1)S(1)}) custom-call(s32[2]{0:T(128)S(1)} %pad_add_fusion.refs_0_.refs_1_, bf16[1,8,16,1536]{3,2,1,0:T(8,128)(2,1)} %refs_1_.1, bf16[1,8,16,1536]{3,2,1,0:T(8,128)(2,1)} %refs_2_.1), custom_call_target="tpu_custom_call" | custom-call | tf_op jit(solution)/shard_map/stage/pallas_call | solution.py:314
  7.0 1.0 %collective-permute-start.2 = (bf16[2,64,1536]{2,1,0:T(8,128)(2,1)S(1)}, bf16[2,64,1536]{2,1,0:T(8,128)(2,1)S(1)}, u32[]{:S(2)}, u32[]{:S(2)}) collective-permute-start(bf16[2,64,1536]{2,1,0:T(8,128)(2,1)S(1)} %get-tuple-element.21), channel_id=1, source_target_pairs={{0,1},{2,3},{1,0},{3,2},{4,5},{6,7},{5,4},{7,6},{8,9},{10,11},{9,8... | collective-permute-start | bytes 1179656 | tf_op jit(solution)/shard_map/ppermute | solution.py:31
  8.1 3.0 %collective-permute-start.3 = (bf16[2,64,1536]{2,1,0:T(8,128)(2,1)S(1)}, bf16[2,64,1536]{2,1,0:T(8,128)(2,1)S(1)}, u32[]{:S(2)}, u32[]{:S(2)}) collective-permute-start(bf16[2,64,1536]{2,1,0:T(8,128)(2,1)S(1)} %get-tuple-element.22), channel_id=1, source_target_pairs={{1,2},{2,1},{5,6},{6,5},{9,10},{10,9},{13,14},{14,13},{17,18},{18,... | collective-permute-start | bytes 1179656 | tf_op jit(solution)/shard_map/ppermute | solution.py:31
  11.1 0.0 collective-permute-done.2.refs_4_.refs_5_
  11.1 6.3 %collective-permute-done.3.refs_5_.refs_6_ = bf16[2,64,1536]{2,1,0:T(8,128)(2,1)S(1)} collective-permute-done((bf16[2,64,1536]{2,1,0:T(8,128)(2,1)S(1)}, bf16[2,64,1536]{2,1,0:T(8,128)(2,1)S(1)}, u32[]{:S(2)}, u32[]{:S(2)}) %collective-permute-start.3) | collective-permute-done | bytes 393248 | tf_op jit(solution)/shard_map/ppermute | solution.py:31
  17.4 0.0 copy-start
  17.4 0.7 %copy-done = s32[18,3]{0,1:T(4,128)S(1)} copy-done((s32[18,3]{0,1:T(4,128)S(1)}, s32[18,3]{0,1:T(4,128)}, u32[]{:S(2)}) %copy-start) | copy-done | bytes 240
  18.1 1.3 %own_stats.1 = (f32[12,3,128]{2,1,0:T(4,128)S(1)}, f32[12,256,128]{2,1,0:T(8,128)S(1)}, f32[12,256,128]{2,1,0:T(8,128)S(1)}) custom-call(s32[3,18]{1,0:T(4,128)S(1)} %bitcast.3, s32[2]{0:T(128)S(1)} %pad_add_fusion.refs_0_.refs_1_, bf16[2,8,16,1536]{3,2,1,0:T(8,128)(2,1)S(1)} %pair.1.refs_2_.refs_5_.refs_1_, ...), custom_call_target="tpu_custom_call" | custom-call | tf_op jit(solution)/shard_map/own_stats/pallas_call | solution.py:302
  19.4 1.8 %collective-permute-done.refs_2_.refs_6_ = bf16[2,8,16,1536]{3,2,1,0:T(8,128)(2,1)S(1)} collective-permute-done((bf16[2,8,16,1536]{3,2,1,0:T(8,128)(2,1)S(1)}, bf16[2,8,16,1536]{3,2,1,0:T(8,128)(2,1)S(1)}, u32[]{:S(2)}, u32[]{:S(2)}) %collective-permute-start) | collective-permute-done | bytes 786464 | tf_op jit(solution)/shard_map/ppermute | solution.py:31
  21.2 0.0 collective-permute-done.1.refs_3_.refs_7_
  21.2 2.0 %near_stats.1 = (f32[12,3,256]{2,1,0:T(4,128)S(1)}, f32[12,4,128]{2,1,0:T(4,128)S(1)}, f32[12,4,128]{2,1,0:T(4,128)S(1)}, f32[12,2,128]{2,1,0:T(2,128)S(1)}, f32...) custom-call(s32[3,18]{1,0:T(4,128)S(1)} %bitcast.4, ...), custom_call_target="tpu_custom_call" | custom-call | tf_op jit(solution)/shard_map/near_stats/pallas_call | solution.py:302
  23.2 0.7 %collective-permute-start.5 = (f32[12,4,128]{2,1,0:T(4,128)S(1)}, f32[12,4,128]{2,1,0:T(4,128)S(1)}, u32[]{:S(2)}, u32[]{:S(2)}) collective-permute-start(f32[12,4,128]{2,1,0:T(4,128)S(1)} %get-tuple-element.26), channel_id=1, source_target_pairs={{4,8},{8,4},{5,9},{9,5},{6,10},{10,6},{7,11},{11,7},{20,24},{24,20... | collective-permute-start | bytes 73736 | tf_op jit(solution)/shard_map/ppermute | solution.py:31
  23.8 6.7 %collective-permute-start.6 = (f32[12,4,128]{2,1,0:T(4,128)S(1)}, f32[12,4,128]{2,1,0:T(4,128)S(1)}, u32[]{:S(2)}, u32[]{:S(2)}) collective-permute-start(f32[12,4,128]{2,1,0:T(4,128)S(1)} %get-tuple-element.27), channel_id=1, source_target_pairs={{0,4},{8,12},{4,0},{12,8},{1,5},{9,13},{5,1},{13,9},{2,6},{10,14},... | collective-permute-start | bytes 73736 | tf_op jit(solution)/shard_map/ppermute | solution.py:31
  30.5 0.1 collective-permute-start.4
  30.6 3.5 %collective-permute-done.4.refs_1_ = f32[12,2,128]{2,1,0:T(2,128)S(1)} collective-permute-done((f32[12,2,128]{2,1,0:T(2,128)S(1)}, f32[12,2,128]{2,1,0:T(2,128)S(1)}, u32[]{:S(2)}, u32[]{:S(2)}) %collective-permute-start.4) | collective-permute-done | bytes 12320 | tf_op jit(solution)/shard_map/ppermute | solution.py:31
  34.1 0.0 collective-permute-done.5.refs_3_
  34.1 0.0 collective-permute-done.6.refs_4_
  34.1 1.7 %halo_grads.1 = (bf16[2,64,1536]{2,1,0:T(8,128)(2,1)S(1)}, bf16[2,64,1536]{2,1,0:T(8,128)(2,1)S(1)}, f32[12,2,384]{2,1,0:T(2,128)S(1)}) custom-call(s32[2]{0:T(128)S(1)} %pad_add_fusion.refs_0_.refs_1_, f32[12,2,128]{2,1,0:T(2,128)S(1)} %collective-permute-done.4.refs_1_, f32[12,2,128]{2,1,0:T(2,128)S(1)} %get-tuple-element.25.refs_2_, ...), custom_call_target="tpu_custom_call" | custom-call | tf_op jit(solution)/shard_map/halo_grads/pallas_call | solution.py:302
  35.8 6.5 %collective-permute-start.7 = (bf16[2,64,1536]{2,1,0:T(8,128)(2,1)S(1)}, bf16[2,64,1536]{2,1,0:T(8,128)(2,1)S(1)}, u32[]{:S(2)}, u32[]{:S(2)}) collective-permute-start(bf16[2,64,1536]{2,1,0:T(8,128)(2,1)S(1)} %get-tuple-element.33), channel_id=1, source_target_pairs={{1,2},{2,1},{5,6},{6,5},{9,10},{10,9},{13,14},{14,13},{17,18},{18,... | collective-permute-start | bytes 1179656 | tf_op jit(solution)/shard_map/ppermute | solution.py:31
  42.2 0.1 collective-permute-start.8
  42.3 0.9 %main_grads.1 = (f32[128,1536]{1,0:T(8,128)S(1)}, f32[128,1536]{1,0:T(8,128)S(1)}) custom-call(f32[12,2,384]{2,1,0:T(2,128)S(1)} %get-tuple-element.35.refs_0_, bf16[2,8,16,1536]{3,2,1,0:T(8,128)(2,1)S(1)} %pair.1.refs_2_.refs_5_.refs_1_, bf16[2,8,16,1536]{3,2,1,0:T(8,128)(2,1)S(1)} %collective-permute-done.refs_2_.refs_6_, ...), custom_call_target="tpu_custom_call" | custom-call | flops 1000000000 | tf_op jit(solution)/shard_map/main_grads/pallas_call | solution.py:302
  43.3 4.4 %collective-permute-done.7.refs_1_ = bf16[2,64,1536]{2,1,0:T(8,128)(2,1)S(1)} collective-permute-done((bf16[2,64,1536]{2,1,0:T(8,128)(2,1)S(1)}, bf16[2,64,1536]{2,1,0:T(8,128)(2,1)S(1)}, u32[]{:S(2)}, u32[]{:S(2)}) %collective-permute-start.7) | collective-permute-done | bytes 393248 | tf_op jit(solution)/shard_map/ppermute | solution.py:31
  47.7 0.0 collective-permute-done.8.refs_2_
  47.7 1.5 %finish.1 = (bf16[1,8,16,1536]{3,2,1,0:T(8,128)(2,1)}, bf16[1,8,16,1536]{3,2,1,0:T(8,128)(2,1)}) custom-call(s32[2]{0:T(128)S(1)} %pad_add_fusion.refs_0_.refs_1_, bf16[2,64,1536]{2,1,0:T(8,128)(2,1)S(1)} %collective-permute-done.7.refs_1_, bf16[2,64,1536]{2,1,0:T(8,128)(2,1)S(1)} %collective-permute-done.8.refs_2_, ...), custom_call_target="tpu_custom_call" | custom-call | tf_op jit(solution)/shard_map/finish/pallas_call | solution.py:379
Async XLA Ops:
  1.8 19.4 %collective-permute-start = (bf16[2,8,16,1536]{3,2,1,0:T(8,128)(2,1)S(1)}, bf16[2,8,16,1536]{3,2,1,0:T(8,128)(2,1)S(1)}, u32[]{:S(2)}, u32[]{:S(2)}) collective-permute-start(bf16[2,8,16,1536]{3,2,1,0:T(8,128)(2,1)S(1)} %pair.1.refs_2_.refs_5_.refs_1_), channel_id=1, source_target_pairs={{0,4},{8,12},{4,0},{12,8},{1,5},{9,13},{5,1},{13,9},{2,6},{10,14},... | collective-permute-start | bytes 2359304 | tf_op jit(solution)/shard_map/ppermute | solution.py:31
  3.9 17.2 %collective-permute-start.1 = (bf16[2,8,16,1536]{3,2,1,0:T(8,128)(2,1)S(1)}, bf16[2,8,16,1536]{3,2,1,0:T(8,128)(2,1)S(1)}, u32[]{:S(2)}, u32[]{:S(2)}) collective-permute-start(bf16[2,8,16,1536]{3,2,1,0:T(8,128)(2,1)S(1)} %pair.1.refs_2_.refs_5_.refs_1_), channel_id=1, source_target_pairs={{4,8},{8,4},{5,9},{9,5},{6,10},{10,6},{7,11},{11,7},{20,24},{24,20... | collective-permute-start | bytes 2359304 | tf_op jit(solution)/shard_map/ppermute | solution.py:31
  7.0 4.1 %collective-permute-start.2 = (bf16[2,64,1536]{2,1,0:T(8,128)(2,1)S(1)}, bf16[2,64,1536]{2,1,0:T(8,128)(2,1)S(1)}, u32[]{:S(2)}, u32[]{:S(2)}) collective-permute-start(bf16[2,64,1536]{2,1,0:T(8,128)(2,1)S(1)} %get-tuple-element.21), channel_id=1, source_target_pairs={{0,1},{2,3},{1,0},{3,2},{4,5},{6,7},{5,4},{7,6},{8,9},{10,11},{9,8... | collective-permute-start | bytes 1179656 | tf_op jit(solution)/shard_map/ppermute | solution.py:31
  8.1 9.4 %collective-permute-start.3 = (bf16[2,64,1536]{2,1,0:T(8,128)(2,1)S(1)}, bf16[2,64,1536]{2,1,0:T(8,128)(2,1)S(1)}, u32[]{:S(2)}, u32[]{:S(2)}) collective-permute-start(bf16[2,64,1536]{2,1,0:T(8,128)(2,1)S(1)} %get-tuple-element.22), channel_id=1, source_target_pairs={{1,2},{2,1},{5,6},{6,5},{9,10},{10,9},{13,14},{14,13},{17,18},{18,... | collective-permute-start | bytes 1179656 | tf_op jit(solution)/shard_map/ppermute | solution.py:31
  17.4 0.7 %copy-start = (s32[18,3]{0,1:T(4,128)S(1)}, s32[18,3]{0,1:T(4,128)}, u32[]{:S(2)}) copy-start(s32[18,3]{0,1:T(4,128)} %param.9) | copy-start | bytes 652
  23.2 10.9 %collective-permute-start.5 = (f32[12,4,128]{2,1,0:T(4,128)S(1)}, f32[12,4,128]{2,1,0:T(4,128)S(1)}, u32[]{:S(2)}, u32[]{:S(2)}) collective-permute-start(f32[12,4,128]{2,1,0:T(4,128)S(1)} %get-tuple-element.26), channel_id=1, source_target_pairs={{4,8},{8,4},{5,9},{9,5},{6,10},{10,6},{7,11},{11,7},{20,24},{24,20... | collective-permute-start | bytes 73736 | tf_op jit(solution)/shard_map/ppermute | solution.py:31
  23.8 10.2 %collective-permute-start.6 = (f32[12,4,128]{2,1,0:T(4,128)S(1)}, f32[12,4,128]{2,1,0:T(4,128)S(1)}, u32[]{:S(2)}, u32[]{:S(2)}) collective-permute-start(f32[12,4,128]{2,1,0:T(4,128)S(1)} %get-tuple-element.27), channel_id=1, source_target_pairs={{0,4},{8,12},{4,0},{12,8},{1,5},{9,13},{5,1},{13,9},{2,6},{10,14},... | collective-permute-start | bytes 73736 | tf_op jit(solution)/shard_map/ppermute | solution.py:31
  30.5 3.5 %collective-permute-start.4 = (f32[12,2,128]{2,1,0:T(2,128)S(1)}, f32[12,2,128]{2,1,0:T(2,128)S(1)}, u32[]{:S(2)}, u32[]{:S(2)}) collective-permute-start(f32[12,2,128]{2,1,0:T(2,128)S(1)} %get-tuple-element.24), channel_id=1, source_target_pairs={{0,8},{4,12},{8,0},{12,4},{1,9},{5,13},{9,1},{13,5},{2,10},{6,14},... | collective-permute-start | bytes 36872 | tf_op jit(solution)/shard_map/ppermute | solution.py:31
  35.8 11.9 %collective-permute-start.7 = (bf16[2,64,1536]{2,1,0:T(8,128)(2,1)S(1)}, bf16[2,64,1536]{2,1,0:T(8,128)(2,1)S(1)}, u32[]{:S(2)}, u32[]{:S(2)}) collective-permute-start(bf16[2,64,1536]{2,1,0:T(8,128)(2,1)S(1)} %get-tuple-element.33), channel_id=1, source_target_pairs={{1,2},{2,1},{5,6},{6,5},{9,10},{10,9},{13,14},{14,13},{17,18},{18,... | collective-permute-start | bytes 1179656 | tf_op jit(solution)/shard_map/ppermute | solution.py:31
  42.2 5.4 %collective-permute-start.8 = (bf16[2,64,1536]{2,1,0:T(8,128)(2,1)S(1)}, bf16[2,64,1536]{2,1,0:T(8,128)(2,1)S(1)}, u32[]{:S(2)}, u32[]{:S(2)}) collective-permute-start(bf16[2,64,1536]{2,1,0:T(8,128)(2,1)S(1)} %get-tuple-element.34), channel_id=1, source_target_pairs={{0,1},{2,3},{1,0},{3,2},{4,5},{6,7},{5,4},{7,6},{8,9},{10,11},{9,8... | collective-permute-start | bytes 1179656 | tf_op jit(solution)/shard_map/ppermute | solution.py:31

commit v5 on v3

--- a/solution.py
+++ b/solution.py
@@ -108,14 +108,25 @@
     return lax.dot_general(a, b, (((1,), (1,)), ((), ())), preferred_element_type=jnp.float32)
 
 
-def edges_kernel(sizes, place_ref, k0, v0, a_out, b_out):
+def run_copies(pairs, sems):
+    copies = [pltpu.make_async_copy(src, dst, sems.at[i]) for i, (src, dst) in enumerate(pairs)]
+    for copy in copies:
+        copy.start()
+    for copy in copies:
+        copy.wait()
+
+
+def stage_kernel(sizes, place_ref, k_in, v_in, k_out, v_out, a_out, b_out, sems):
     _, _, height, strip = sizes
     even = (place_ref[1] & 1) == 0
-    for which, ref in enumerate((k0, v0)):
-        left = ref[0, :, :TW, :].reshape(height * TW, -1)
-        right = ref[0, :, strip - TW :, :].reshape(height * TW, -1)
-        a_out[which] = jnp.where(even, right, left)
-        b_out[which] = jnp.where(even, left, right)
+    start_a = pl.multiple_of(jnp.where(even, strip - TW, 0), TW)
+    start_b = pl.multiple_of(jnp.where(even, 0, strip - TW), TW)
+    pairs = []
+    for edge, start in ((a_out, start_a), (b_out, start_b)):
+        for which, ref in enumerate((k_in, v_in)):
+            for row in range(height):
+                pairs.append((ref.at[0, row, pl.ds(start, TW), :], edge.at[which, row * TW : (row + 1) * TW, :]))
+    run_copies(pairs + [(k_in, k_out), (v_in, v_out)], sems)
 
 
 def scores_kernel(sizes, window_ref, place_ref, q0, qa, qb, g0, k0, v0, ha, hb, expo_out, gp_out, st_out, delta_out, bias_ref):
@@ -237,19 +248,29 @@
         dv_out[:, lanes] = value_part
 
 
-def finish_kernel(sizes, step_rows, place_ref, rb, ra, dk, dv, dk_out, dv_out):
+def finish_kernel(sizes, place_ref, rb, ra, dk, dv, dk_out, dv_out, full_ref, sems):
     _, _, height, strip = sizes
     even = (place_ref[1] & 1) == 0
-    step = pl.program_id(0)
-    edge = pl.ds(pl.multiple_of(step * step_rows * TW, step_rows * TW), step_rows * TW)
-    span = pl.ds(pl.multiple_of(step * step_rows * strip, step_rows * strip), step_rows * strip)
-    for which, (part, out) in enumerate(((dk, dk_out), (dv, dv_out))):
-        from_a = ra[which, edge, :].astype(jnp.float32).reshape(step_rows, TW, -1)
-        from_b = rb[which, edge, :].astype(jnp.float32).reshape(step_rows, TW, -1)
-        full = part[span, :].reshape(step_rows, strip, -1)
-        left = full[:, :TW] + jnp.where(even, from_b, from_a)
-        right = full[:, TW:] + jnp.where(even, from_a, from_b)
-        out[0] = jnp.concatenate([left, right], axis=1).astype(jnp.bfloat16)
+    count = height // FINISH_STEPS
+    copies = []
+    for step in range(FINISH_STEPS):
+        lines = slice(step * count, (step + 1) * count)
+        edge = slice(step * count * TW, (step + 1) * count * TW)
+        span = slice(step * count * strip, (step + 1) * count * strip)
+        for which, (part, out) in enumerate(((dk, dk_out), (dv, dv_out))):
+            from_a = ra[which, edge, :].astype(jnp.float32).reshape(count, TW, -1)
+            from_b = rb[which, edge, :].astype(jnp.float32).reshape(count, TW, -1)
+            full = part[span, :].reshape(count, strip, -1)
+            left = full[:, :TW] + jnp.where(even, from_b, from_a)
+            right = full[:, TW:] + jnp.where(even, from_a, from_b)
+            full_ref[which, lines] = jnp.concatenate([left, right], axis=1).astype(jnp.bfloat16)
+            copy = pltpu.make_async_copy(
+                full_ref.at[which, lines], out.at[0, lines], sems.at[2 * step + which]
+            )
+            copy.start()
+            copies.append(copy)
+    for copy in copies:
+        copy.wait()
 
 
 def vmem(value):
@@ -276,10 +297,11 @@
     ga = swap(grad_out, "frame", frame_even)
     gb = swap(grad_out, "frame", frame_odd)
 
+    raw = pl.BlockSpec(memory_space=pl.ANY)
     smem = pl.BlockSpec(memory_space=pltpu.SMEM)
     whole = pl.BlockSpec(memory_space=pltpu.VMEM)
 
-    def call(kernel, name, scalars, arrays, outs, scratch=(), flops=FLOPS):
+    def call(kernel, name, scalars, arrays, outs, scratch=(), flops=0):
         return pl.pallas_call(
             lambda *refs: kernel(sizes, *refs),
             name=name,
@@ -292,9 +314,17 @@
         )(*scalars, *[vmem(x) for x in arrays])
 
     f32 = jnp.float32
-    ea, eb = call(
-        edges_kernel, "edges", (place,), (keys, values), [((2, half, chans), jnp.bfloat16)] * 2
-    )
+    edge = (2, half, chans)
+    keys, values, ea, eb = pl.pallas_call(
+        lambda *refs: stage_kernel(sizes, *refs),
+        name="stage",
+        in_specs=[smem, raw, raw],
+        out_specs=[whole] * 4,
+        out_shape=[pltpu.VMEM(shape, jnp.bfloat16) for shape in (keys.shape, values.shape, edge, edge)],
+        scratch_shapes=[pltpu.SemaphoreType.DMA((4 * height + 2,))],
+        compiler_params=pltpu.CompilerParams(vmem_limit_bytes=KERNEL_VMEM),
+        cost_estimate=pl.CostEstimate(flops=0, transcendentals=0, bytes_accessed=0),
+    )(place, *[pltpu.with_memory_space_constraint(x, pltpu.HBM) for x in (keys, values)])
     ha = swap(ea, "tile", tile_even)
     hb = swap(eb, "tile", tile_odd)
     expo, p0, st, own_delta = call(
@@ -341,18 +371,20 @@
         (),
         (row,) + data,
         [((rows, chans), f32)] * 2,
-    )
-
-    step_rows = height // FINISH_STEPS
-    out_spec = pl.BlockSpec((1, step_rows, strip, chans), lambda i: (0, i, 0, 0))
+        flops=FLOPS,
+    )
+
     return pl.pallas_call(
-        lambda *refs: finish_kernel(sizes, step_rows, *refs),
+        lambda *refs: finish_kernel(sizes, *refs),
         name="finish",
-        grid=(FINISH_STEPS,),
         compiler_params=pltpu.CompilerParams(vmem_limit_bytes=KERNEL_VMEM),
         in_specs=[smem] + [whole] * 4,
-        out_specs=[out_spec, out_spec],
-        out_shape=[jax.ShapeDtypeStruct(keys.shape, jnp.bfloat16)] * 2,
+        out_specs=[raw, raw],
+        out_shape=[jax.ShapeDtypeStruct(queries.shape, jnp.bfloat16)] * 2,
+        scratch_shapes=[
+            pltpu.VMEM((2, height, strip, chans), jnp.bfloat16),
+            pltpu.SemaphoreType.DMA((2 * FINISH_STEPS,)),
+        ],
     )(place, vmem(rb), vmem(ra), vmem(dk), vmem(dv))
 
 

time: 46.7 us -> 46.3 us (level)
  Pallas kernels: 9.79 us -> 10.8 us
  local copies, waits for them, and re-layouts: 3.77 us -> 2.77 us
  waiting for transfers between devices: 8.73 us -> 7.97 us
    pallas_call x1 -> x2, Pallas kernels: 2.03 us -> 4.54 us  [the longest x1 3.04 us: on_device(): pl.pallas_call(lambda *refs: stage_kernel(sizes, *refs), name='stage', in...]
    pallas_call x5 -> x4, Pallas kernels: 7.76 us -> 6.24 us  [call(): pl.pallas_call(lambda *refs: kernel(sizes, *refs), name=name, in_specs=[s...]
    unnamed x13 -> x9, local copies, waits for them, and re-layouts: 3.77 us -> 2.77 us
    ppermute x11, waiting for transfers between devices: 8.73 us -> 7.97 us  [swap(): return lax.ppermute(value, axis, pairs)]
  transfers between devices with their start and end apart: 11 -> 11, of which waited for: 4 -> 4; matrix products, arithmetic and copies ran while one was open for 2% -> 2% of each run, Pallas kernels for 11% -> 14%
where the time goes in v5:
time: 46.3 us; the launch traced here: 46 us
  starting transfers between devices  23.6 us (51%)
  Pallas kernels  10.8 us (23%)
  waiting for transfers between devices  7.97 us (17%)
  local copies, waits for them, and re-layouts  2.77 us (6%)
  between operations  0.74 us (2%)
    ppermute x11, starting transfers between devices, swap(): return lax.ppermute(value, axis, pairs)  23.6 us
    ppermute x11, waiting for transfers between devices, swap(): return lax.ppermute(value, axis, pairs)  7.97 us
    pallas_call x4, Pallas kernels, call(): pl.pallas_call(lambda *refs: kernel(sizes, *refs), name=name, in_specs=[s...  6.24 us
    pallas_call x1, Pallas kernels, on_device(): pl.pallas_call(lambda *refs: stage_kernel(sizes, *refs), name='stage', in...  3.04 us
    unnamed x9, local copies, waits for them, and re-layouts  2.77 us
    pallas_call x1, Pallas kernels, on_device(): pl.pallas_call(lambda *refs: finish_kernel(sizes, *refs), name='finish',...  1.51 us
  transfers between devices with their start and end apart: 11, of which 4 were waited for; matrix products, arithmetic and copies ran while one was open for 2% of the time, Pallas kernels for 14%

profile of v5, /device:TPU:1, one launch (start us, length us, event | category | flops | bytes accessed | tf_op | source)
XLA Modules:
  0.0 46.0 jit_solution(16791694245136765416)
XLA Ops:
  0.6 2.2 %collective-permute-start = (bf16[1,8,16,1536]{3,2,1,0:T(8,128)(2,1)}, bf16[1,8,16,1536]{3,2,1,0:T(8,128)(2,1)S(1)}, u32[]{:S(2)}, u32[]{:S(2)}) collective-permute-start(bf16[1,8,16,1536]{3,2,1,0:T(8,128)(2,1)} %refs_1_.5), channel_id=1, source_target_pairs={{0,4},{8,12},{4,0},{12,8},{1,5},{9,13},{5,1},{13,9},{2,6},{10,14},... | collective-permute-start | bytes 1179656 | tf_op jit(solution)/shard_map/ppermute | solution.py:31
  2.8 0.7 %collective-permute-start.1 = (bf16[1,8,16,1536]{3,2,1,0:T(8,128)(2,1)}, bf16[1,8,16,1536]{3,2,1,0:T(8,128)(2,1)S(1)}, u32[]{:S(2)}, u32[]{:S(2)}) collective-permute-start(bf16[1,8,16,1536]{3,2,1,0:T(8,128)(2,1)} %refs_1_.5), channel_id=1, source_target_pairs={{4,8},{8,4},{5,9},{9,5},{6,10},{10,6},{7,11},{11,7},{20,24},{24,20... | collective-permute-start | bytes 1179656 | tf_op jit(solution)/shard_map/ppermute | solution.py:31
  3.5 0.1 pad_add_fusion.refs_0_.refs_1_
  3.6 3.0 %stage.1 = (bf16[1,8,16,1536]{3,2,1,0:T(8,128)(2,1)S(1)}, bf16[1,8,16,1536]{3,2,1,0:T(8,128)(2,1)S(1)}, bf16[2,64,1536]{2,1,0:T(8,128)(2,1)}, bf16[2,64,1536]{2,1,0:T(8,128)(2,1)S(1)}) custom-call(s32[2]{0:T(128)S(1)} %pad_add_fusion.refs_0_.refs_1_, bf16[1,8,16,1536]{3,2,1,0:T(8,128)(2,1)} %refs_1_.3, bf16[1,8,16,1536]{3,2,1,0:T(8,128)(2,1)} %refs_2_.2), custom_call_target="tpu_custom_call" | custom-call | tf_op jit(solution)/shard_map/stage/pallas_call | solution.py:318
  6.6 1.0 %collective-permute-start.4 = (bf16[2,64,1536]{2,1,0:T(8,128)(2,1)}, bf16[2,64,1536]{2,1,0:T(8,128)(2,1)S(1)}, u32[]{:S(2)}, u32[]{:S(2)}) collective-permute-start(bf16[2,64,1536]{2,1,0:T(8,128)(2,1)} %get-tuple-element.23), channel_id=1, source_target_pairs={{0,1},{2,3},{1,0},{3,2},{4,5},{6,7},{5,4},{7,6},{8,9},{10,11},{9,8... | collective-permute-start | bytes 1179656 | tf_op jit(solution)/shard_map/ppermute | solution.py:31
  7.6 3.0 %collective-permute-start.5 = (bf16[2,64,1536]{2,1,0:T(8,128)(2,1)S(1)}, bf16[2,64,1536]{2,1,0:T(8,128)(2,1)S(1)}, u32[]{:S(2)}, u32[]{:S(2)}) collective-permute-start(bf16[2,64,1536]{2,1,0:T(8,128)(2,1)S(1)} %get-tuple-element.24), channel_id=1, source_target_pairs={{1,2},{2,1},{5,6},{6,5},{9,10},{10,9},{13,14},{14,13},{17,18},{18,... | collective-permute-start | bytes 1179656 | tf_op jit(solution)/shard_map/ppermute | solution.py:31
  10.7 4.2 %collective-permute-start.2 = (bf16[1,8,16,1536]{3,2,1,0:T(8,128)(2,1)}, bf16[1,8,16,1536]{3,2,1,0:T(8,128)(2,1)S(1)}, u32[]{:S(2)}, u32[]{:S(2)}) collective-permute-start(bf16[1,8,16,1536]{3,2,1,0:T(8,128)(2,1)} %refs_4_.3), channel_id=1, source_target_pairs={{0,4},{8,12},{4,0},{12,8},{1,5},{9,13},{5,1},{13,9},{2,6},{10,14},... | collective-permute-start | bytes 1179656 | tf_op jit(solution)/shard_map/ppermute | solution.py:31
  14.9 0.0 collective-permute-done.refs_3_.refs_2_
  14.9 0.7 %collective-permute-start.3 = (bf16[1,8,16,1536]{3,2,1,0:T(8,128)(2,1)}, bf16[1,8,16,1536]{3,2,1,0:T(8,128)(2,1)S(1)}, u32[]{:S(2)}, u32[]{:S(2)}) collective-permute-start(bf16[1,8,16,1536]{3,2,1,0:T(8,128)(2,1)} %refs_4_.3), channel_id=1, source_target_pairs={{4,8},{8,4},{5,9},{9,5},{6,10},{10,6},{7,11},{11,7},{20,24},{24,20... | collective-permute-start | bytes 1179656 | tf_op jit(solution)/shard_map/ppermute | solution.py:31
  15.5 0.8 %copy.7.refs_0_ = s32[18,3]{1,0:T(8,128)S(1)} copy(s32[18,3]{0,1:T(4,128)} %param.9) | data formatting | bytes 432 | tf_op args[4]
  16.3 0.0 collective-permute-done.1.refs_4_.refs_3_
  16.3 0.0 collective-permute-done.4.refs_8_.refs_4_
  16.3 0.7 %collective-permute-done.5.refs_9_.refs_5_ = bf16[2,64,1536]{2,1,0:T(8,128)(2,1)S(1)} collective-permute-done((bf16[2,64,1536]{2,1,0:T(8,128)(2,1)S(1)}, bf16[2,64,1536]{2,1,0:T(8,128)(2,1)S(1)}, u32[]{:S(2)}, u32[]{:S(2)}) %collective-permute-start.5) | collective-permute-done | bytes 393248 | tf_op jit(solution)/shard_map/ppermute | solution.py:31
  17.0 1.0 %copy-done = bf16[1,8,16,1536]{3,2,1,0:T(8,128)(2,1)S(1)} copy-done((bf16[1,8,16,1536]{3,2,1,0:T(8,128)(2,1)S(1)}, bf16[1,8,16,1536]{3,2,1,0:T(8,128)(2,1)}, u32[]{:S(2)}) %copy-start) | copy-done | bytes 393240
  18.0 1.0 %copy-done.2 = bf16[1,8,16,1536]{3,2,1,0:T(8,128)(2,1)S(1)} copy-done((bf16[1,8,16,1536]{3,2,1,0:T(8,128)(2,1)S(1)}, bf16[1,8,16,1536]{3,2,1,0:T(8,128)(2,1)}, u32[]{:S(2)}) %copy-start.2) | copy-done | bytes 393240
  19.0 2.6 %scores.1 = (f32[12,256,384]{2,1,0:T(8,128)S(1)}, f32[12,256,128]{2,1,0:T(8,128)S(1)}, f32[12,3,384]{2,1,0:T(4,128)S(1)}, f32[12,1,128]{2,1,0:T(1,128)S(1)}) custom-call(s32[18,3]{1,0:T(8,128)S(1)} %copy.7.refs_0_, s32[2]{0:T(128)S(1)} %pad_add_fusion.refs_0_.refs_1_, bf16[1,8,16,1536]{3,2,1,0:T(8,128)(2,1)S(1)} %copy-done, ...), custom_call_target="tpu_custom_call" | custom-call | tf_op jit(solution)/shard_map/scores/pallas_call | solution.py:305
  21.6 0.7 %collective-permute-done.2.refs_1_.refs_5_ = bf16[1,8,16,1536]{3,2,1,0:T(8,128)(2,1)S(1)} collective-permute-done((bf16[1,8,16,1536]{3,2,1,0:T(8,128)(2,1)}, bf16[1,8,16,1536]{3,2,1,0:T(8,128)(2,1)S(1)}, u32[]{:S(2)}, u32[]{:S(2)}) %collective-permute-start.2) | collective-permute-done | bytes 393248 | tf_op jit(solution)/shard_map/ppermute | solution.py:31
  22.3 0.0 collective-permute-done.3.refs_2_.refs_6_
  22.3 1.1 %deltas.1 = (f32[12,256,256]{2,1,0:T(8,128)S(1)}, f32[12,1,384]{2,1,0:T(1,128)S(1)}, f32[12,4,128]{2,1,0:T(4,128)S(1)}, f32[12,4,128]{2,1,0:T(4,128)S(1)}, f32[1...) custom-call(s32[2]{0:T(128)S(1)} %pad_add_fusion.refs_0_.refs_1_, ...), custom_call_target="tpu_custom_call" | custom-call | tf_op jit(solution)/shard_map/deltas/pallas_call | solution.py:305
  23.4 5.8 %collective-permute-start.6 = (f32[12,4,128]{2,1,0:T(4,128)S(1)}, f32[12,4,128]{2,1,0:T(4,128)S(1)}, u32[]{:S(2)}, u32[]{:S(2)}) collective-permute-start(f32[12,4,128]{2,1,0:T(4,128)S(1)} %get-tuple-element.31), channel_id=1, source_target_pairs={{0,4},{8,12},{4,0},{12,8},{1,5},{9,13},{5,1},{13,9},{2,6},{10,14},... | collective-permute-start | bytes 73736 | tf_op jit(solution)/shard_map/ppermute | solution.py:31
  29.2 0.7 %collective-permute-start.7 = (f32[12,4,128]{2,1,0:T(4,128)S(1)}, f32[12,4,128]{2,1,0:T(4,128)S(1)}, u32[]{:S(2)}, u32[]{:S(2)}) collective-permute-start(f32[12,4,128]{2,1,0:T(4,128)S(1)} %get-tuple-element.32), channel_id=1, source_target_pairs={{4,8},{8,4},{5,9},{9,5},{6,10},{10,6},{7,11},{11,7},{20,24},{24,20... | collective-permute-start | bytes 73736 | tf_op jit(solution)/shard_map/ppermute | solution.py:31
  29.9 2.5 %collective-permute-start.8 = (f32[12,2,128]{2,1,0:T(2,128)S(1)}, f32[12,2,128]{2,1,0:T(2,128)S(1)}, u32[]{:S(2)}, u32[]{:S(2)}) collective-permute-start(f32[12,2,128]{2,1,0:T(2,128)S(1)} %get-tuple-element.33), channel_id=1, source_target_pairs={{0,8},{4,12},{8,0},{12,4},{1,9},{5,13},{9,1},{13,5},{2,10},{6,14},... | collective-permute-start | bytes 36872 | tf_op jit(solution)/shard_map/ppermute | solution.py:31
  32.4 1.3 %collective-permute-done.8.refs_14_ = f32[12,2,128]{2,1,0:T(2,128)S(1)} collective-permute-done((f32[12,2,128]{2,1,0:T(2,128)S(1)}, f32[12,2,128]{2,1,0:T(2,128)S(1)}, u32[]{:S(2)}, u32[]{:S(2)}) %collective-permute-start.8) | collective-permute-done | bytes 12320 | tf_op jit(solution)/shard_map/ppermute | solution.py:31
  33.6 0.0 collective-permute-done.6.refs_12_
  33.6 0.0 collective-permute-done.7.refs_13_
  33.6 1.7 %halo_grads.1 = (bf16[2,64,1536]{2,1,0:T(8,128)(2,1)S(1)}, bf16[2,64,1536]{2,1,0:T(8,128)(2,1)S(1)}, f32[12,2,384]{2,1,0:T(2,128)S(1)}) custom-call(s32[2]{0:T(128)S(1)} %pad_add_fusion.refs_0_.refs_1_, bf16[1,8,16,1536]{3,2,1,0:T(8,128)(2,1)S(1)} %copy-done.1, bf16[1,8,16,1536]{3,2,1,0:T(8,128)(2,1)S(1)} %collective-permute-done.refs_3_.refs_2_, ...), custom_call_target="tpu_custom_call" | custom-call | tf_op jit(solution)/shard_map/halo_grads/pallas_call | solution.py:305
  35.3 2.8 %collective-permute-start.9 = (bf16[2,64,1536]{2,1,0:T(8,128)(2,1)S(1)}, bf16[2,64,1536]{2,1,0:T(8,128)(2,1)S(1)}, u32[]{:S(2)}, u32[]{:S(2)}) collective-permute-start(bf16[2,64,1536]{2,1,0:T(8,128)(2,1)S(1)} %get-tuple-element.35), channel_id=1, source_target_pairs={{1,2},{2,1},{5,6},{6,5},{9,10},{10,9},{13,14},{14,13},{17,18},{18,... | collective-permute-start | bytes 1179656 | tf_op jit(solution)/shard_map/ppermute | solution.py:31
  38.2 0.1 collective-permute-start.10
  38.3 0.8 %main_grads.1 = (f32[128,1536]{1,0:T(8,128)S(1)}, f32[128,1536]{1,0:T(8,128)S(1)}) custom-call(f32[12,2,384]{2,1,0:T(2,128)S(1)} %get-tuple-element.37.refs_0_, bf16[1,8,16,1536]{3,2,1,0:T(8,128)(2,1)S(1)} %copy-done.1, bf16[1,8,16,1536]{3,2,1,0:T(8,128)(2,1)S(1)} %collective-permute-done.refs_3_.refs_2_, ...), custom_call_target="tpu_custom_call" | custom-call | flops 1500000000 | tf_op jit(solution)/shard_map/main_grads/pallas_call | solution.py:305
  39.1 5.3 %collective-permute-done.9.refs_1_ = bf16[2,64,1536]{2,1,0:T(8,128)(2,1)S(1)} collective-permute-done((bf16[2,64,1536]{2,1,0:T(8,128)(2,1)S(1)}, bf16[2,64,1536]{2,1,0:T(8,128)(2,1)S(1)}, u32[]{:S(2)}, u32[]{:S(2)}) %collective-permute-start.9) | collective-permute-done | bytes 393248 | tf_op jit(solution)/shard_map/ppermute | solution.py:31
  44.4 0.0 collective-permute-done.10.refs_2_
  44.4 1.5 %finish.1 = (bf16[1,8,16,1536]{3,2,1,0:T(8,128)(2,1)}, bf16[1,8,16,1536]{3,2,1,0:T(8,128)(2,1)}) custom-call(s32[2]{0:T(128)S(1)} %pad_add_fusion.refs_0_.refs_1_, bf16[2,64,1536]{2,1,0:T(8,128)(2,1)S(1)} %collective-permute-done.9.refs_1_, bf16[2,64,1536]{2,1,0:T(8,128)(2,1)S(1)} %collective-permute-done.10.refs_2_, ...), custom_call_target="tpu_custom_call" | custom-call | tf_op jit(solution)/shard_map/finish/pallas_call | solution.py:377
  (6 shorter events, 0.0 us)
Async XLA Ops:
  0.6 14.2 %collective-permute-start = (bf16[1,8,16,1536]{3,2,1,0:T(8,128)(2,1)}, bf16[1,8,16,1536]{3,2,1,0:T(8,128)(2,1)S(1)}, u32[]{:S(2)}, u32[]{:S(2)}) collective-permute-start(bf16[1,8,16,1536]{3,2,1,0:T(8,128)(2,1)} %refs_1_.5), channel_id=1, source_target_pairs={{0,4},{8,12},{4,0},{12,8},{1,5},{9,13},{5,1},{13,9},{2,6},{10,14},... | collective-permute-start | bytes 1179656 | tf_op jit(solution)/shard_map/ppermute | solution.py:31
  2.8 13.5 %collective-permute-start.1 = (bf16[1,8,16,1536]{3,2,1,0:T(8,128)(2,1)}, bf16[1,8,16,1536]{3,2,1,0:T(8,128)(2,1)S(1)}, u32[]{:S(2)}, u32[]{:S(2)}) collective-permute-start(bf16[1,8,16,1536]{3,2,1,0:T(8,128)(2,1)} %refs_1_.5), channel_id=1, source_target_pairs={{4,8},{8,4},{5,9},{9,5},{6,10},{10,6},{7,11},{11,7},{20,24},{24,20... | collective-permute-start | bytes 1179656 | tf_op jit(solution)/shard_map/ppermute | solution.py:31
  6.6 9.7 %collective-permute-start.4 = (bf16[2,64,1536]{2,1,0:T(8,128)(2,1)}, bf16[2,64,1536]{2,1,0:T(8,128)(2,1)S(1)}, u32[]{:S(2)}, u32[]{:S(2)}) collective-permute-start(bf16[2,64,1536]{2,1,0:T(8,128)(2,1)} %get-tuple-element.23), channel_id=1, source_target_pairs={{0,1},{2,3},{1,0},{3,2},{4,5},{6,7},{5,4},{7,6},{8,9},{10,11},{9,8... | collective-permute-start | bytes 1179656 | tf_op jit(solution)/shard_map/ppermute | solution.py:31
  7.6 9.4 %collective-permute-start.5 = (bf16[2,64,1536]{2,1,0:T(8,128)(2,1)S(1)}, bf16[2,64,1536]{2,1,0:T(8,128)(2,1)S(1)}, u32[]{:S(2)}, u32[]{:S(2)}) collective-permute-start(bf16[2,64,1536]{2,1,0:T(8,128)(2,1)S(1)} %get-tuple-element.24), channel_id=1, source_target_pairs={{1,2},{2,1},{5,6},{6,5},{9,10},{10,9},{13,14},{14,13},{17,18},{18,... | collective-permute-start | bytes 1179656 | tf_op jit(solution)/shard_map/ppermute | solution.py:31
  10.7 11.6 %collective-permute-start.2 = (bf16[1,8,16,1536]{3,2,1,0:T(8,128)(2,1)}, bf16[1,8,16,1536]{3,2,1,0:T(8,128)(2,1)S(1)}, u32[]{:S(2)}, u32[]{:S(2)}) collective-permute-start(bf16[1,8,16,1536]{3,2,1,0:T(8,128)(2,1)} %refs_4_.3), channel_id=1, source_target_pairs={{0,4},{8,12},{4,0},{12,8},{1,5},{9,13},{5,1},{13,9},{2,6},{10,14},... | collective-permute-start | bytes 1179656 | tf_op jit(solution)/shard_map/ppermute | solution.py:31
  14.9 7.4 %collective-permute-start.3 = (bf16[1,8,16,1536]{3,2,1,0:T(8,128)(2,1)}, bf16[1,8,16,1536]{3,2,1,0:T(8,128)(2,1)S(1)}, u32[]{:S(2)}, u32[]{:S(2)}) collective-permute-start(bf16[1,8,16,1536]{3,2,1,0:T(8,128)(2,1)} %refs_4_.3), channel_id=1, source_target_pairs={{4,8},{8,4},{5,9},{9,5},{6,10},{10,6},{7,11},{11,7},{20,24},{24,20... | collective-permute-start | bytes 1179656 | tf_op jit(solution)/shard_map/ppermute | solution.py:31
  17.0 1.0 %copy-start = (bf16[1,8,16,1536]{3,2,1,0:T(8,128)(2,1)S(1)}, bf16[1,8,16,1536]{3,2,1,0:T(8,128)(2,1)}, u32[]{:S(2)}) copy-start(bf16[1,8,16,1536]{3,2,1,0:T(8,128)(2,1)} %refs_1_.5) | copy-start | bytes 1179652
  18.0 1.0 %copy-start.2 = (bf16[1,8,16,1536]{3,2,1,0:T(8,128)(2,1)S(1)}, bf16[1,8,16,1536]{3,2,1,0:T(8,128)(2,1)}, u32[]{:S(2)}) copy-start(bf16[1,8,16,1536]{3,2,1,0:T(8,128)(2,1)} %refs_4_.3) | copy-start | bytes 1179652
  22.3 11.4 %copy-start.1 = (bf16[1,8,16,1536]{3,2,1,0:T(8,128)(2,1)S(1)}, bf16[1,8,16,1536]{3,2,1,0:T(8,128)(2,1)}, u32[]{:S(2)}) copy-start(bf16[1,8,16,1536]{3,2,1,0:T(8,128)(2,1)} %refs_1_.5) | copy-start | bytes 1179652
  22.3 11.4 %copy-start.3 = (bf16[1,8,16,1536]{3,2,1,0:T(8,128)(2,1)S(1)}, bf16[1,8,16,1536]{3,2,1,0:T(8,128)(2,1)}, u32[]{:S(2)}) copy-start(bf16[1,8,16,1536]{3,2,1,0:T(8,128)(2,1)} %refs_4_.3) | copy-start | bytes 1179652
  23.4 10.2 %collective-permute-start.6 = (f32[12,4,128]{2,1,0:T(4,128)S(1)}, f32[12,4,128]{2,1,0:T(4,128)S(1)}, u32[]{:S(2)}, u32[]{:S(2)}) collective-permute-start(f32[12,4,128]{2,1,0:T(4,128)S(1)} %get-tuple-element.31), channel_id=1, source_target_pairs={{0,4},{8,12},{4,0},{12,8},{1,5},{9,13},{5,1},{13,9},{2,6},{10,14},... | collective-permute-start | bytes 73736 | tf_op jit(solution)/shard_map/ppermute | solution.py:31
  29.2 4.4 %collective-permute-start.7 = (f32[12,4,128]{2,1,0:T(4,128)S(1)}, f32[12,4,128]{2,1,0:T(4,128)S(1)}, u32[]{:S(2)}, u32[]{:S(2)}) collective-permute-start(f32[12,4,128]{2,1,0:T(4,128)S(1)} %get-tuple-element.32), channel_id=1, source_target_pairs={{4,8},{8,4},{5,9},{9,5},{6,10},{10,6},{7,11},{11,7},{20,24},{24,20... | collective-permute-start | bytes 73736 | tf_op jit(solution)/shard_map/ppermute | solution.py:31
  29.9 3.8 %collective-permute-start.8 = (f32[12,2,128]{2,1,0:T(2,128)S(1)}, f32[12,2,128]{2,1,0:T(2,128)S(1)}, u32[]{:S(2)}, u32[]{:S(2)}) collective-permute-start(f32[12,2,128]{2,1,0:T(2,128)S(1)} %get-tuple-element.33), channel_id=1, source_target_pairs={{0,8},{4,12},{8,0},{12,4},{1,9},{5,13},{9,1},{13,5},{2,10},{6,14},... | collective-permute-start | bytes 36872 | tf_op jit(solution)/shard_map/ppermute | solution.py:31
  35.3 9.1 %collective-permute-start.9 = (bf16[2,64,1536]{2,1,0:T(8,128)(2,1)S(1)}, bf16[2,64,1536]{2,1,0:T(8,128)(2,1)S(1)}, u32[]{:S(2)}, u32[]{:S(2)}) collective-permute-start(bf16[2,64,1536]{2,1,0:T(8,128)(2,1)S(1)} %get-tuple-element.35), channel_id=1, source_target_pairs={{1,2},{2,1},{5,6},{6,5},{9,10},{10,9},{13,14},{14,13},{17,18},{18,... | collective-permute-start | bytes 1179656 | tf_op jit(solution)/shard_map/ppermute | solution.py:31
  38.2 6.3 %collective-permute-start.10 = (bf16[2,64,1536]{2,1,0:T(8,128)(2,1)S(1)}, bf16[2,64,1536]{2,1,0:T(8,128)(2,1)S(1)}, u32[]{:S(2)}, u32[]{:S(2)}) collective-permute-start(bf16[2,64,1536]{2,1,0:T(8,128)(2,1)S(1)} %get-tuple-element.36), channel_id=1, source_target_pairs={{0,1},{2,3},{1,0},{3,2},{4,5},{6,7},{5,4},{7,6},{8,9},{10,11},{9,8... | collective-permute-start | bytes 1179656 | tf_op jit(solution)/shard_map/ppermute | solution.py:31

commit v6 on v5

--- a/solution.py
+++ b/solution.py
@@ -116,7 +116,7 @@
         copy.wait()
 
 
-def stage_kernel(sizes, place_ref, k_in, v_in, k_out, v_out, a_out, b_out, sems):
+def stage_kernel(sizes, place_ref, _, k_in, v_in, k_out, v_out, a_out, b_out, sems):
     _, _, height, strip = sizes
     even = (place_ref[1] & 1) == 0
     start_a = pl.multiple_of(jnp.where(even, strip - TW, 0), TW)
@@ -318,13 +318,13 @@
     keys, values, ea, eb = pl.pallas_call(
         lambda *refs: stage_kernel(sizes, *refs),
         name="stage",
-        in_specs=[smem, raw, raw],
+        in_specs=[smem, whole, raw, raw],
         out_specs=[whole] * 4,
         out_shape=[pltpu.VMEM(shape, jnp.bfloat16) for shape in (keys.shape, values.shape, edge, edge)],
         scratch_shapes=[pltpu.SemaphoreType.DMA((4 * height + 2,))],
         compiler_params=pltpu.CompilerParams(vmem_limit_bytes=KERNEL_VMEM),
         cost_estimate=pl.CostEstimate(flops=0, transcendentals=0, bytes_accessed=0),
-    )(place, *[pltpu.with_memory_space_constraint(x, pltpu.HBM) for x in (keys, values)])
+    )(place, vmem(ga), *[pltpu.with_memory_space_constraint(x, pltpu.HBM) for x in (keys, values)])
     ha = swap(ea, "tile", tile_even)
     hb = swap(eb, "tile", tile_odd)
     expo, p0, st, own_delta = call(

time: 46.3 us -> 53.3 us (1.15)
  the two profiles are of different devices: /device:TPU:1 before, /device:TPU:11 now
where the time goes in v6:
time: 53.3 us; the launch traced here: 53 us
  starting transfers between devices  22.7 us (43%)
  waiting for transfers between devices  16 us (30%)
  Pallas kernels  10.6 us (20%)
  local copies, waits for them, and re-layouts  2.77 us (5%)
  between operations  0.76 us (1%)
    ppermute x11, starting transfers between devices, swap(): return lax.ppermute(value, axis, pairs)  22.7 us
    ppermute x11, waiting for transfers between devices, swap(): return lax.ppermute(value, axis, pairs)  16 us
    pallas_call x4, Pallas kernels, call(): pl.pallas_call(lambda *refs: kernel(sizes, *refs), name=name, in_specs=[s...  6.1 us
    pallas_call x1, Pallas kernels, on_device(): pl.pallas_call(lambda *refs: stage_kernel(sizes, *refs), name='stage', in...  3.04 us
    unnamed x9, local copies, waits for them, and re-layouts  2.77 us
    pallas_call x1, Pallas kernels, on_device(): pl.pallas_call(lambda *refs: finish_kernel(sizes, *refs), name='finish',...  1.51 us
  transfers between devices with their start and end apart: 11, of which 5 were waited for; matrix products, arithmetic and copies ran while one was open for 2% of the time, Pallas kernels for 12%

profile of v6, /device:TPU:11, one launch (start us, length us, event | category | flops | bytes accessed | tf_op | source)
XLA Modules:
  0.0 53.0 jit_solution(12777788547012935035)
XLA Ops:
  0.6 0.2 collective-permute-start.2
  0.9 1.3 %collective-permute-start = (bf16[1,8,16,1536]{3,2,1,0:T(8,128)(2,1)}, bf16[1,8,16,1536]{3,2,1,0:T(8,128)(2,1)S(1)}, u32[]{:S(2)}, u32[]{:S(2)}) collective-permute-start(bf16[1,8,16,1536]{3,2,1,0:T(8,128)(2,1)} %refs_1_.3), channel_id=1, source_target_pairs={{0,4},{8,12},{4,0},{12,8},{1,5},{9,13},{5,1},{13,9},{2,6},{10,14},... | collective-permute-start | bytes 1179656 | tf_op jit(solution)/shard_map/ppermute | solution.py:31
  2.2 3.2 %collective-permute-start.1 = (bf16[1,8,16,1536]{3,2,1,0:T(8,128)(2,1)}, bf16[1,8,16,1536]{3,2,1,0:T(8,128)(2,1)S(1)}, u32[]{:S(2)}, u32[]{:S(2)}) collective-permute-start(bf16[1,8,16,1536]{3,2,1,0:T(8,128)(2,1)} %refs_1_.3), channel_id=1, source_target_pairs={{4,8},{8,4},{5,9},{9,5},{6,10},{10,6},{7,11},{11,7},{20,24},{24,20... | collective-permute-start | bytes 1179656 | tf_op jit(solution)/shard_map/ppermute | solution.py:31
  5.4 0.1 pad_add_fusion.refs_0_.refs_1_
  5.4 5.5 %collective-permute-done.2.refs_1_.refs_5_ = bf16[1,8,16,1536]{3,2,1,0:T(8,128)(2,1)S(1)} collective-permute-done((bf16[1,8,16,1536]{3,2,1,0:T(8,128)(2,1)}, bf16[1,8,16,1536]{3,2,1,0:T(8,128)(2,1)S(1)}, u32[]{:S(2)}, u32[]{:S(2)}) %collective-permute-start.2) | collective-permute-done | bytes 393248 | tf_op jit(solution)/shard_map/ppermute | solution.py:31
  10.9 3.0 %stage.1 = (bf16[1,8,16,1536]{3,2,1,0:T(8,128)(2,1)S(1)}, bf16[1,8,16,1536]{3,2,1,0:T(8,128)(2,1)S(1)}, bf16[2,64,1536]{2,1,0:T(8,128)(2,1)}, bf16[2,64,1536]{2,1,0:T(8,128)(2,1)S(1)}) custom-call(s32[2]{0:T(128)S(1)} %pad_add_fusion.refs_0_.refs_1_, bf16[1,8,16,1536]{3,2,1,0:T(8,128)(2,1)S(1)} %collective-permute-done.2.refs_1_.refs_5_, ...), custom_call_target="tpu_custom_call" | custom-call | tf_op jit(solution)/shard_map/stage/pallas_call | solution.py:318
  13.9 2.7 %collective-permute-start.4 = (bf16[2,64,1536]{2,1,0:T(8,128)(2,1)}, bf16[2,64,1536]{2,1,0:T(8,128)(2,1)S(1)}, u32[]{:S(2)}, u32[]{:S(2)}) collective-permute-start(bf16[2,64,1536]{2,1,0:T(8,128)(2,1)} %get-tuple-element.23), channel_id=1, source_target_pairs={{0,1},{2,3},{1,0},{3,2},{4,5},{6,7},{5,4},{7,6},{8,9},{10,11},{9,8... | collective-permute-start | bytes 1179656 | tf_op jit(solution)/shard_map/ppermute | solution.py:31
  16.7 3.0 %collective-permute-start.5 = (bf16[2,64,1536]{2,1,0:T(8,128)(2,1)S(1)}, bf16[2,64,1536]{2,1,0:T(8,128)(2,1)S(1)}, u32[]{:S(2)}, u32[]{:S(2)}) collective-permute-start(bf16[2,64,1536]{2,1,0:T(8,128)(2,1)S(1)} %get-tuple-element.24), channel_id=1, source_target_pairs={{1,2},{2,1},{5,6},{6,5},{9,10},{10,9},{13,14},{14,13},{17,18},{18,... | collective-permute-start | bytes 1179656 | tf_op jit(solution)/shard_map/ppermute | solution.py:31
  19.7 3.2 %collective-permute-start.3 = (bf16[1,8,16,1536]{3,2,1,0:T(8,128)(2,1)}, bf16[1,8,16,1536]{3,2,1,0:T(8,128)(2,1)S(1)}, u32[]{:S(2)}, u32[]{:S(2)}) collective-permute-start(bf16[1,8,16,1536]{3,2,1,0:T(8,128)(2,1)} %refs_4_.3), channel_id=1, source_target_pairs={{4,8},{8,4},{5,9},{9,5},{6,10},{10,6},{7,11},{11,7},{20,24},{24,20... | collective-permute-start | bytes 1179656 | tf_op jit(solution)/shard_map/ppermute | solution.py:31
  22.9 0.8 %copy.7.refs_0_ = s32[18,3]{1,0:T(8,128)S(1)} copy(s32[18,3]{0,1:T(4,128)} %param.9) | data formatting | bytes 432 | tf_op args[4]
  23.7 0.0 collective-permute-done.refs_3_.refs_2_
  23.7 0.0 collective-permute-done.1.refs_4_.refs_3_
  23.7 0.0 collective-permute-done.4.refs_8_.refs_4_
  23.7 2.3 %collective-permute-done.5.refs_9_.refs_5_ = bf16[2,64,1536]{2,1,0:T(8,128)(2,1)S(1)} collective-permute-done((bf16[2,64,1536]{2,1,0:T(8,128)(2,1)S(1)}, bf16[2,64,1536]{2,1,0:T(8,128)(2,1)S(1)}, u32[]{:S(2)}, u32[]{:S(2)}) %collective-permute-start.5) | collective-permute-done | bytes 393248 | tf_op jit(solution)/shard_map/ppermute | solution.py:31
  26.1 1.0 %copy-done = bf16[1,8,16,1536]{3,2,1,0:T(8,128)(2,1)S(1)} copy-done((bf16[1,8,16,1536]{3,2,1,0:T(8,128)(2,1)S(1)}, bf16[1,8,16,1536]{3,2,1,0:T(8,128)(2,1)}, u32[]{:S(2)}) %copy-start) | copy-done | bytes 393240
  27.1 1.0 %copy-done.2 = bf16[1,8,16,1536]{3,2,1,0:T(8,128)(2,1)S(1)} copy-done((bf16[1,8,16,1536]{3,2,1,0:T(8,128)(2,1)S(1)}, bf16[1,8,16,1536]{3,2,1,0:T(8,128)(2,1)}, u32[]{:S(2)}) %copy-start.2) | copy-done | bytes 393240
  28.0 2.6 %scores.1 = (f32[12,256,384]{2,1,0:T(8,128)S(1)}, f32[12,256,128]{2,1,0:T(8,128)S(1)}, f32[12,3,384]{2,1,0:T(4,128)S(1)}, f32[12,1,128]{2,1,0:T(1,128)S(1)}) custom-call(s32[18,3]{1,0:T(8,128)S(1)} %copy.7.refs_0_, s32[2]{0:T(128)S(1)} %pad_add_fusion.refs_0_.refs_1_, bf16[1,8,16,1536]{3,2,1,0:T(8,128)(2,1)S(1)} %copy-done, ...), custom_call_target="tpu_custom_call" | custom-call | tf_op jit(solution)/shard_map/scores/pallas_call | solution.py:305
  30.6 0.2 collective-permute-done.3.refs_2_.refs_6_
  30.8 1.2 %deltas.1 = (f32[12,256,256]{2,1,0:T(8,128)S(1)}, f32[12,1,384]{2,1,0:T(1,128)S(1)}, f32[12,4,128]{2,1,0:T(4,128)S(1)}, f32[12,4,128]{2,1,0:T(4,128)S(1)}, f32[1...) custom-call(s32[2]{0:T(128)S(1)} %pad_add_fusion.refs_0_.refs_1_, ...), custom_call_target="tpu_custom_call" | custom-call | tf_op jit(solution)/shard_map/deltas/pallas_call | solution.py:305
  32.0 0.1 collective-permute-start.6
  32.0 4.0 %collective-permute-start.7 = (f32[12,4,128]{2,1,0:T(4,128)S(1)}, f32[12,4,128]{2,1,0:T(4,128)S(1)}, u32[]{:S(2)}, u32[]{:S(2)}) collective-permute-start(f32[12,4,128]{2,1,0:T(4,128)S(1)} %get-tuple-element.32), channel_id=1, source_target_pairs={{4,8},{8,4},{5,9},{9,5},{6,10},{10,6},{7,11},{11,7},{20,24},{24,20... | collective-permute-start | bytes 73736 | tf_op jit(solution)/shard_map/ppermute | solution.py:31
  36.1 0.1 collective-permute-start.8
  36.2 3.4 %collective-permute-done.8.refs_14_ = f32[12,2,128]{2,1,0:T(2,128)S(1)} collective-permute-done((f32[12,2,128]{2,1,0:T(2,128)S(1)}, f32[12,2,128]{2,1,0:T(2,128)S(1)}, u32[]{:S(2)}, u32[]{:S(2)}) %collective-permute-start.8) | collective-permute-done | bytes 12320 | tf_op jit(solution)/shard_map/ppermute | solution.py:31
  39.6 0.0 collective-permute-done.6.refs_12_
  39.6 0.0 collective-permute-done.7.refs_13_
  39.6 1.6 %halo_grads.1 = (bf16[2,64,1536]{2,1,0:T(8,128)(2,1)S(1)}, bf16[2,64,1536]{2,1,0:T(8,128)(2,1)S(1)}, f32[12,2,384]{2,1,0:T(2,128)S(1)}) custom-call(s32[2]{0:T(128)S(1)} %pad_add_fusion.refs_0_.refs_1_, bf16[1,8,16,1536]{3,2,1,0:T(8,128)(2,1)S(1)} %copy-done.1, bf16[1,8,16,1536]{3,2,1,0:T(8,128)(2,1)S(1)} %collective-permute-done.refs_3_.refs_2_, ...), custom_call_target="tpu_custom_call" | custom-call | tf_op jit(solution)/shard_map/halo_grads/pallas_call | solution.py:305
  41.2 4.8 %collective-permute-start.9 = (bf16[2,64,1536]{2,1,0:T(8,128)(2,1)S(1)}, bf16[2,64,1536]{2,1,0:T(8,128)(2,1)S(1)}, u32[]{:S(2)}, u32[]{:S(2)}) collective-permute-start(bf16[2,64,1536]{2,1,0:T(8,128)(2,1)S(1)} %get-tuple-element.35), channel_id=1, source_target_pairs={{1,2},{2,1},{5,6},{6,5},{9,10},{10,9},{13,14},{14,13},{17,18},{18,... | collective-permute-start | bytes 1179656 | tf_op jit(solution)/shard_map/ppermute | solution.py:31
  46.0 0.1 collective-permute-start.10
  46.1 0.8 %main_grads.1 = (f32[128,1536]{1,0:T(8,128)S(1)}, f32[128,1536]{1,0:T(8,128)S(1)}) custom-call(f32[12,2,384]{2,1,0:T(2,128)S(1)} %get-tuple-element.37.refs_0_, bf16[1,8,16,1536]{3,2,1,0:T(8,128)(2,1)S(1)} %copy-done.1, bf16[1,8,16,1536]{3,2,1,0:T(8,128)(2,1)S(1)} %collective-permute-done.refs_3_.refs_2_, ...), custom_call_target="tpu_custom_call" | custom-call | flops 1500000000 | tf_op jit(solution)/shard_map/main_grads/pallas_call | solution.py:305
  46.9 4.6 %collective-permute-done.9.refs_1_ = bf16[2,64,1536]{2,1,0:T(8,128)(2,1)S(1)} collective-permute-done((bf16[2,64,1536]{2,1,0:T(8,128)(2,1)S(1)}, bf16[2,64,1536]{2,1,0:T(8,128)(2,1)S(1)}, u32[]{:S(2)}, u32[]{:S(2)}) %collective-permute-start.9) | collective-permute-done | bytes 393248 | tf_op jit(solution)/shard_map/ppermute | solution.py:31
  51.4 0.0 collective-permute-done.10.refs_2_
  51.5 1.5 %finish.1 = (bf16[1,8,16,1536]{3,2,1,0:T(8,128)(2,1)}, bf16[1,8,16,1536]{3,2,1,0:T(8,128)(2,1)}) custom-call(s32[2]{0:T(128)S(1)} %pad_add_fusion.refs_0_.refs_1_, bf16[2,64,1536]{2,1,0:T(8,128)(2,1)S(1)} %collective-permute-done.9.refs_1_, bf16[2,64,1536]{2,1,0:T(8,128)(2,1)S(1)} %collective-permute-done.10.refs_2_, ...), custom_call_target="tpu_custom_call" | custom-call | tf_op jit(solution)/shard_map/finish/pallas_call | solution.py:377
  (6 shorter events, 0.0 us)
Async XLA Ops:
  0.6 10.3 %collective-permute-start.2 = (bf16[1,8,16,1536]{3,2,1,0:T(8,128)(2,1)}, bf16[1,8,16,1536]{3,2,1,0:T(8,128)(2,1)S(1)}, u32[]{:S(2)}, u32[]{:S(2)}) collective-permute-start(bf16[1,8,16,1536]{3,2,1,0:T(8,128)(2,1)} %refs_4_.3), channel_id=1, source_target_pairs={{0,4},{8,12},{4,0},{12,8},{1,5},{9,13},{5,1},{13,9},{2,6},{10,14},... | collective-permute-start | bytes 1179656 | tf_op jit(solution)/shard_map/ppermute | solution.py:31
  0.9 22.9 %collective-permute-start = (bf16[1,8,16,1536]{3,2,1,0:T(8,128)(2,1)}, bf16[1,8,16,1536]{3,2,1,0:T(8,128)(2,1)S(1)}, u32[]{:S(2)}, u32[]{:S(2)}) collective-permute-start(bf16[1,8,16,1536]{3,2,1,0:T(8,128)(2,1)} %refs_1_.3), channel_id=1, source_target_pairs={{0,4},{8,12},{4,0},{12,8},{1,5},{9,13},{5,1},{13,9},{2,6},{10,14},... | collective-permute-start | bytes 1179656 | tf_op jit(solution)/shard_map/ppermute | solution.py:31
  2.2 21.6 %collective-permute-start.1 = (bf16[1,8,16,1536]{3,2,1,0:T(8,128)(2,1)}, bf16[1,8,16,1536]{3,2,1,0:T(8,128)(2,1)S(1)}, u32[]{:S(2)}, u32[]{:S(2)}) collective-permute-start(bf16[1,8,16,1536]{3,2,1,0:T(8,128)(2,1)} %refs_1_.3), channel_id=1, source_target_pairs={{4,8},{8,4},{5,9},{9,5},{6,10},{10,6},{7,11},{11,7},{20,24},{24,20... | collective-permute-start | bytes 1179656 | tf_op jit(solution)/shard_map/ppermute | solution.py:31
  13.9 9.8 %collective-permute-start.4 = (bf16[2,64,1536]{2,1,0:T(8,128)(2,1)}, bf16[2,64,1536]{2,1,0:T(8,128)(2,1)S(1)}, u32[]{:S(2)}, u32[]{:S(2)}) collective-permute-start(bf16[2,64,1536]{2,1,0:T(8,128)(2,1)} %get-tuple-element.23), channel_id=1, source_target_pairs={{0,1},{2,3},{1,0},{3,2},{4,5},{6,7},{5,4},{7,6},{8,9},{10,11},{9,8... | collective-permute-start | bytes 1179656 | tf_op jit(solution)/shard_map/ppermute | solution.py:31
  16.7 9.4 %collective-permute-start.5 = (bf16[2,64,1536]{2,1,0:T(8,128)(2,1)S(1)}, bf16[2,64,1536]{2,1,0:T(8,128)(2,1)S(1)}, u32[]{:S(2)}, u32[]{:S(2)}) collective-permute-start(bf16[2,64,1536]{2,1,0:T(8,128)(2,1)S(1)} %get-tuple-element.24), channel_id=1, source_target_pairs={{1,2},{2,1},{5,6},{6,5},{9,10},{10,9},{13,14},{14,13},{17,18},{18,... | collective-permute-start | bytes 1179656 | tf_op jit(solution)/shard_map/ppermute | solution.py:31
  19.7 11.1 %collective-permute-start.3 = (bf16[1,8,16,1536]{3,2,1,0:T(8,128)(2,1)}, bf16[1,8,16,1536]{3,2,1,0:T(8,128)(2,1)S(1)}, u32[]{:S(2)}, u32[]{:S(2)}) collective-permute-start(bf16[1,8,16,1536]{3,2,1,0:T(8,128)(2,1)} %refs_4_.3), channel_id=1, source_target_pairs={{4,8},{8,4},{5,9},{9,5},{6,10},{10,6},{7,11},{11,7},{20,24},{24,20... | collective-permute-start | bytes 1179656 | tf_op jit(solution)/shard_map/ppermute | solution.py:31
  26.1 1.0 %copy-start = (bf16[1,8,16,1536]{3,2,1,0:T(8,128)(2,1)S(1)}, bf16[1,8,16,1536]{3,2,1,0:T(8,128)(2,1)}, u32[]{:S(2)}) copy-start(bf16[1,8,16,1536]{3,2,1,0:T(8,128)(2,1)} %refs_1_.3) | copy-start | bytes 1179652
  27.1 1.0 %copy-start.2 = (bf16[1,8,16,1536]{3,2,1,0:T(8,128)(2,1)S(1)}, bf16[1,8,16,1536]{3,2,1,0:T(8,128)(2,1)}, u32[]{:S(2)}) copy-start(bf16[1,8,16,1536]{3,2,1,0:T(8,128)(2,1)} %refs_4_.3) | copy-start | bytes 1179652
  30.8 8.8 %copy-start.1 = (bf16[1,8,16,1536]{3,2,1,0:T(8,128)(2,1)S(1)}, bf16[1,8,16,1536]{3,2,1,0:T(8,128)(2,1)}, u32[]{:S(2)}) copy-start(bf16[1,8,16,1536]{3,2,1,0:T(8,128)(2,1)} %refs_1_.3) | copy-start | bytes 1179652
  30.8 8.8 %copy-start.3 = (bf16[1,8,16,1536]{3,2,1,0:T(8,128)(2,1)S(1)}, bf16[1,8,16,1536]{3,2,1,0:T(8,128)(2,1)}, u32[]{:S(2)}) copy-start(bf16[1,8,16,1536]{3,2,1,0:T(8,128)(2,1)} %refs_4_.3) | copy-start | bytes 1179652
  32.0 7.6 %collective-permute-start.6 = (f32[12,4,128]{2,1,0:T(4,128)S(1)}, f32[12,4,128]{2,1,0:T(4,128)S(1)}, u32[]{:S(2)}, u32[]{:S(2)}) collective-permute-start(f32[12,4,128]{2,1,0:T(4,128)S(1)} %get-tuple-element.31), channel_id=1, source_target_pairs={{0,4},{8,12},{4,0},{12,8},{1,5},{9,13},{5,1},{13,9},{2,6},{10,14},... | collective-permute-start | bytes 73736 | tf_op jit(solution)/shard_map/ppermute | solution.py:31
  32.0 7.6 %collective-permute-start.7 = (f32[12,4,128]{2,1,0:T(4,128)S(1)}, f32[12,4,128]{2,1,0:T(4,128)S(1)}, u32[]{:S(2)}, u32[]{:S(2)}) collective-permute-start(f32[12,4,128]{2,1,0:T(4,128)S(1)} %get-tuple-element.32), channel_id=1, source_target_pairs={{4,8},{8,4},{5,9},{9,5},{6,10},{10,6},{7,11},{11,7},{20,24},{24,20... | collective-permute-start | bytes 73736 | tf_op jit(solution)/shard_map/ppermute | solution.py:31
  36.1 3.5 %collective-permute-start.8 = (f32[12,2,128]{2,1,0:T(2,128)S(1)}, f32[12,2,128]{2,1,0:T(2,128)S(1)}, u32[]{:S(2)}, u32[]{:S(2)}) collective-permute-start(f32[12,2,128]{2,1,0:T(2,128)S(1)} %get-tuple-element.33), channel_id=1, source_target_pairs={{0,8},{4,12},{8,0},{12,4},{1,9},{5,13},{9,1},{13,5},{2,10},{6,14},... | collective-permute-start | bytes 36872 | tf_op jit(solution)/shard_map/ppermute | solution.py:31
  41.2 10.2 %collective-permute-start.9 = (bf16[2,64,1536]{2,1,0:T(8,128)(2,1)S(1)}, bf16[2,64,1536]{2,1,0:T(8,128)(2,1)S(1)}, u32[]{:S(2)}, u32[]{:S(2)}) collective-permute-start(bf16[2,64,1536]{2,1,0:T(8,128)(2,1)S(1)} %get-tuple-element.35), channel_id=1, source_target_pairs={{1,2},{2,1},{5,6},{6,5},{9,10},{10,9},{13,14},{14,13},{17,18},{18,... | collective-permute-start | bytes 1179656 | tf_op jit(solution)/shard_map/ppermute | solution.py:31
  46.0 5.4 %collective-permute-start.10 = (bf16[2,64,1536]{2,1,0:T(8,128)(2,1)S(1)}, bf16[2,64,1536]{2,1,0:T(8,128)(2,1)S(1)}, u32[]{:S(2)}, u32[]{:S(2)}) collective-permute-start(bf16[2,64,1536]{2,1,0:T(8,128)(2,1)S(1)} %get-tuple-element.36), channel_id=1, source_target_pairs={{0,1},{2,3},{1,0},{3,2},{4,5},{6,7},{5,4},{7,6},{8,9},{10,11},{9,8... | collective-permute-start | bytes 1179656 | tf_op jit(solution)/shard_map/ppermute | solution.py:31
